TPU v7x, 256 devices: a whole 4x4x8 slice. The times are simulated.
256 devices in a mesh: row: 16 (over y, x), col: 16 (over z, core).
Axes of the slice: x: 4, y: 4, z: 8, core: 2. Of those that a mesh axis runs over, the one named last changes fastest.
Arguments:
- features: bfloat16 [4096, 256, 512], P(('row', 'col')), may hold values from -6 to 6
- analysis: bfloat16 [4096, 64, 256], P(('row', 'col')), may hold values from -0.375 to 0.375
- transitions: bfloat16 [12, 4096, 64, 128], P(None, ('row', 'col')), may hold values from -0.5 to 0.5
- synthesis: bfloat16 [4096, 64, 256], P(('row', 'col')), may hold values from -0.75 to 0.75
Outputs:
- filtered: bfloat16 [4096, 256, 512], P(('row', 'col'))
All inputs are finite; a program needn't handle non-finite values.
Results may differ from a plain program's by a relative error of at most 0.02.
Values may be sent and summed in bfloat16 or wider, within the bound.
No kernel may reach another device: no remote copies, remote signals or barrier semaphores. Data moves between devices by JAX's collectives and lax.ppermute only.
A program may use at most 64 MiB of HBM per device.

v0:
```python
import functools

import jax
import jax.numpy as jnp
from jax import lax
from jax.experimental import pallas as pl
from jax.experimental.pallas import tpu as pltpu
from jax.sharding import PartitionSpec as P


RANK = 64
LANES = 512
PTS = 256
SLOTS = 16
N_ROW = 16
N_COL = 16
N_Z = 8
HOST_LEVELS = 3
MSG = LANES + HOST_LEVELS * 2 * RANK
BF = jnp.bfloat16
F32 = jnp.float32
VMEM = pl.BlockSpec(memory_space=pltpu.VMEM)


def spread(r):
    return r ^ ((r << 1) & 14)


def gather(v):
    return v ^ ((v << 1) & 14) ^ ((v << 2) & 12) ^ ((v << 3) & 8)


def z_swap(array, d):
    return lax.ppermute(array, "col", [(c, c ^ (2 * d)) for c in range(N_COL)])


def to_target_row(array, b):
    pairs = []
    for r in range(N_ROW):
        for c in range(N_COL):
            pairs.append((r * N_COL + c, (spread(r) ^ (2 * (c >> 1)) ^ b) * N_COL + c))
    return lax.ppermute(array, ("row", "col"), pairs)


def dot(a, b):
    return lax.dot_general(a, b, (((1,), (0,)), ((), ())), preferred_element_type=F32)


def ordered(bit, first, second):
    low = jnp.where(bit == 0, first, second)
    high = jnp.where(bit == 0, second, first)
    return jnp.concatenate([low, high], axis=0)


def front_kernel(leaves, f_ref, a_ref, t_ref, o_ref):
    step = pl.program_id(0)
    for l in range(leaves):
        o_ref[step * leaves + l] = dot(a_ref[l], f_ref[l]).astype(BF)

    @pl.when(step == pl.num_programs(0) - 1)
    def _():
        for level in range(4):
            stride = 1 << level
            for lo in range(SLOTS):
                if lo & stride:
                    continue
                hi = lo + stride
                merge_pair(o_ref, t_ref.at[level], lo, hi)


def merge_pair(c_ref, t_ref, lo, hi):
    joined = jnp.concatenate([c_ref[lo], c_ref[hi]], axis=0)
    weights = jnp.concatenate([t_ref[lo], t_ref[hi]], axis=0)
    merged = dot(weights, joined).astype(BF)
    c_ref[lo] = merged[:RANK]
    c_ref[hi] = merged[RANK:]


def front(features, analysis, transitions):
    leaves = 2
    return pl.pallas_call(
        functools.partial(front_kernel, leaves),
        grid=(SLOTS // leaves,),
        in_specs=[
            pl.BlockSpec((leaves, PTS, LANES), lambda i: (i, 0, 0)),
            pl.BlockSpec((leaves, RANK, PTS), lambda i: (i, 0, 0)),
            pl.BlockSpec((4, SLOTS, RANK, 2 * RANK), lambda i: (0, 0, 0, 0)),
        ],
        out_specs=pl.BlockSpec((SLOTS, RANK, LANES), lambda i: (0, 0, 0)),
        out_shape=jax.ShapeDtypeStruct((SLOTS, RANK, LANES), BF),
        cost_estimate=pl.CostEstimate(flops=800_000_000, bytes_accessed=7_000_000, transcendentals=0),
        compiler_params=pltpu.CompilerParams(vmem_limit_bytes=60 << 20),
        name="front",
    )(features, analysis, transitions)


def message_kernel(b, r_ref, own_ref, partner_ref, t_ref, *outs):
    r, z, core = r_ref[0], r_ref[1], r_ref[2]
    for d in range(N_Z):
        host = z ^ d
        s = spread(r) ^ (2 * host) ^ b
        out = outs[d]
        own, partner = own_ref[s], partner_ref[s]
        joined = ordered(core, own, partner)
        out[:, :LANES] = dot(t_ref[0, s], joined).astype(BF)
        for e in range(HOST_LEVELS):
            out[:, LANES + e * 2 * RANK : LANES + (e + 1) * 2 * RANK] = t_ref[1 + e, s]


def messages(b, where, own, partner, transitions):
    return pl.pallas_call(
        functools.partial(message_kernel, b),
        grid=(1,),
        in_specs=[
            pl.BlockSpec(memory_space=pltpu.SMEM),
            VMEM,
            VMEM,
            pl.BlockSpec((4, SLOTS, RANK, 2 * RANK), lambda i: (1, 0, 0, 0)),
        ],
        out_specs=[VMEM] * N_Z,
        out_shape=[jax.ShapeDtypeStruct((RANK, MSG), BF)] * N_Z,
        cost_estimate=pl.CostEstimate(flops=70_000_000, bytes_accessed=3_000_000, transcendentals=0),
        compiler_params=pltpu.CompilerParams(vmem_limit_bytes=12 << 20),
    )(where, own, partner, transitions)


def host_kernel(r_ref, *refs):
    msgs, out = refs[:N_Z], refs[N_Z]
    for e in range(HOST_LEVELS):
        stride = 1 << e
        bit = (r_ref[1] >> e) & 1
        lanes = slice(LANES + e * 2 * RANK, LANES + (e + 1) * 2 * RANK)
        for lo in range(N_Z):
            if lo & stride:
                continue
            hi = lo + stride
            if e == 0:
                joined = ordered(bit, msgs[lo][:, :LANES], msgs[hi][:, :LANES])
            else:
                joined = ordered(bit, out[lo], out[hi])
            weights = jnp.concatenate([msgs[lo][:, lanes], msgs[hi][:, lanes]], axis=0)
            merged = dot(weights, joined).astype(BF)
            out[lo] = merged[:RANK]
            out[hi] = merged[RANK:]


def host_merge(where, msgs):
    return pl.pallas_call(
        host_kernel,
        in_specs=[pl.BlockSpec(memory_space=pltpu.SMEM)] + [VMEM] * N_Z,
        out_specs=VMEM,
        out_shape=jax.ShapeDtypeStruct((N_Z, RANK, LANES), BF),
        cost_estimate=pl.CostEstimate(flops=200_000_000, bytes_accessed=1_400_000, transcendentals=0),
        compiler_params=pltpu.CompilerParams(vmem_limit_bytes=6 << 20),
    )(where, *msgs)


def tail_kernel(leaves, r_ref, *refs):
    msgs, (t_ref, s_ref, o_ref, c_ref) = refs[: 2 * N_Z], refs[2 * N_Z :]
    step = pl.program_id(0)

    @pl.when(step == 0)
    def _():
        base = gather(r_ref[0] ^ (2 * r_ref[1]))
        for b in range(2):
            for d in range(N_Z):
                c_ref[base ^ gather(2 * d ^ b)] = msgs[b * N_Z + d][...]
        for level in range(4):
            stride = 1 << level
            for lo in range(SLOTS):
                if lo & stride:
                    continue
                merge_pair(c_ref, t_ref.at[level], lo, lo + stride)

    for l in range(leaves):
        o_ref[l] = lax.dot_general(
            s_ref[l], c_ref[step * leaves + l], (((0,), (0,)), ((), ())), preferred_element_type=F32
        ).astype(BF)


def tail(where, msgs, transitions, synthesis):
    leaves = 2
    return pl.pallas_call(
        functools.partial(tail_kernel, leaves),
        grid=(SLOTS // leaves,),
        in_specs=[pl.BlockSpec(memory_space=pltpu.SMEM)]
        + [VMEM] * (2 * N_Z)
        + [
            pl.BlockSpec((4, SLOTS, RANK, 2 * RANK), lambda i: (2, 0, 0, 0)),
            pl.BlockSpec((leaves, RANK, PTS), lambda i: (i, 0, 0)),
        ],
        out_specs=pl.BlockSpec((leaves, PTS, LANES), lambda i: (i, 0, 0)),
        out_shape=jax.ShapeDtypeStruct((SLOTS, PTS, LANES), BF),
        scratch_shapes=[pltpu.VMEM((SLOTS, RANK, LANES), BF)],
        cost_estimate=pl.CostEstimate(flops=800_000_000, bytes_accessed=7_000_000, transcendentals=0),
        compiler_params=pltpu.CompilerParams(vmem_limit_bytes=14 << 20),
        name="tail",
    )(where, *msgs, transitions, synthesis)


FAR_FIRST = (4, 5, 3, 7, 6, 2, 1)


def pipeline(features, analysis, transitions, synthesis):
    col = lax.axis_index("col")
    where = jnp.stack([lax.axis_index("row"), col >> 1, col & 1]).astype(jnp.int32)
    blocks = front(features, analysis, transitions)
    partner = lax.ppermute(blocks, "col", [(c, c ^ 1) for c in range(N_COL)])
    groups = []
    for b in range(2):
        sent = messages(b, where, blocks, partner, transitions)
        group = list(sent)
        for d in FAR_FIRST:
            group[d] = z_swap(sent[d], d)
        groups.append(group)
    arrived = []
    for b in range(2):
        merged = host_merge(where, groups[b])
        merged = to_target_row(merged, b)
        group = [merged[0]] * N_Z
        for d in FAR_FIRST:
            group[d] = z_swap(merged[d], d)
        arrived += group
    return tail(where, arrived, transitions, synthesis)


def solution(mesh):
    in_specs = (
        P(("row", "col"), None, None),
        P(("row", "col"), None, None),
        P(None, ("row", "col"), None, None),
        P(("row", "col"), None, None),
    )
    out_specs = P(("row", "col"), None, None)
    return jax.shard_map(
        pipeline, mesh=mesh, in_specs=in_specs, out_specs=out_specs, check_vma=False
    )
```

profile of v0, /device:TPU:2, one launch (start us, length us, event | category | flops | bytes accessed | tf_op | source)
XLA Modules:
  0.0 124.2 jit_solution(551709108521156640)
XLA Ops:
  0.0 8.1 %front.1.own_ref = bf16[16,64,512]{2,1,0:T(8,128)(2,1)} custom-call(bf16[16,256,512]{2,1,0:T(8,128)(2,1)} %f_ref.1, bf16[16,64,256]{2,1,0:T(8,128)(2,1)} %a_ref.1, bf16[12,16,64,128]{3,2,1,0:T(8,128)(2,1)} %refs_16_.1), custom_call_target="tpu_custom_call" | custom-call | flops 800000000 | bytes 7000000 | tf_op jit(solution)/shard_map/front/pallas_call | solution.py:81
  8.1 0.0 collective-permute-start
  8.1 0.1 pad_add_fusion.r_ref
  8.2 2.9 %collective-permute-done.partner_ref = bf16[16,64,512]{2,1,0:T(8,128)(2,1)} collective-permute-done((bf16[16,64,512]{2,1,0:T(8,128)(2,1)}, bf16[16,64,512]{2,1,0:T(8,128)(2,1)}, u32[]{:S(2)}, u32[]{:S(2)}) %collective-permute-start) | collective-permute-done | bytes 1048608 | tf_op jit(solution)/shard_map/ppermute | solution.py:208
  11.1 1.2 copy-done.1
  12.4 1.5 %shard_map.46 = (bf16[64,896]{1,0:T(8,128)(2,1)S(1)}, bf16[64,896]{1,0:T(8,128)(2,1)S(1)}, bf16[64,896]{1,0:T(8,128)(2,1)S(1)}, bf16[64,896]{1,0:T(8,128)(2,1)S(...) custom-call(s32[3]{0:T(128)S(1)} %pad_add_fusion.r_ref, ...), custom_call_target="tpu_custom_call" | custom-call | flops 70000000 | bytes 3000000 | tf_op jit(solution)/shard_map/pallas_call | solution.py:111
  13.9 2.0 %collective-permute-start.1 = (bf16[64,896]{1,0:T(8,128)(2,1)S(1)}, bf16[64,896]{1,0:T(8,128)(2,1)S(1)}, u32[]{:S(2)}, u32[]{:S(2)}) collective-permute-start(bf16[64,896]{1,0:T(8,128)(2,1)S(1)} %get-tuple-element.22), channel_id=1, source_target_pairs={{0,2},{1,3},{2,0},{3,1},{4,6},{5,7},{6,4},{7,5},{8,10},{9,11},{10,... | collective-permute-start | bytes 344072 | tf_op jit(solution)/shard_map/ppermute | solution.py:34
  15.9 3.3 %collective-permute-start.2 = (bf16[64,896]{1,0:T(8,128)(2,1)S(1)}, bf16[64,896]{1,0:T(8,128)(2,1)S(1)}, u32[]{:S(2)}, u32[]{:S(2)}) collective-permute-start(bf16[64,896]{1,0:T(8,128)(2,1)S(1)} %get-tuple-element.23), channel_id=1, source_target_pairs={{0,4},{1,5},{2,6},{3,7},{4,0},{5,1},{6,2},{7,3},{8,12},{9,13},{10,... | collective-permute-start | bytes 344072 | tf_op jit(solution)/shard_map/ppermute | solution.py:34
  19.2 0.0 collective-permute-start.3
  19.2 6.4 %collective-permute-start.4 = (bf16[64,896]{1,0:T(8,128)(2,1)S(1)}, bf16[64,896]{1,0:T(8,128)(2,1)S(1)}, u32[]{:S(2)}, u32[]{:S(2)}) collective-permute-start(bf16[64,896]{1,0:T(8,128)(2,1)S(1)} %get-tuple-element.25), channel_id=1, source_target_pairs={{0,8},{1,9},{2,10},{3,11},{4,12},{5,13},{6,14},{7,15},{8,0},{9,1},... | collective-permute-start | bytes 344072 | tf_op jit(solution)/shard_map/ppermute | solution.py:34
  25.6 0.0 collective-permute-start.5
  25.6 0.0 collective-permute-done.1.refs_1_
  25.6 4.6 %collective-permute-start.6 = (bf16[64,896]{1,0:T(8,128)(2,1)S(1)}, bf16[64,896]{1,0:T(8,128)(2,1)S(1)}, u32[]{:S(2)}, u32[]{:S(2)}) collective-permute-start(bf16[64,896]{1,0:T(8,128)(2,1)S(1)} %get-tuple-element.27), channel_id=1, source_target_pairs={{0,12},{1,13},{2,14},{3,15},{4,8},{5,9},{6,10},{7,11},{8,4},{9,5},... | collective-permute-start | bytes 344072 | tf_op jit(solution)/shard_map/ppermute | solution.py:34
  30.2 4.2 %collective-permute-done.2.refs_2_ = bf16[64,896]{1,0:T(8,128)(2,1)S(1)} collective-permute-done((bf16[64,896]{1,0:T(8,128)(2,1)S(1)}, bf16[64,896]{1,0:T(8,128)(2,1)S(1)}, u32[]{:S(2)}, u32[]{:S(2)}) %collective-permute-start.2) | collective-permute-done | bytes 114720 | tf_op jit(solution)/shard_map/ppermute | solution.py:34
  34.4 4.8 %collective-permute-start.7 = (bf16[64,896]{1,0:T(8,128)(2,1)S(1)}, bf16[64,896]{1,0:T(8,128)(2,1)S(1)}, u32[]{:S(2)}, u32[]{:S(2)}) collective-permute-start(bf16[64,896]{1,0:T(8,128)(2,1)S(1)} %get-tuple-element.28), channel_id=1, source_target_pairs={{0,14},{1,15},{2,12},{3,13},{4,10},{5,11},{6,8},{7,9},{8,6},{9,7},... | collective-permute-start | bytes 344072 | tf_op jit(solution)/shard_map/ppermute | solution.py:34
  39.2 1.5 %shard_map.48 = (bf16[64,896]{1,0:T(8,128)(2,1)S(1)}, bf16[64,896]{1,0:T(8,128)(2,1)S(1)}, bf16[64,896]{1,0:T(8,128)(2,1)S(1)}, bf16[64,896]{1,0:T(8,128)(2,1)S(...) custom-call(s32[3]{0:T(128)S(1)} %pad_add_fusion.r_ref, ...), custom_call_target="tpu_custom_call" | custom-call | flops 70000000 | bytes 3000000 | tf_op jit(solution)/shard_map/pallas_call | solution.py:111
  40.7 0.0 collective-permute-done.3.refs_3_
  40.7 0.1 collective-permute-start.16
  40.8 0.0 collective-permute-done.4.refs_4_
  40.9 2.3 %collective-permute-start.17 = (bf16[64,896]{1,0:T(8,128)(2,1)S(1)}, bf16[64,896]{1,0:T(8,128)(2,1)S(1)}, u32[]{:S(2)}, u32[]{:S(2)}) collective-permute-start(bf16[64,896]{1,0:T(8,128)(2,1)S(1)} %get-tuple-element.31), channel_id=1, source_target_pairs={{0,4},{1,5},{2,6},{3,7},{4,0},{5,1},{6,2},{7,3},{8,12},{9,13},{10,... | collective-permute-start | bytes 344072 | tf_op jit(solution)/shard_map/ppermute | solution.py:34
  43.1 0.0 collective-permute-done.5.refs_5_
  43.1 2.1 %collective-permute-start.18 = (bf16[64,896]{1,0:T(8,128)(2,1)S(1)}, bf16[64,896]{1,0:T(8,128)(2,1)S(1)}, u32[]{:S(2)}, u32[]{:S(2)}) collective-permute-start(bf16[64,896]{1,0:T(8,128)(2,1)S(1)} %get-tuple-element.32), channel_id=1, source_target_pairs={{0,6},{1,7},{2,4},{3,5},{4,2},{5,3},{6,0},{7,1},{8,14},{9,15},{10,... | collective-permute-start | bytes 344072 | tf_op jit(solution)/shard_map/ppermute | solution.py:34
  45.2 0.0 collective-permute-done.6.refs_6_
  45.2 1.2 collective-permute-done.7.refs_7_
  46.4 1.3 %shard_map.47 = bf16[8,64,512]{2,1,0:T(8,128)(2,1)S(1)} custom-call(s32[3]{0:T(128)S(1)} %pad_add_fusion.r_ref, bf16[64,896]{1,0:T(8,128)(2,1)S(1)} %get-tuple-element.21.refs_0_, bf16[64,896]{1,0:T(8,128)(2,1)S(1)} %collective-permute-done.1.refs_1_, bf16[64,896]{1,0:T(8,128)(2,1)S(1)} %collective-permute-done.2.refs_2_, ...), custom_call_target="tpu_custom_call" | custom-call | flops 200000000 | bytes 1400000 | tf_op jit(solution)/shard_map/pallas_call | solution.py:148
  47.7 4.0 %collective-permute-start.8 = (bf16[8,64,512]{2,1,0:T(8,128)(2,1)S(1)}, bf16[8,64,512]{2,1,0:T(8,128)(2,1)S(1)}, u32[]{:S(2)}, u32[]{:S(2)}) collective-permute-start(bf16[8,64,512]{2,1,0:T(8,128)(2,1)S(1)} %shard_map.47), channel_id=1, source_target_pairs={{0,0},{1,1},{2,34},{3,35},{4,68},{5,69},{6,102},{7,103},{8,136},{9... | collective-permute-start | bytes 1572872 | tf_op jit(solution)/shard_map/ppermute | solution.py:42
  51.7 5.9 %collective-permute-start.19 = (bf16[64,896]{1,0:T(8,128)(2,1)S(1)}, bf16[64,896]{1,0:T(8,128)(2,1)S(1)}, u32[]{:S(2)}, u32[]{:S(2)}) collective-permute-start(bf16[64,896]{1,0:T(8,128)(2,1)S(1)} %get-tuple-element.33), channel_id=1, source_target_pairs={{0,8},{1,9},{2,10},{3,11},{4,12},{5,13},{6,14},{7,15},{8,0},{9,1},... | collective-permute-start | bytes 344072 | tf_op jit(solution)/shard_map/ppermute | solution.py:34
  57.7 0.0 collective-permute-done.16.refs_1_
  57.7 0.0 collective-permute-start.20
  57.7 0.0 collective-permute-done.17.refs_2_
  57.7 2.8 %collective-permute-start.21 = (bf16[64,896]{1,0:T(8,128)(2,1)S(1)}, bf16[64,896]{1,0:T(8,128)(2,1)S(1)}, u32[]{:S(2)}, u32[]{:S(2)}) collective-permute-start(bf16[64,896]{1,0:T(8,128)(2,1)S(1)} %get-tuple-element.35), channel_id=1, source_target_pairs={{0,12},{1,13},{2,14},{3,15},{4,8},{5,9},{6,10},{7,11},{8,4},{9,5},... | collective-permute-start | bytes 344072 | tf_op jit(solution)/shard_map/ppermute | solution.py:34
  60.5 0.0 collective-permute-done.18.refs_3_
  60.5 0.5 collective-permute-start.22
  61.0 1.4 %collective-permute-done.19.refs_4_ = bf16[64,896]{1,0:T(8,128)(2,1)S(1)} collective-permute-done((bf16[64,896]{1,0:T(8,128)(2,1)S(1)}, bf16[64,896]{1,0:T(8,128)(2,1)S(1)}, u32[]{:S(2)}, u32[]{:S(2)}) %collective-permute-start.19) | collective-permute-done | bytes 114720 | tf_op jit(solution)/shard_map/ppermute | solution.py:34
  62.4 7.7 %collective-permute-done.20.refs_5_ = bf16[64,896]{1,0:T(8,128)(2,1)S(1)} collective-permute-done((bf16[64,896]{1,0:T(8,128)(2,1)S(1)}, bf16[64,896]{1,0:T(8,128)(2,1)S(1)}, u32[]{:S(2)}, u32[]{:S(2)}) %collective-permute-start.20) | collective-permute-done | bytes 114720 | tf_op jit(solution)/shard_map/ppermute | solution.py:34
  70.1 2.5 %collective-permute-done.21.refs_6_ = bf16[64,896]{1,0:T(8,128)(2,1)S(1)} collective-permute-done((bf16[64,896]{1,0:T(8,128)(2,1)S(1)}, bf16[64,896]{1,0:T(8,128)(2,1)S(1)}, u32[]{:S(2)}, u32[]{:S(2)}) %collective-permute-start.21) | collective-permute-done | bytes 114720 | tf_op jit(solution)/shard_map/ppermute | solution.py:34
  72.5 3.3 %collective-permute-done.22.refs_7_ = bf16[64,896]{1,0:T(8,128)(2,1)S(1)} collective-permute-done((bf16[64,896]{1,0:T(8,128)(2,1)S(1)}, bf16[64,896]{1,0:T(8,128)(2,1)S(1)}, u32[]{:S(2)}, u32[]{:S(2)}) %collective-permute-start.22) | collective-permute-done | bytes 114720 | tf_op jit(solution)/shard_map/ppermute | solution.py:34
  75.8 1.3 %shard_map.49 = bf16[8,64,512]{2,1,0:T(8,128)(2,1)S(1)} custom-call(s32[3]{0:T(128)S(1)} %pad_add_fusion.r_ref, bf16[64,896]{1,0:T(8,128)(2,1)S(1)} %get-tuple-element.29.refs_0_, bf16[64,896]{1,0:T(8,128)(2,1)S(1)} %collective-permute-done.16.refs_1_, bf16[64,896]{1,0:T(8,128)(2,1)S(1)} %collective-permute-done.17.refs_2_, ...), custom_call_target="tpu_custom_call" | custom-call | flops 200000000 | bytes 1400000 | tf_op jit(solution)/shard_map/pallas_call | solution.py:148
  77.1 0.3 collective-permute-start.23
  77.4 0.0 collective-permute-done.8
  77.5 4.4 %collective-permute-start.15 = (bf16[64,512]{1,0:T(8,128)(2,1)S(1)}, bf16[64,512]{1,0:T(8,128)(2,1)S(1)}, u32[]{:S(2)}, u32[]{:S(2)}) collective-permute-start(bf16[64,512]{1,0:T(8,128)(2,1)S(1)} %get-tuple-element.45), channel_id=1, source_target_pairs={{0,14},{1,15},{2,12},{3,13},{4,10},{5,11},{6,8},{7,9},{8,6},{9,7},... | collective-permute-start | bytes 196616 | tf_op jit(solution)/shard_map/ppermute | solution.py:34
  81.9 0.0 collective-permute-start.14
  81.9 3.4 %collective-permute-start.13 = (bf16[64,512]{1,0:T(8,128)(2,1)S(1)}, bf16[64,512]{1,0:T(8,128)(2,1)S(1)}, u32[]{:S(2)}, u32[]{:S(2)}) collective-permute-start(bf16[64,512]{1,0:T(8,128)(2,1)S(1)} %get-tuple-element.47), channel_id=1, source_target_pairs={{0,10},{1,11},{2,8},{3,9},{4,14},{5,15},{6,12},{7,13},{8,2},{9,3},... | collective-permute-start | bytes 196616 | tf_op jit(solution)/shard_map/ppermute | solution.py:34
  85.2 2.7 %collective-permute-start.12 = (bf16[64,512]{1,0:T(8,128)(2,1)S(1)}, bf16[64,512]{1,0:T(8,128)(2,1)S(1)}, u32[]{:S(2)}, u32[]{:S(2)}) collective-permute-start(bf16[64,512]{1,0:T(8,128)(2,1)S(1)} %get-tuple-element.48), channel_id=1, source_target_pairs={{0,8},{1,9},{2,10},{3,11},{4,12},{5,13},{6,14},{7,15},{8,0},{9,1},... | collective-permute-start | bytes 196616 | tf_op jit(solution)/shard_map/ppermute | solution.py:34
  87.9 2.3 %collective-permute-done.23 = bf16[8,64,512]{2,1,0:T(8,128)(2,1)S(1)} collective-permute-done((bf16[8,64,512]{2,1,0:T(8,128)(2,1)S(1)}, bf16[8,64,512]{2,1,0:T(8,128)(2,1)S(1)}, u32[]{:S(2)}, u32[]{:S(2)}) %collective-permute-start.23) | collective-permute-done | bytes 524320 | tf_op jit(solution)/shard_map/ppermute | solution.py:42
  90.2 1.3 %collective-permute-start.11 = (bf16[64,512]{1,0:T(8,128)(2,1)S(1)}, bf16[64,512]{1,0:T(8,128)(2,1)S(1)}, u32[]{:S(2)}, u32[]{:S(2)}) collective-permute-start(bf16[64,512]{1,0:T(8,128)(2,1)S(1)} %get-tuple-element.49), channel_id=1, source_target_pairs={{0,6},{1,7},{2,4},{3,5},{4,2},{5,3},{6,0},{7,1},{8,14},{9,15},{10,... | collective-permute-start | bytes 196616 | tf_op jit(solution)/shard_map/ppermute | solution.py:34
  91.6 1.2 %collective-permute-start.10 = (bf16[64,512]{1,0:T(8,128)(2,1)S(1)}, bf16[64,512]{1,0:T(8,128)(2,1)S(1)}, u32[]{:S(2)}, u32[]{:S(2)}) collective-permute-start(bf16[64,512]{1,0:T(8,128)(2,1)S(1)} %get-tuple-element.50), channel_id=1, source_target_pairs={{0,4},{1,5},{2,6},{3,7},{4,0},{5,1},{6,2},{7,3},{8,12},{9,13},{10,... | collective-permute-start | bytes 196616 | tf_op jit(solution)/shard_map/ppermute | solution.py:34
  92.8 1.9 %collective-permute-start.9 = (bf16[64,512]{1,0:T(8,128)(2,1)S(1)}, bf16[64,512]{1,0:T(8,128)(2,1)S(1)}, u32[]{:S(2)}, u32[]{:S(2)}) collective-permute-start(bf16[64,512]{1,0:T(8,128)(2,1)S(1)} %get-tuple-element.51), channel_id=1, source_target_pairs={{0,2},{1,3},{2,0},{3,1},{4,6},{5,7},{6,4},{7,5},{8,10},{9,11},{10,... | collective-permute-start | bytes 196616 | tf_op jit(solution)/shard_map/ppermute | solution.py:34
  94.7 6.1 %collective-permute-start.30 = (bf16[64,512]{1,0:T(8,128)(2,1)S(1)}, bf16[64,512]{1,0:T(8,128)(2,1)S(1)}, u32[]{:S(2)}, u32[]{:S(2)}) collective-permute-start(bf16[64,512]{1,0:T(8,128)(2,1)S(1)} %get-tuple-element.37), channel_id=1, source_target_pairs={{0,14},{1,15},{2,12},{3,13},{4,10},{5,11},{6,8},{7,9},{8,6},{9,7},... | collective-permute-start | bytes 196616 | tf_op jit(solution)/shard_map/ppermute | solution.py:34
  100.8 0.0 collective-permute-start.29
  100.8 0.0 collective-permute-done.11.refs_3_
  100.8 2.8 %collective-permute-start.28 = (bf16[64,512]{1,0:T(8,128)(2,1)S(1)}, bf16[64,512]{1,0:T(8,128)(2,1)S(1)}, u32[]{:S(2)}, u32[]{:S(2)}) collective-permute-start(bf16[64,512]{1,0:T(8,128)(2,1)S(1)} %get-tuple-element.39), channel_id=1, source_target_pairs={{0,10},{1,11},{2,8},{3,9},{4,14},{5,15},{6,12},{7,13},{8,2},{9,3},... | collective-permute-start | bytes 196616 | tf_op jit(solution)/shard_map/ppermute | solution.py:34
  103.6 3.3 %collective-permute-start.27 = (bf16[64,512]{1,0:T(8,128)(2,1)S(1)}, bf16[64,512]{1,0:T(8,128)(2,1)S(1)}, u32[]{:S(2)}, u32[]{:S(2)}) collective-permute-start(bf16[64,512]{1,0:T(8,128)(2,1)S(1)} %get-tuple-element.40), channel_id=1, source_target_pairs={{0,8},{1,9},{2,10},{3,11},{4,12},{5,13},{6,14},{7,15},{8,0},{9,1},... | collective-permute-start | bytes 196616 | tf_op jit(solution)/shard_map/ppermute | solution.py:34
  106.9 0.0 collective-permute-done.9.refs_1_
  106.9 1.0 collective-permute-start.26
  107.9 0.0 collective-permute-done.30.refs_15_
  107.9 1.0 collective-permute-start.25
  108.9 2.8 %collective-permute-start.24 = (bf16[64,512]{1,0:T(8,128)(2,1)S(1)}, bf16[64,512]{1,0:T(8,128)(2,1)S(1)}, u32[]{:S(2)}, u32[]{:S(2)}) collective-permute-start(bf16[64,512]{1,0:T(8,128)(2,1)S(1)} %get-tuple-element.43), channel_id=1, source_target_pairs={{0,2},{1,3},{2,0},{3,1},{4,6},{5,7},{6,4},{7,5},{8,10},{9,11},{10,... | collective-permute-start | bytes 196616 | tf_op jit(solution)/shard_map/ppermute | solution.py:34
  111.7 0.0 collective-permute-done.28.refs_13_
  111.7 1.7 %collective-permute-done.27.refs_12_ = bf16[64,512]{1,0:T(8,128)(2,1)S(1)} collective-permute-done((bf16[64,512]{1,0:T(8,128)(2,1)S(1)}, bf16[64,512]{1,0:T(8,128)(2,1)S(1)}, u32[]{:S(2)}, u32[]{:S(2)}) %collective-permute-start.27) | collective-permute-done | bytes 65568 | tf_op jit(solution)/shard_map/ppermute | solution.py:34
  113.3 1.7 %collective-permute-done.26.refs_11_ = bf16[64,512]{1,0:T(8,128)(2,1)S(1)} collective-permute-done((bf16[64,512]{1,0:T(8,128)(2,1)S(1)}, bf16[64,512]{1,0:T(8,128)(2,1)S(1)}, u32[]{:S(2)}, u32[]{:S(2)}) %collective-permute-start.26) | collective-permute-done | bytes 65568 | tf_op jit(solution)/shard_map/ppermute | solution.py:34
  115.1 2.4 %collective-permute-done.25.refs_10_ = bf16[64,512]{1,0:T(8,128)(2,1)S(1)} collective-permute-done((bf16[64,512]{1,0:T(8,128)(2,1)S(1)}, bf16[64,512]{1,0:T(8,128)(2,1)S(1)}, u32[]{:S(2)}, u32[]{:S(2)}) %collective-permute-start.25) | collective-permute-done | bytes 65568 | tf_op jit(solution)/shard_map/ppermute | solution.py:34
  117.4 0.0 collective-permute-done.24.refs_9_
  117.4 6.7 %tail.1 = bf16[16,256,512]{2,1,0:T(8,128)(2,1)} custom-call(s32[3]{0:T(128)S(1)} %pad_add_fusion.r_ref, bf16[64,512]{1,0:T(8,128)(2,1)S(1)} %get-tuple-element.52.refs_0_, bf16[64,512]{1,0:T(8,128)(2,1)S(1)} %collective-permute-done.9.refs_1_, bf16[64,512]{1,0:T(8,128)(2,1)S(1)} %collective-permute-done.10.refs_2_, ...), custom_call_target="tpu_custom_call" | custom-call | flops 800000000 | bytes 7000000 | tf_op jit(solution)/shard_map/tail/pallas_call | solution.py:183
  (13 shorter events, 0.1 us)
Async XLA Ops:
  0.0 11.1 %copy-start = (bf16[12,16,64,128]{3,2,1,0:T(8,128)(2,1)S(1)}, bf16[12,16,64,128]{3,2,1,0:T(8,128)(2,1)}, u32[]{:S(2)}) copy-start(bf16[12,16,64,128]{3,2,1,0:T(8,128)(2,1)} %refs_16_.1) | copy-start | bytes 9437188
  8.1 3.0 %collective-permute-start = (bf16[16,64,512]{2,1,0:T(8,128)(2,1)}, bf16[16,64,512]{2,1,0:T(8,128)(2,1)}, u32[]{:S(2)}, u32[]{:S(2)}) collective-permute-start(bf16[16,64,512]{2,1,0:T(8,128)(2,1)} %front.1.own_ref), channel_id=1, source_target_pairs={{0,1},{1,0},{2,3},{3,2},{4,5},{5,4},{6,7},{7,6},{8,9},{9,8},{10,11... | collective-permute-start | bytes 3145736 | tf_op jit(solution)/shard_map/ppermute | solution.py:208
  11.1 1.2 copy-start.1
  13.9 11.7 %collective-permute-start.1 = (bf16[64,896]{1,0:T(8,128)(2,1)S(1)}, bf16[64,896]{1,0:T(8,128)(2,1)S(1)}, u32[]{:S(2)}, u32[]{:S(2)}) collective-permute-start(bf16[64,896]{1,0:T(8,128)(2,1)S(1)} %get-tuple-element.22), channel_id=1, source_target_pairs={{0,2},{1,3},{2,0},{3,1},{4,6},{5,7},{6,4},{7,5},{8,10},{9,11},{10,... | collective-permute-start | bytes 344072 | tf_op jit(solution)/shard_map/ppermute | solution.py:34
  15.9 18.5 %collective-permute-start.2 = (bf16[64,896]{1,0:T(8,128)(2,1)S(1)}, bf16[64,896]{1,0:T(8,128)(2,1)S(1)}, u32[]{:S(2)}, u32[]{:S(2)}) collective-permute-start(bf16[64,896]{1,0:T(8,128)(2,1)S(1)} %get-tuple-element.23), channel_id=1, source_target_pairs={{0,4},{1,5},{2,6},{3,7},{4,0},{5,1},{6,2},{7,3},{8,12},{9,13},{10,... | collective-permute-start | bytes 344072 | tf_op jit(solution)/shard_map/ppermute | solution.py:34
  19.2 21.6 %collective-permute-start.3 = (bf16[64,896]{1,0:T(8,128)(2,1)S(1)}, bf16[64,896]{1,0:T(8,128)(2,1)S(1)}, u32[]{:S(2)}, u32[]{:S(2)}) collective-permute-start(bf16[64,896]{1,0:T(8,128)(2,1)S(1)} %get-tuple-element.24), channel_id=1, source_target_pairs={{0,6},{1,7},{2,4},{3,5},{4,2},{5,3},{6,0},{7,1},{8,14},{9,15},{10,... | collective-permute-start | bytes 344072 | tf_op jit(solution)/shard_map/ppermute | solution.py:34
  19.2 21.7 %collective-permute-start.4 = (bf16[64,896]{1,0:T(8,128)(2,1)S(1)}, bf16[64,896]{1,0:T(8,128)(2,1)S(1)}, u32[]{:S(2)}, u32[]{:S(2)}) collective-permute-start(bf16[64,896]{1,0:T(8,128)(2,1)S(1)} %get-tuple-element.25), channel_id=1, source_target_pairs={{0,8},{1,9},{2,10},{3,11},{4,12},{5,13},{6,14},{7,15},{8,0},{9,1},... | collective-permute-start | bytes 344072 | tf_op jit(solution)/shard_map/ppermute | solution.py:34
  25.6 17.5 %collective-permute-start.5 = (bf16[64,896]{1,0:T(8,128)(2,1)S(1)}, bf16[64,896]{1,0:T(8,128)(2,1)S(1)}, u32[]{:S(2)}, u32[]{:S(2)}) collective-permute-start(bf16[64,896]{1,0:T(8,128)(2,1)S(1)} %get-tuple-element.26), channel_id=1, source_target_pairs={{0,10},{1,11},{2,8},{3,9},{4,14},{5,15},{6,12},{7,13},{8,2},{9,3},... | collective-permute-start | bytes 344072 | tf_op jit(solution)/shard_map/ppermute | solution.py:34
  25.6 19.7 %collective-permute-start.6 = (bf16[64,896]{1,0:T(8,128)(2,1)S(1)}, bf16[64,896]{1,0:T(8,128)(2,1)S(1)}, u32[]{:S(2)}, u32[]{:S(2)}) collective-permute-start(bf16[64,896]{1,0:T(8,128)(2,1)S(1)} %get-tuple-element.27), channel_id=1, source_target_pairs={{0,12},{1,13},{2,14},{3,15},{4,8},{5,9},{6,10},{7,11},{8,4},{9,5},... | collective-permute-start | bytes 344072 | tf_op jit(solution)/shard_map/ppermute | solution.py:34
  34.4 83.0 %copy-start.2 = (bf16[16,64,256]{2,1,0:T(8,128)(2,1)S(1)}, bf16[16,64,256]{2,1,0:T(8,128)(2,1)}, u32[]{:S(2)}) copy-start(bf16[16,64,256]{2,1,0:T(8,128)(2,1)} %refs_17_.1) | copy-start | bytes 1572868
  34.4 12.0 %collective-permute-start.7 = (bf16[64,896]{1,0:T(8,128)(2,1)S(1)}, bf16[64,896]{1,0:T(8,128)(2,1)S(1)}, u32[]{:S(2)}, u32[]{:S(2)}) collective-permute-start(bf16[64,896]{1,0:T(8,128)(2,1)S(1)} %get-tuple-element.28), channel_id=1, source_target_pairs={{0,14},{1,15},{2,12},{3,13},{4,10},{5,11},{6,8},{7,9},{8,6},{9,7},... | collective-permute-start | bytes 344072 | tf_op jit(solution)/shard_map/ppermute | solution.py:34
  40.7 16.9 %collective-permute-start.16 = (bf16[64,896]{1,0:T(8,128)(2,1)S(1)}, bf16[64,896]{1,0:T(8,128)(2,1)S(1)}, u32[]{:S(2)}, u32[]{:S(2)}) collective-permute-start(bf16[64,896]{1,0:T(8,128)(2,1)S(1)} %get-tuple-element.30), channel_id=1, source_target_pairs={{0,2},{1,3},{2,0},{3,1},{4,6},{5,7},{6,4},{7,5},{8,10},{9,11},{10,... | collective-permute-start | bytes 344072 | tf_op jit(solution)/shard_map/ppermute | solution.py:34
  40.9 16.8 %collective-permute-start.17 = (bf16[64,896]{1,0:T(8,128)(2,1)S(1)}, bf16[64,896]{1,0:T(8,128)(2,1)S(1)}, u32[]{:S(2)}, u32[]{:S(2)}) collective-permute-start(bf16[64,896]{1,0:T(8,128)(2,1)S(1)} %get-tuple-element.31), channel_id=1, source_target_pairs={{0,4},{1,5},{2,6},{3,7},{4,0},{5,1},{6,2},{7,3},{8,12},{9,13},{10,... | collective-permute-start | bytes 344072 | tf_op jit(solution)/shard_map/ppermute | solution.py:34
  43.1 17.4 %collective-permute-start.18 = (bf16[64,896]{1,0:T(8,128)(2,1)S(1)}, bf16[64,896]{1,0:T(8,128)(2,1)S(1)}, u32[]{:S(2)}, u32[]{:S(2)}) collective-permute-start(bf16[64,896]{1,0:T(8,128)(2,1)S(1)} %get-tuple-element.32), channel_id=1, source_target_pairs={{0,6},{1,7},{2,4},{3,5},{4,2},{5,3},{6,0},{7,1},{8,14},{9,15},{10,... | collective-permute-start | bytes 344072 | tf_op jit(solution)/shard_map/ppermute | solution.py:34
  47.7 29.7 %collective-permute-start.8 = (bf16[8,64,512]{2,1,0:T(8,128)(2,1)S(1)}, bf16[8,64,512]{2,1,0:T(8,128)(2,1)S(1)}, u32[]{:S(2)}, u32[]{:S(2)}) collective-permute-start(bf16[8,64,512]{2,1,0:T(8,128)(2,1)S(1)} %shard_map.47), channel_id=1, source_target_pairs={{0,0},{1,1},{2,34},{3,35},{4,68},{5,69},{6,102},{7,103},{8,136},{9... | collective-permute-start | bytes 1572872 | tf_op jit(solution)/shard_map/ppermute | solution.py:42
  51.7 10.7 %collective-permute-start.19 = (bf16[64,896]{1,0:T(8,128)(2,1)S(1)}, bf16[64,896]{1,0:T(8,128)(2,1)S(1)}, u32[]{:S(2)}, u32[]{:S(2)}) collective-permute-start(bf16[64,896]{1,0:T(8,128)(2,1)S(1)} %get-tuple-element.33), channel_id=1, source_target_pairs={{0,8},{1,9},{2,10},{3,11},{4,12},{5,13},{6,14},{7,15},{8,0},{9,1},... | collective-permute-start | bytes 344072 | tf_op jit(solution)/shard_map/ppermute | solution.py:34
  57.7 12.4 %collective-permute-start.20 = (bf16[64,896]{1,0:T(8,128)(2,1)S(1)}, bf16[64,896]{1,0:T(8,128)(2,1)S(1)}, u32[]{:S(2)}, u32[]{:S(2)}) collective-permute-start(bf16[64,896]{1,0:T(8,128)(2,1)S(1)} %get-tuple-element.34), channel_id=1, source_target_pairs={{0,10},{1,11},{2,8},{3,9},{4,14},{5,15},{6,12},{7,13},{8,2},{9,3},... | collective-permute-start | bytes 344072 | tf_op jit(solution)/shard_map/ppermute | solution.py:34
  57.7 14.8 %collective-permute-start.21 = (bf16[64,896]{1,0:T(8,128)(2,1)S(1)}, bf16[64,896]{1,0:T(8,128)(2,1)S(1)}, u32[]{:S(2)}, u32[]{:S(2)}) collective-permute-start(bf16[64,896]{1,0:T(8,128)(2,1)S(1)} %get-tuple-element.35), channel_id=1, source_target_pairs={{0,12},{1,13},{2,14},{3,15},{4,8},{5,9},{6,10},{7,11},{8,4},{9,5},... | collective-permute-start | bytes 344072 | tf_op jit(solution)/shard_map/ppermute | solution.py:34
  60.5 15.3 %collective-permute-start.22 = (bf16[64,896]{1,0:T(8,128)(2,1)S(1)}, bf16[64,896]{1,0:T(8,128)(2,1)S(1)}, u32[]{:S(2)}, u32[]{:S(2)}) collective-permute-start(bf16[64,896]{1,0:T(8,128)(2,1)S(1)} %get-tuple-element.36), channel_id=1, source_target_pairs={{0,14},{1,15},{2,12},{3,13},{4,10},{5,11},{6,8},{7,9},{8,6},{9,7},... | collective-permute-start | bytes 344072 | tf_op jit(solution)/shard_map/ppermute | solution.py:34
  77.1 13.1 %collective-permute-start.23 = (bf16[8,64,512]{2,1,0:T(8,128)(2,1)S(1)}, bf16[8,64,512]{2,1,0:T(8,128)(2,1)S(1)}, u32[]{:S(2)}, u32[]{:S(2)}) collective-permute-start(bf16[8,64,512]{2,1,0:T(8,128)(2,1)S(1)} %shard_map.49), channel_id=1, source_target_pairs={{0,16},{1,17},{2,50},{3,51},{4,84},{5,85},{6,118},{7,119},{8,152},... | collective-permute-start | bytes 1572872 | tf_op jit(solution)/shard_map/ppermute | solution.py:42
  77.5 14.1 %collective-permute-start.15 = (bf16[64,512]{1,0:T(8,128)(2,1)S(1)}, bf16[64,512]{1,0:T(8,128)(2,1)S(1)}, u32[]{:S(2)}, u32[]{:S(2)}) collective-permute-start(bf16[64,512]{1,0:T(8,128)(2,1)S(1)} %get-tuple-element.45), channel_id=1, source_target_pairs={{0,14},{1,15},{2,12},{3,13},{4,10},{5,11},{6,8},{7,9},{8,6},{9,7},... | collective-permute-start | bytes 196616 | tf_op jit(solution)/shard_map/ppermute | solution.py:34
  81.9 10.9 %collective-permute-start.14 = (bf16[64,512]{1,0:T(8,128)(2,1)S(1)}, bf16[64,512]{1,0:T(8,128)(2,1)S(1)}, u32[]{:S(2)}, u32[]{:S(2)}) collective-permute-start(bf16[64,512]{1,0:T(8,128)(2,1)S(1)} %get-tuple-element.46), channel_id=1, source_target_pairs={{0,12},{1,13},{2,14},{3,15},{4,8},{5,9},{6,10},{7,11},{8,4},{9,5},... | collective-permute-start | bytes 196616 | tf_op jit(solution)/shard_map/ppermute | solution.py:34
  81.9 12.9 %collective-permute-start.13 = (bf16[64,512]{1,0:T(8,128)(2,1)S(1)}, bf16[64,512]{1,0:T(8,128)(2,1)S(1)}, u32[]{:S(2)}, u32[]{:S(2)}) collective-permute-start(bf16[64,512]{1,0:T(8,128)(2,1)S(1)} %get-tuple-element.47), channel_id=1, source_target_pairs={{0,10},{1,11},{2,8},{3,9},{4,14},{5,15},{6,12},{7,13},{8,2},{9,3},... | collective-permute-start | bytes 196616 | tf_op jit(solution)/shard_map/ppermute | solution.py:34
  85.2 15.6 %collective-permute-start.12 = (bf16[64,512]{1,0:T(8,128)(2,1)S(1)}, bf16[64,512]{1,0:T(8,128)(2,1)S(1)}, u32[]{:S(2)}, u32[]{:S(2)}) collective-permute-start(bf16[64,512]{1,0:T(8,128)(2,1)S(1)} %get-tuple-element.48), channel_id=1, source_target_pairs={{0,8},{1,9},{2,10},{3,11},{4,12},{5,13},{6,14},{7,15},{8,0},{9,1},... | collective-permute-start | bytes 196616 | tf_op jit(solution)/shard_map/ppermute | solution.py:34
  90.2 10.6 %collective-permute-start.11 = (bf16[64,512]{1,0:T(8,128)(2,1)S(1)}, bf16[64,512]{1,0:T(8,128)(2,1)S(1)}, u32[]{:S(2)}, u32[]{:S(2)}) collective-permute-start(bf16[64,512]{1,0:T(8,128)(2,1)S(1)} %get-tuple-element.49), channel_id=1, source_target_pairs={{0,6},{1,7},{2,4},{3,5},{4,2},{5,3},{6,0},{7,1},{8,14},{9,15},{10,... | collective-permute-start | bytes 196616 | tf_op jit(solution)/shard_map/ppermute | solution.py:34
  91.6 12.0 %collective-permute-start.10 = (bf16[64,512]{1,0:T(8,128)(2,1)S(1)}, bf16[64,512]{1,0:T(8,128)(2,1)S(1)}, u32[]{:S(2)}, u32[]{:S(2)}) collective-permute-start(bf16[64,512]{1,0:T(8,128)(2,1)S(1)} %get-tuple-element.50), channel_id=1, source_target_pairs={{0,4},{1,5},{2,6},{3,7},{4,0},{5,1},{6,2},{7,3},{8,12},{9,13},{10,... | collective-permute-start | bytes 196616 | tf_op jit(solution)/shard_map/ppermute | solution.py:34
  92.8 14.0 %collective-permute-start.9 = (bf16[64,512]{1,0:T(8,128)(2,1)S(1)}, bf16[64,512]{1,0:T(8,128)(2,1)S(1)}, u32[]{:S(2)}, u32[]{:S(2)}) collective-permute-start(bf16[64,512]{1,0:T(8,128)(2,1)S(1)} %get-tuple-element.51), channel_id=1, source_target_pairs={{0,2},{1,3},{2,0},{3,1},{4,6},{5,7},{6,4},{7,5},{8,10},{9,11},{10,... | collective-permute-start | bytes 196616 | tf_op jit(solution)/shard_map/ppermute | solution.py:34
  94.7 13.1 %collective-permute-start.30 = (bf16[64,512]{1,0:T(8,128)(2,1)S(1)}, bf16[64,512]{1,0:T(8,128)(2,1)S(1)}, u32[]{:S(2)}, u32[]{:S(2)}) collective-permute-start(bf16[64,512]{1,0:T(8,128)(2,1)S(1)} %get-tuple-element.37), channel_id=1, source_target_pairs={{0,14},{1,15},{2,12},{3,13},{4,10},{5,11},{6,8},{7,9},{8,6},{9,7},... | collective-permute-start | bytes 196616 | tf_op jit(solution)/shard_map/ppermute | solution.py:34
  100.8 8.1 %collective-permute-start.29 = (bf16[64,512]{1,0:T(8,128)(2,1)S(1)}, bf16[64,512]{1,0:T(8,128)(2,1)S(1)}, u32[]{:S(2)}, u32[]{:S(2)}) collective-permute-start(bf16[64,512]{1,0:T(8,128)(2,1)S(1)} %get-tuple-element.38), channel_id=1, source_target_pairs={{0,12},{1,13},{2,14},{3,15},{4,8},{5,9},{6,10},{7,11},{8,4},{9,5},... | collective-permute-start | bytes 196616 | tf_op jit(solution)/shard_map/ppermute | solution.py:34
  100.8 10.8 %collective-permute-start.28 = (bf16[64,512]{1,0:T(8,128)(2,1)S(1)}, bf16[64,512]{1,0:T(8,128)(2,1)S(1)}, u32[]{:S(2)}, u32[]{:S(2)}) collective-permute-start(bf16[64,512]{1,0:T(8,128)(2,1)S(1)} %get-tuple-element.39), channel_id=1, source_target_pairs={{0,10},{1,11},{2,8},{3,9},{4,14},{5,15},{6,12},{7,13},{8,2},{9,3},... | collective-permute-start | bytes 196616 | tf_op jit(solution)/shard_map/ppermute | solution.py:34
  103.6 9.7 %collective-permute-start.27 = (bf16[64,512]{1,0:T(8,128)(2,1)S(1)}, bf16[64,512]{1,0:T(8,128)(2,1)S(1)}, u32[]{:S(2)}, u32[]{:S(2)}) collective-permute-start(bf16[64,512]{1,0:T(8,128)(2,1)S(1)} %get-tuple-element.40), channel_id=1, source_target_pairs={{0,8},{1,9},{2,10},{3,11},{4,12},{5,13},{6,14},{7,15},{8,0},{9,1},... | collective-permute-start | bytes 196616 | tf_op jit(solution)/shard_map/ppermute | solution.py:34
  106.9 8.2 %collective-permute-start.26 = (bf16[64,512]{1,0:T(8,128)(2,1)S(1)}, bf16[64,512]{1,0:T(8,128)(2,1)S(1)}, u32[]{:S(2)}, u32[]{:S(2)}) collective-permute-start(bf16[64,512]{1,0:T(8,128)(2,1)S(1)} %get-tuple-element.41), channel_id=1, source_target_pairs={{0,6},{1,7},{2,4},{3,5},{4,2},{5,3},{6,0},{7,1},{8,14},{9,15},{10,... | collective-permute-start | bytes 196616 | tf_op jit(solution)/shard_map/ppermute | solution.py:34
  107.9 9.6 %collective-permute-start.25 = (bf16[64,512]{1,0:T(8,128)(2,1)S(1)}, bf16[64,512]{1,0:T(8,128)(2,1)S(1)}, u32[]{:S(2)}, u32[]{:S(2)}) collective-permute-start(bf16[64,512]{1,0:T(8,128)(2,1)S(1)} %get-tuple-element.42), channel_id=1, source_target_pairs={{0,4},{1,5},{2,6},{3,7},{4,0},{5,1},{6,2},{7,3},{8,12},{9,13},{10,... | collective-permute-start | bytes 196616 | tf_op jit(solution)/shard_map/ppermute | solution.py:34
  108.9 8.5 %collective-permute-start.24 = (bf16[64,512]{1,0:T(8,128)(2,1)S(1)}, bf16[64,512]{1,0:T(8,128)(2,1)S(1)}, u32[]{:S(2)}, u32[]{:S(2)}) collective-permute-start(bf16[64,512]{1,0:T(8,128)(2,1)S(1)} %get-tuple-element.43), channel_id=1, source_target_pairs={{0,2},{1,3},{2,0},{3,1},{4,6},{5,7},{6,4},{7,5},{8,10},{9,11},{10,... | collective-permute-start | bytes 196616 | tf_op jit(solution)/shard_map/ppermute | solution.py:34
where the time goes:
time: 124 us
  starting transfers between devices  71 us (57%)
  waiting for transfers between devices  31.2 us (25%)
  Pallas kernels  20.5 us (17%)
  local copies, waits for them, and re-layouts  1.3 us (1%)
    ppermute x28, starting transfers between devices, z_swap(): return lax.ppermute(array, 'col', [(c, c ^ 2 * d) for c in range(N_COL)])  66.6 us
    ppermute x28, waiting for transfers between devices, z_swap(): return lax.ppermute(array, 'col', [(c, c ^ 2 * d) for c in range(N_COL)])  26 us
    pallas_call x1, Pallas kernels, front(): pl.pallas_call(functools.partial(front_kernel, leaves), grid=(SLOTS // le...  8.12 us
    pallas_call x1, Pallas kernels, tail(): pl.pallas_call(functools.partial(tail_kernel, leaves), grid=(SLOTS // lea...  6.74 us
    ppermute x2, starting transfers between devices, to_target_row(): return lax.ppermute(array, ('row', 'col'), pairs)  4.34 us
    pallas_call x2, Pallas kernels, messages(): pl.pallas_call(functools.partial(message_kernel, b), grid=(1,), in_specs=...  3.07 us
    ppermute x1, waiting for transfers between devices, pipeline(): partner = lax.ppermute(blocks, 'col', [(c, c ^ 1) for c in range(N_COL)])  2.92 us
    pallas_call x2, Pallas kernels, host_merge(): pl.pallas_call(host_kernel, in_specs=[pl.BlockSpec(memory_space=pltpu.SME...  2.54 us
  transfers between devices with their start and end apart: 31, of which 11 were waited for; matrix products, arithmetic and copies ran while one was open for 0% of the time, Pallas kernels for 3%

commit v1 on v0

v1 whole, which is shorter than its diff:
```python
import functools

import jax
import jax.numpy as jnp
from jax import lax
from jax.experimental import pallas as pl
from jax.experimental.pallas import tpu as pltpu
from jax.sharding import PartitionSpec as P


RANK = 64
LANES = 512
PTS = 256
SLOTS = 16
N_ROW = 16
N_COL = 16
N_Z = 8
Z_LEVELS = 3
PAIR = 2 * RANK
MSG = LANES + Z_LEVELS * PAIR
BF = jnp.bfloat16
F32 = jnp.float32
VMEM = pl.BlockSpec(memory_space=pltpu.VMEM)
SMEM = pl.BlockSpec(memory_space=pltpu.SMEM)
HBM = pl.BlockSpec(memory_space=pltpu.HBM)
FAR_FIRST = (4, 5, 3, 7, 6, 2, 1)
FAR = (4, 5)
NEAR = (3, 7, 6, 2, 1)


def base_of(r_ref):
    return r_ref[0] ^ r_ref[1] ^ (10 * r_ref[2])


def z_swap(array, d):
    return lax.ppermute(array, "col", [(c, c ^ (2 * d)) for c in range(N_COL)])


def to_target_row(array, b, d=0):
    pairs = []
    for r in range(N_ROW):
        for c in range(N_COL):
            to_col = c ^ (2 * d)
            to_row = r ^ (to_col >> 1) ^ (8 * b) ^ (10 * (c & 1))
            pairs.append((r * N_COL + c, to_row * N_COL + to_col))
    return lax.ppermute(array, ("row", "col"), pairs)


def dot(a, b):
    return lax.dot_general(a, b, (((1,), (0,)), ((), ())), preferred_element_type=F32)


def merge_pair(c_ref, lo, hi, t_lo, t_hi):
    joined = jnp.concatenate([c_ref[lo], c_ref[hi]], axis=0)
    merged = dot(jnp.concatenate([t_lo, t_hi], axis=0), joined).astype(BF)
    c_ref[lo] = merged[:RANK]
    c_ref[hi] = merged[RANK:]


def front_kernel(f_hbm, a_hbm, t_hbm, c_ref, f_buf, a_buf, t_buf, f_sem, t_sem, a_sem):
    f_copies = [pltpu.make_async_copy(f_hbm.at[l], f_buf.at[l], f_sem.at[l]) for l in range(SLOTS)]
    a_copies = [
        pltpu.make_async_copy(a_hbm.at[pl.ds(4 * i, 4)], a_buf.at[pl.ds(4 * i, 4)], a_sem.at[i]) for i in range(4)
    ]
    t_copies = [pltpu.make_async_copy(t_hbm.at[e], t_buf.at[e], t_sem.at[e]) for e in range(4)]
    for l in range(SLOTS):
        if l % 4 == 0:
            a_copies[l // 4].start()
        f_copies[l].start()
        if l in (3, 7):
            t_copies[2 * (l // 4)].start()
            t_copies[2 * (l // 4) + 1].start()

    def level(e, first, count):
        stride = 1 << e
        for lo in range(first, first + count):
            if not lo & stride:
                merge_pair(c_ref, lo, lo + stride, t_buf[e, lo], t_buf[e, lo + stride])

    for group in range(4):
        a_copies[group].wait()
        for l in range(4 * group, 4 * group + 4):
            f_copies[l].wait()
        if group == 1:
            t_copies[0].wait()
            t_copies[1].wait()
        if group == 3:
            t_copies[2].wait()
            t_copies[3].wait()
        for l in range(4 * group, 4 * group + 4):
            c_ref[l] = dot(a_buf[l], f_buf[l]).astype(BF)
        if group:
            level(0, 4 * group - 4, 4)
            level(1, 4 * group - 4, 4)
        if group == 3:
            level(2, 0, 8)
    level(0, 12, 4)
    level(1, 12, 4)
    level(2, 8, 8)
    level(3, 0, 16)


def front(features, analysis, transitions):
    return pl.pallas_call(
        front_kernel,
        in_specs=[HBM] * 3,
        out_specs=VMEM,
        out_shape=jax.ShapeDtypeStruct((SLOTS, RANK, LANES), BF),
        scratch_shapes=[
            pltpu.VMEM((SLOTS, PTS, LANES), BF),
            pltpu.VMEM((SLOTS, RANK, PTS), BF),
            pltpu.VMEM((4, SLOTS, RANK, PAIR), BF),
            pltpu.SemaphoreType.DMA((SLOTS,)),
            pltpu.SemaphoreType.DMA((4,)),
            pltpu.SemaphoreType.DMA((4,)),
        ],
        cost_estimate=pl.CostEstimate(flops=800_000_000, bytes_accessed=7_000_000, transcendentals=0),
        compiler_params=pltpu.CompilerParams(vmem_limit_bytes=65_600_000),
        name="front",
    )(features, analysis, transitions)


def message_kernel(b, r_ref, own_ref, partner_ref, t_ref, *outs):
    base = base_of(r_ref)
    for core in range(2):

        @pl.when(r_ref[2] == core)
        def _(low=partner_ref if core else own_ref, high=own_ref if core else partner_ref):
            for d in range(N_Z):
                s = base ^ (d | 8 * b)
                joined = jnp.concatenate([low[s], high[s]], axis=0)
                outs[d][:, :LANES] = dot(t_ref[0, s], joined).astype(BF)
                for e in range(Z_LEVELS):
                    outs[d][:, LANES + e * PAIR : LANES + (e + 1) * PAIR] = t_ref[1 + e, s]


def messages(b, where, own, partner, t_mid):
    return pl.pallas_call(
        functools.partial(message_kernel, b),
        in_specs=[SMEM, VMEM, VMEM, VMEM],
        out_specs=[VMEM] * N_Z,
        out_shape=[jax.ShapeDtypeStruct((RANK, MSG), BF)] * N_Z,
        cost_estimate=pl.CostEstimate(flops=70_000_000, bytes_accessed=3_000_000, transcendentals=0),
        compiler_params=pltpu.CompilerParams(vmem_limit_bytes=8 << 20),
    )(where, own, partner, t_mid)


def host_kernel(r_ref, *refs):
    msgs, (out, c_ref) = refs[:N_Z], refs[N_Z:]
    for d in range(N_Z):
        c_ref[r_ref[1] ^ d] = msgs[d][...]
    for e in range(Z_LEVELS):
        stride = 1 << e
        lanes = slice(LANES + e * PAIR, LANES + (e + 1) * PAIR)
        for lo in range(N_Z):
            if lo & stride:
                continue
            hi = lo + stride
            joined = jnp.concatenate([c_ref[lo, :, :LANES], c_ref[hi, :, :LANES]], axis=0)
            weights = jnp.concatenate([c_ref[lo, :, lanes], c_ref[hi, :, lanes]], axis=0)
            merged = dot(weights, joined).astype(BF)
            for z, block in ((lo, merged[:RANK]), (hi, merged[RANK:])):
                if e < Z_LEVELS - 1:
                    c_ref[z, :, :LANES] = block
                else:
                    out[r_ref[1] ^ z] = block


def host_merge(where, msgs):
    return pl.pallas_call(
        host_kernel,
        in_specs=[SMEM] + [VMEM] * N_Z,
        out_specs=VMEM,
        out_shape=jax.ShapeDtypeStruct((N_Z, RANK, LANES), BF),
        scratch_shapes=[pltpu.VMEM((N_Z, RANK, MSG), BF)],
        cost_estimate=pl.CostEstimate(flops=200_000_000, bytes_accessed=1_400_000, transcendentals=0),
        compiler_params=pltpu.CompilerParams(vmem_limit_bytes=6 << 20),
    )(where, *msgs)


def half_levels(b, r_ref, msgs, t_ref, c_ref):
    base = base_of(r_ref)
    top = (base & 8) ^ (8 * b)
    for d in range(N_Z):
        c_ref[base ^ (d | 8 * b)] = msgs[d][...]
    for e in range(3):
        stride = 1 << e
        for j in range(N_Z):
            if j & stride:
                continue
            lo, hi = top + j, top + j + stride
            merge_pair(c_ref, lo, hi, t_ref[e, lo], t_ref[e, hi])


def first_half_kernel(r_ref, *refs):
    msgs, (t_ref, c_ref) = refs[:N_Z], refs[N_Z:]
    half_levels(0, r_ref, msgs, t_ref, c_ref)


def first_half(where, msgs, t_tail):
    return pl.pallas_call(
        first_half_kernel,
        in_specs=[SMEM] + [VMEM] * (N_Z + 1),
        out_specs=VMEM,
        out_shape=jax.ShapeDtypeStruct((SLOTS, RANK, LANES), BF),
        cost_estimate=pl.CostEstimate(flops=200_000_000, bytes_accessed=1_400_000, transcendentals=0),
        compiler_params=pltpu.CompilerParams(vmem_limit_bytes=6 << 20),
        name="first_half",
    )(where, *msgs, t_tail)


def tail_kernel(r_ref, *refs):
    msgs, (half_ref, t_ref, s_ref, o_hbm, c_ref, o_buf, sem) = refs[:N_Z], refs[N_Z:]
    base = base_of(r_ref)
    half_levels(1, r_ref, msgs, t_ref, c_ref)
    for j in range(N_Z):
        c_ref[(base & 8) + j] = half_ref[(base & 8) + j]
    copies = []
    for j in range(N_Z):
        merge_pair(c_ref, j, j + 8, t_ref[3, j], t_ref[3, j + 8])
        for l in (j, j + 8):
            o_buf[l] = lax.dot_general(
                s_ref[l], c_ref[l], (((0,), (0,)), ((), ())), preferred_element_type=F32
            ).astype(BF)
            copies.append(pltpu.make_async_copy(o_buf.at[l], o_hbm.at[l], sem.at[l]))
            copies[-1].start()
    for copy in copies:
        copy.wait()


def tail(where, msgs, half, t_tail, synthesis):
    return pl.pallas_call(
        tail_kernel,
        in_specs=[SMEM] + [VMEM] * (N_Z + 3),
        out_specs=HBM,
        out_shape=jax.ShapeDtypeStruct((SLOTS, PTS, LANES), BF),
        scratch_shapes=[
            pltpu.VMEM((SLOTS, RANK, LANES), BF),
            pltpu.VMEM((SLOTS, PTS, LANES), BF),
            pltpu.SemaphoreType.DMA((SLOTS,)),
        ],
        cost_estimate=pl.CostEstimate(flops=800_000_000, bytes_accessed=7_000_000, transcendentals=0),
        compiler_params=pltpu.CompilerParams(vmem_limit_bytes=14 << 20),
        name="tail",
    )(where, *msgs, half, t_tail, synthesis)


def pipeline(features, analysis, transitions, synthesis):
    col = lax.axis_index("col")
    where = jnp.stack([lax.axis_index("row"), col >> 1, col & 1]).astype(jnp.int32)
    blocks = front(features, analysis, transitions)
    t_mid, t_tail = transitions[4:8], transitions[8:12]
    partner = lax.ppermute(blocks, "col", [(c, c ^ 1) for c in range(N_COL)])
    groups = []
    for b in range(2):
        group = list(messages(b, where, blocks, partner, t_mid))
        for d in FAR_FIRST + (0,):
            if b:
                group[d] = to_target_row(group[d], b, d)
            elif d:
                group[d] = z_swap(group[d], d)
        groups.append(group)
    merged, arrived = [], []
    for b in range(2):
        blocks = host_merge(where, groups[b])
        if b == 0:
            blocks = to_target_row(blocks, 0)
        group = [blocks[0]] * N_Z
        for d in NEAR:
            group[d] = z_swap(blocks[d], d)
        merged.append(blocks)
        arrived.append(group)
    for d in FAR:
        pair = z_swap(jnp.stack([merged[0][d], merged[1][d]]), d)
        arrived[0][d], arrived[1][d] = pair[0], pair[1]
    half = first_half(where, arrived[0], t_tail)
    return tail(where, arrived[1], half, t_tail, synthesis)


def solution(mesh):
    in_specs = (
        P(("row", "col"), None, None),
        P(("row", "col"), None, None),
        P(None, ("row", "col"), None, None),
        P(("row", "col"), None, None),
    )
    out_specs = P(("row", "col"), None, None)
    return jax.shard_map(pipeline, mesh=mesh, in_specs=in_specs, out_specs=out_specs, check_vma=False)
```

time: 124 us -> 125 us (level); the launches traced: 124 us -> 124 us
  starting transfers between devices: 71 us -> 78.1 us
  Pallas kernels: 20.5 us -> 16.1 us
  waiting for transfers between devices: 31.2 us -> 27.2 us
    ppermute x2 -> x9, starting transfers between devices: 4.34 us -> 32 us  [to_target_row(): return lax.ppermute(array, ('row', 'col'), pairs)]
    ppermute x28 -> x19, starting transfers between devices: 66.6 us -> 46 us  [z_swap(): return lax.ppermute(array, 'col', [(c, c ^ 2 * d) for c in range(N_COL)])]
    ppermute x28 -> x19, waiting for transfers between devices: 26 us -> 15.9 us  [z_swap(): return lax.ppermute(array, 'col', [(c, c ^ 2 * d) for c in range(N_COL)])]
    ppermute x2 -> x9, waiting for transfers between devices: 2.29 us -> 10.3 us  [to_target_row(): return lax.ppermute(array, ('row', 'col'), pairs)]
    pallas_call x6 -> x7, Pallas kernels: 20.5 us -> 16.1 us  [the longest x1 5.92 us: front(): pl.pallas_call(front_kernel, in_specs=[HBM] * 3, out_specs=VMEM, out_shap...]
    ppermute x1, waiting for transfers between devices: 2.92 us -> 0.96 us  [pipeline(): partner = lax.ppermute(blocks, 'col', [(c, c ^ 1) for c in range(N_COL)])]
    slice x0 -> x1, local copies, waits for them, and re-layouts: none -> 1.81 us  [pipeline(): t_mid, t_tail = (transitions[4:8], transitions[8:12])]
  transfers between devices with their start and end apart: 31 -> 29, of which waited for: 11 -> 11; matrix products, arithmetic and copies ran while one was open for 0% -> 2% of each run, Pallas kernels for 3% -> 3%
where the time goes in v1:
time: 125 us; the launch traced here: 124 us
  starting transfers between devices  78.1 us (62%)
  waiting for transfers between devices  27.2 us (22%)
  Pallas kernels  16.1 us (13%)
  local copies, waits for them, and re-layouts  1.92 us (2%)
    ppermute x19, starting transfers between devices, z_swap(): return lax.ppermute(array, 'col', [(c, c ^ 2 * d) for c in range(N_COL)])  46 us
    ppermute x9, starting transfers between devices, to_target_row(): return lax.ppermute(array, ('row', 'col'), pairs)  32 us
    ppermute x19, waiting for transfers between devices, z_swap(): return lax.ppermute(array, 'col', [(c, c ^ 2 * d) for c in range(N_COL)])  15.9 us
    ppermute x9, waiting for transfers between devices, to_target_row(): return lax.ppermute(array, ('row', 'col'), pairs)  10.3 us
    pallas_call x1, Pallas kernels, front(): pl.pallas_call(front_kernel, in_specs=[HBM] * 3, out_specs=VMEM, out_shap...  5.92 us
    pallas_call x1, Pallas kernels, tail(): pl.pallas_call(tail_kernel, in_specs=[SMEM] + [VMEM] * (N_Z + 3), out_spe...  4.61 us
    pallas_call x2, Pallas kernels, host_merge(): pl.pallas_call(host_kernel, in_specs=[SMEM] + [VMEM] * N_Z, out_specs=VME...  2.62 us
  transfers between devices with their start and end apart: 29, of which 11 were waited for; matrix products, arithmetic and copies ran while one was open for 2% of the time, Pallas kernels for 3%

profile of v1, /device:TPU:2, one launch (start us, length us, event | category | flops | bytes accessed | tf_op | source)
XLA Modules:
  0.0 123.8 jit_solution(6220296755715843151)
XLA Ops:
  0.0 5.9 %front.1.own_ref = bf16[16,64,512]{2,1,0:T(8,128)(2,1)} custom-call(bf16[16,256,512]{2,1,0:T(8,128)(2,1)} %f_hbm.1, bf16[16,64,256]{2,1,0:T(8,128)(2,1)} %a_hbm.1, bf16[12,16,64,128]{3,2,1,0:T(8,128)(2,1)} %t_hbm.1), custom_call_target="tpu_custom_call" | custom-call | flops 800000000 | bytes 7000000 | tf_op jit(solution)/shard_map/front/pallas_call | solution.py:104
  5.9 0.0 copy-start
  5.9 0.1 collective-permute-start
  6.1 0.1 pad_add_fusion.r_ref
  6.1 1.8 %fusion = (bf16[4,16,64,128]{3,2,1,0:T(8,128)(2,1)S(1)}, bf16[4,16,64,128]{3,2,1,0:T(8,128)(2,1)S(1)}) fusion(bf16[12,16,64,128]{3,2,1,0:T(8,128)(2,1)} %t_hbm.1), kind=kLoop, calls=%fused_computation.19 | loop fusion | bytes 4194304 | tf_op jit(solution)/shard_map/slice | solution.py:252
  7.9 1.0 collective-permute-done.partner_ref
  8.9 0.8 shard_map.48
  9.8 2.0 %collective-permute-start.12 = (bf16[64,896]{1,0:T(8,128)(2,1)S(1)}, bf16[64,896]{1,0:T(8,128)(2,1)S(1)}, u32[]{:S(2)}, u32[]{:S(2)}) collective-permute-start(bf16[64,896]{1,0:T(8,128)(2,1)S(1)} %get-tuple-element.30), channel_id=1, source_target_pairs={{0,2},{1,3},{2,0},{3,1},{4,6},{5,7},{6,4},{7,5},{8,10},{9,11},{10,... | collective-permute-start | bytes 344072 | tf_op jit(solution)/shard_map/ppermute | solution.py:36
  11.8 3.3 %collective-permute-start.13 = (bf16[64,896]{1,0:T(8,128)(2,1)S(1)}, bf16[64,896]{1,0:T(8,128)(2,1)S(1)}, u32[]{:S(2)}, u32[]{:S(2)}) collective-permute-start(bf16[64,896]{1,0:T(8,128)(2,1)S(1)} %get-tuple-element.31), channel_id=1, source_target_pairs={{0,4},{1,5},{2,6},{3,7},{4,0},{5,1},{6,2},{7,3},{8,12},{9,13},{10,... | collective-permute-start | bytes 344072 | tf_op jit(solution)/shard_map/ppermute | solution.py:36
  15.0 0.0 collective-permute-start.14
  15.0 6.4 %collective-permute-start.15 = (bf16[64,896]{1,0:T(8,128)(2,1)S(1)}, bf16[64,896]{1,0:T(8,128)(2,1)S(1)}, u32[]{:S(2)}, u32[]{:S(2)}) collective-permute-start(bf16[64,896]{1,0:T(8,128)(2,1)S(1)} %get-tuple-element.33), channel_id=1, source_target_pairs={{0,8},{1,9},{2,10},{3,11},{4,12},{5,13},{6,14},{7,15},{8,0},{9,1},... | collective-permute-start | bytes 344072 | tf_op jit(solution)/shard_map/ppermute | solution.py:36
  21.4 0.0 collective-permute-start.16
  21.4 0.0 collective-permute-done.12.refs_1_
  21.4 4.6 %collective-permute-start.17 = (bf16[64,896]{1,0:T(8,128)(2,1)S(1)}, bf16[64,896]{1,0:T(8,128)(2,1)S(1)}, u32[]{:S(2)}, u32[]{:S(2)}) collective-permute-start(bf16[64,896]{1,0:T(8,128)(2,1)S(1)} %get-tuple-element.35), channel_id=1, source_target_pairs={{0,12},{1,13},{2,14},{3,15},{4,8},{5,9},{6,10},{7,11},{8,4},{9,5},... | collective-permute-start | bytes 344072 | tf_op jit(solution)/shard_map/ppermute | solution.py:36
  26.0 4.2 %collective-permute-done.13.refs_2_ = bf16[64,896]{1,0:T(8,128)(2,1)S(1)} collective-permute-done((bf16[64,896]{1,0:T(8,128)(2,1)S(1)}, bf16[64,896]{1,0:T(8,128)(2,1)S(1)}, u32[]{:S(2)}, u32[]{:S(2)}) %collective-permute-start.13) | collective-permute-done | bytes 114720 | tf_op jit(solution)/shard_map/ppermute | solution.py:36
  30.2 4.8 %collective-permute-start.18 = (bf16[64,896]{1,0:T(8,128)(2,1)S(1)}, bf16[64,896]{1,0:T(8,128)(2,1)S(1)}, u32[]{:S(2)}, u32[]{:S(2)}) collective-permute-start(bf16[64,896]{1,0:T(8,128)(2,1)S(1)} %get-tuple-element.36), channel_id=1, source_target_pairs={{0,14},{1,15},{2,12},{3,13},{4,10},{5,11},{6,8},{7,9},{8,6},{9,7},... | collective-permute-start | bytes 344072 | tf_op jit(solution)/shard_map/ppermute | solution.py:36
  35.0 0.0 collective-permute-done.14.refs_3_
  35.0 0.0 collective-permute-done.15.refs_4_
  35.0 3.8 %collective-permute-done.16.refs_5_ = bf16[64,896]{1,0:T(8,128)(2,1)S(1)} collective-permute-done((bf16[64,896]{1,0:T(8,128)(2,1)S(1)}, bf16[64,896]{1,0:T(8,128)(2,1)S(1)}, u32[]{:S(2)}, u32[]{:S(2)}) %collective-permute-start.16) | collective-permute-done | bytes 114720 | tf_op jit(solution)/shard_map/ppermute | solution.py:36
  38.9 0.3 collective-permute-done.17.refs_6_
  39.2 3.1 %collective-permute-done.18.refs_7_ = bf16[64,896]{1,0:T(8,128)(2,1)S(1)} collective-permute-done((bf16[64,896]{1,0:T(8,128)(2,1)S(1)}, bf16[64,896]{1,0:T(8,128)(2,1)S(1)}, u32[]{:S(2)}, u32[]{:S(2)}) %collective-permute-start.18) | collective-permute-done | bytes 114720 | tf_op jit(solution)/shard_map/ppermute | solution.py:36
  42.3 1.3 %shard_map.49 = bf16[8,64,512]{2,1,0:T(8,128)(2,1)S(1)} custom-call(s32[3]{0:T(128)S(1)} %pad_add_fusion.r_ref, bf16[64,896]{1,0:T(8,128)(2,1)S(1)} %get-tuple-element.29.refs_0_, bf16[64,896]{1,0:T(8,128)(2,1)S(1)} %collective-permute-done.12.refs_1_, bf16[64,896]{1,0:T(8,128)(2,1)S(1)} %collective-permute-done.13.refs_2_, ...), custom_call_target="tpu_custom_call" | custom-call | flops 200000000 | bytes 1400000 | tf_op jit(solution)/shard_map/pallas_call | solution.py:170
  43.6 0.7 collective-permute-start.19
  44.3 0.9 shard_map.46
  45.2 0.0 copy-start.1
  45.2 5.2 %collective-permute-start.1 = (bf16[64,896]{1,0:T(8,128)(2,1)S(1)}, bf16[64,896]{1,0:T(8,128)(2,1)S(1)}, u32[]{:S(2)}, u32[]{:S(2)}) collective-permute-start(bf16[64,896]{1,0:T(8,128)(2,1)S(1)} %get-tuple-element.21), channel_id=1, source_target_pairs={{0,128},{1,33},{2,146},{3,51},{4,164},{5,5},{6,182},{7,23},{8,200}... | collective-permute-start | bytes 344072 | tf_op jit(solution)/shard_map/ppermute | solution.py:46
  50.4 2.5 %collective-permute-start.2 = (bf16[64,896]{1,0:T(8,128)(2,1)S(1)}, bf16[64,896]{1,0:T(8,128)(2,1)S(1)}, u32[]{:S(2)}, u32[]{:S(2)}) collective-permute-start(bf16[64,896]{1,0:T(8,128)(2,1)S(1)} %get-tuple-element.22), channel_id=1, source_target_pairs={{0,146},{1,51},{2,128},{3,33},{4,182},{5,23},{6,164},{7,5},{8,218}... | collective-permute-start | bytes 344072 | tf_op jit(solution)/shard_map/ppermute | solution.py:46
  52.9 7.8 %collective-permute-start.3 = (bf16[64,896]{1,0:T(8,128)(2,1)S(1)}, bf16[64,896]{1,0:T(8,128)(2,1)S(1)}, u32[]{:S(2)}, u32[]{:S(2)}) collective-permute-start(bf16[64,896]{1,0:T(8,128)(2,1)S(1)} %get-tuple-element.23), channel_id=1, source_target_pairs={{0,164},{1,5},{2,182},{3,23},{4,128},{5,33},{6,146},{7,51},{8,236}... | collective-permute-start | bytes 344072 | tf_op jit(solution)/shard_map/ppermute | solution.py:46
  60.7 4.9 %collective-permute-start.5 = (bf16[64,896]{1,0:T(8,128)(2,1)S(1)}, bf16[64,896]{1,0:T(8,128)(2,1)S(1)}, u32[]{:S(2)}, u32[]{:S(2)}) collective-permute-start(bf16[64,896]{1,0:T(8,128)(2,1)S(1)} %get-tuple-element.25), channel_id=1, source_target_pairs={{0,200},{1,105},{2,218},{3,123},{4,236},{5,77},{6,254},{7,95},{8,1... | collective-permute-start | bytes 344072 | tf_op jit(solution)/shard_map/ppermute | solution.py:46
  65.7 0.0 collective-permute-done.2.refs_1_
  65.7 3.5 %collective-permute-start.6 = (bf16[64,896]{1,0:T(8,128)(2,1)S(1)}, bf16[64,896]{1,0:T(8,128)(2,1)S(1)}, u32[]{:S(2)}, u32[]{:S(2)}) collective-permute-start(bf16[64,896]{1,0:T(8,128)(2,1)S(1)} %get-tuple-element.26), channel_id=1, source_target_pairs={{0,218},{1,123},{2,200},{3,105},{4,254},{5,95},{6,236},{7,77},{8,1... | collective-permute-start | bytes 344072 | tf_op jit(solution)/shard_map/ppermute | solution.py:46
  69.2 0.0 collective-permute-done.3.refs_2_
  69.2 5.7 %collective-permute-start.7 = (bf16[64,896]{1,0:T(8,128)(2,1)S(1)}, bf16[64,896]{1,0:T(8,128)(2,1)S(1)}, u32[]{:S(2)}, u32[]{:S(2)}) collective-permute-start(bf16[64,896]{1,0:T(8,128)(2,1)S(1)} %get-tuple-element.27), channel_id=1, source_target_pairs={{0,236},{1,77},{2,254},{3,95},{4,200},{5,105},{6,218},{7,123},{8,1... | collective-permute-start | bytes 344072 | tf_op jit(solution)/shard_map/ppermute | solution.py:46
  74.8 0.0 collective-permute-done.4.refs_3_
  74.8 1.7 %collective-permute-start.8 = (bf16[64,896]{1,0:T(8,128)(2,1)S(1)}, bf16[64,896]{1,0:T(8,128)(2,1)S(1)}, u32[]{:S(2)}, u32[]{:S(2)}) collective-permute-start(bf16[64,896]{1,0:T(8,128)(2,1)S(1)} %get-tuple-element.28), channel_id=1, source_target_pairs={{0,254},{1,95},{2,236},{3,77},{4,218},{5,123},{6,200},{7,105},{8,1... | collective-permute-start | bytes 344072 | tf_op jit(solution)/shard_map/ppermute | solution.py:46
  76.5 3.4 %collective-permute-done.6.refs_5_ = bf16[64,896]{1,0:T(8,128)(2,1)S(1)} collective-permute-done((bf16[64,896]{1,0:T(8,128)(2,1)S(1)}, bf16[64,896]{1,0:T(8,128)(2,1)S(1)}, u32[]{:S(2)}, u32[]{:S(2)}) %collective-permute-start.6) | collective-permute-done | bytes 114720 | tf_op jit(solution)/shard_map/ppermute | solution.py:46
  79.9 1.7 %collective-permute-done.7.refs_6_ = bf16[64,896]{1,0:T(8,128)(2,1)S(1)} collective-permute-done((bf16[64,896]{1,0:T(8,128)(2,1)S(1)}, bf16[64,896]{1,0:T(8,128)(2,1)S(1)}, u32[]{:S(2)}, u32[]{:S(2)}) %collective-permute-start.7) | collective-permute-done | bytes 114720 | tf_op jit(solution)/shard_map/ppermute | solution.py:46
  81.6 5.2 %collective-permute-done.8.refs_7_ = bf16[64,896]{1,0:T(8,128)(2,1)S(1)} collective-permute-done((bf16[64,896]{1,0:T(8,128)(2,1)S(1)}, bf16[64,896]{1,0:T(8,128)(2,1)S(1)}, u32[]{:S(2)}, u32[]{:S(2)}) %collective-permute-start.8) | collective-permute-done | bytes 114720 | tf_op jit(solution)/shard_map/ppermute | solution.py:46
  86.8 1.3 %shard_map.47 = bf16[8,64,512]{2,1,0:T(8,128)(2,1)S(1)} custom-call(s32[3]{0:T(128)S(1)} %pad_add_fusion.r_ref, bf16[64,896]{1,0:T(8,128)(2,1)S(1)} %collective-permute-done.1.refs_0_, bf16[64,896]{1,0:T(8,128)(2,1)S(1)} %collective-permute-done.2.refs_1_, bf16[64,896]{1,0:T(8,128)(2,1)S(1)} %collective-permute-done.3.refs_2_, ...), custom_call_target="tpu_custom_call" | custom-call | flops 200000000 | bytes 1400000 | tf_op jit(solution)/shard_map/pallas_call | solution.py:170
  88.2 0.0 collective-permute-done.19
  88.2 3.5 %collective-permute-start.20 = (bf16[2,64,512]{2,1,0:T(8,128)(2,1)S(1)}, bf16[2,64,512]{2,1,0:T(8,128)(2,1)S(1)}, u32[]{:S(2)}, u32[]{:S(2)}) collective-permute-start(bf16[2,64,512]{2,1,0:T(8,128)(2,1)S(1)} %pad_maximum_fusion), channel_id=1, source_target_pairs={{0,8},{1,9},{2,10},{3,11},{4,12},{5,13},{6,14},{7,15},{8,0},{9,1},... | collective-permute-start | bytes 393224 | tf_op jit(solution)/shard_map/ppermute | solution.py:36
  91.7 1.0 collective-permute-start.28
  92.8 5.6 %collective-permute-start.27 = (bf16[64,512]{1,0:T(8,128)(2,1)S(1)}, bf16[64,512]{1,0:T(8,128)(2,1)S(1)}, u32[]{:S(2)}, u32[]{:S(2)}) collective-permute-start(bf16[64,512]{1,0:T(8,128)(2,1)S(1)} %get-tuple-element.40), channel_id=1, source_target_pairs={{0,12},{1,13},{2,14},{3,15},{4,8},{5,9},{6,10},{7,11},{8,4},{9,5},... | collective-permute-start | bytes 196616 | tf_op jit(solution)/shard_map/ppermute | solution.py:36
  98.3 1.3 %collective-permute-start.26 = (bf16[64,512]{1,0:T(8,128)(2,1)S(1)}, bf16[64,512]{1,0:T(8,128)(2,1)S(1)}, u32[]{:S(2)}, u32[]{:S(2)}) collective-permute-start(bf16[64,512]{1,0:T(8,128)(2,1)S(1)} %get-tuple-element.41), channel_id=1, source_target_pairs={{0,6},{1,7},{2,4},{3,5},{4,2},{5,3},{6,0},{7,1},{8,14},{9,15},{10,... | collective-permute-start | bytes 196616 | tf_op jit(solution)/shard_map/ppermute | solution.py:36
  99.6 0.0 collective-permute-start.25
  99.6 2.8 %collective-permute-done.28.refs_7_ = bf16[64,512]{1,0:T(8,128)(2,1)S(1)} collective-permute-done((bf16[64,512]{1,0:T(8,128)(2,1)S(1)}, bf16[64,512]{1,0:T(8,128)(2,1)S(1)}, u32[]{:S(2)}, u32[]{:S(2)}) %collective-permute-start.28) | collective-permute-done | bytes 65568 | tf_op jit(solution)/shard_map/ppermute | solution.py:36
  102.4 1.0 collective-permute-start.24
  103.4 0.0 collective-permute-done.20
  103.4 2.0 %collective-permute-start.21 = (bf16[2,64,512]{2,1,0:T(8,128)(2,1)S(1)}, bf16[2,64,512]{2,1,0:T(8,128)(2,1)S(1)}, u32[]{:S(2)}, u32[]{:S(2)}) collective-permute-start(bf16[2,64,512]{2,1,0:T(8,128)(2,1)S(1)} %pad_maximum_fusion.1), channel_id=1, source_target_pairs={{0,10},{1,11},{2,8},{3,9},{4,14},{5,15},{6,12},{7,13},{8,2},{9,3},... | collective-permute-start | bytes 393224 | tf_op jit(solution)/shard_map/ppermute | solution.py:36
  105.3 0.0 collective-permute-done.27.refs_6_
  105.3 1.0 collective-permute-start.23
  106.3 0.0 collective-permute-done.26.refs_3_
  106.3 4.7 %collective-permute-start.22 = (bf16[64,512]{1,0:T(8,128)(2,1)S(1)}, bf16[64,512]{1,0:T(8,128)(2,1)S(1)}, u32[]{:S(2)}, u32[]{:S(2)}) collective-permute-start(bf16[64,512]{1,0:T(8,128)(2,1)S(1)} %get-tuple-element.48), channel_id=1, source_target_pairs={{0,12},{1,13},{2,14},{3,15},{4,8},{5,9},{6,10},{7,11},{8,4},{9,5},... | collective-permute-start | bytes 196616 | tf_op jit(solution)/shard_map/ppermute | solution.py:36
  111.0 0.0 collective-permute-done.25.refs_2_
  111.0 1.3 %collective-permute-start.11 = (bf16[64,512]{1,0:T(8,128)(2,1)S(1)}, bf16[64,512]{1,0:T(8,128)(2,1)S(1)}, u32[]{:S(2)}, u32[]{:S(2)}) collective-permute-start(bf16[64,512]{1,0:T(8,128)(2,1)S(1)} %get-tuple-element.51), channel_id=1, source_target_pairs={{0,6},{1,7},{2,4},{3,5},{4,2},{5,3},{6,0},{7,1},{8,14},{9,15},{10,... | collective-permute-start | bytes 196616 | tf_op jit(solution)/shard_map/ppermute | solution.py:36
  112.3 0.0 collective-permute-done.24.refs_1_
  112.3 0.0 collective-permute-start.10
  112.3 0.0 collective-permute-done.21
  112.3 3.7 %collective-permute-start.9 = (bf16[64,512]{1,0:T(8,128)(2,1)S(1)}, bf16[64,512]{1,0:T(8,128)(2,1)S(1)}, u32[]{:S(2)}, u32[]{:S(2)}) collective-permute-start(bf16[64,512]{1,0:T(8,128)(2,1)S(1)} %get-tuple-element.53), channel_id=1, source_target_pairs={{0,2},{1,3},{2,0},{3,1},{4,6},{5,7},{6,4},{7,5},{8,10},{9,11},{10,... | collective-permute-start | bytes 196616 | tf_op jit(solution)/shard_map/ppermute | solution.py:36
  116.0 1.3 %first_half.1.refs_8_ = bf16[16,64,512]{2,1,0:T(8,128)(2,1)S(1)} custom-call(s32[3]{0:T(128)S(1)} %pad_add_fusion.r_ref, bf16[64,512]{1,0:T(8,128)(2,1)S(1)} %get-tuple-element.44.refs_0_, bf16[64,512]{1,0:T(8,128)(2,1)S(1)} %collective-permute-done.24.refs_1_, bf16[64,512]{1,0:T(8,128)(2,1)S(1)} %collective-permute-done.25.refs_2_, ...), custom_call_target="tpu_custom_call" | custom-call | flops 200000000 | bytes 1400000 | tf_op jit(solution)/shard_map/first_half/pallas_call | solution.py:201
  117.3 0.0 collective-permute-done.22.refs_6_
  117.3 1.1 collective-permute-done.11.refs_3_
  118.4 0.6 collective-permute-done.9.refs_1_
  119.0 4.6 %tail.1 = bf16[16,256,512]{2,1,0:T(8,128)(2,1)} custom-call(s32[3]{0:T(128)S(1)} %pad_add_fusion.r_ref, bf16[64,512]{1,0:T(8,128)(2,1)S(1)} %get-tuple-element.54.refs_0_, bf16[64,512]{1,0:T(8,128)(2,1)S(1)} %collective-permute-done.9.refs_1_, bf16[64,512]{1,0:T(8,128)(2,1)S(1)} %collective-permute-done.10.refs_2_, ...), custom_call_target="tpu_custom_call" | custom-call | flops 800000000 | bytes 7000000 | tf_op jit(solution)/shard_map/tail/pallas_call | solution.py:232
  (13 shorter events, 0.1 us)
Async XLA Ops:
  5.9 3.0 %copy-start = (bf16[16,64,512]{2,1,0:T(8,128)(2,1)S(1)}, bf16[16,64,512]{2,1,0:T(8,128)(2,1)}, u32[]{:S(2)}) copy-start(bf16[16,64,512]{2,1,0:T(8,128)(2,1)} %front.1.own_ref) | copy-start | bytes 3145732
  5.9 3.0 %collective-permute-start = (bf16[16,64,512]{2,1,0:T(8,128)(2,1)}, bf16[16,64,512]{2,1,0:T(8,128)(2,1)S(1)}, u32[]{:S(2)}, u32[]{:S(2)}) collective-permute-start(bf16[16,64,512]{2,1,0:T(8,128)(2,1)} %front.1.own_ref), channel_id=1, source_target_pairs={{0,1},{1,0},{2,3},{3,2},{4,5},{5,4},{6,7},{7,6},{8,9},{9,8},{10,11... | collective-permute-start | bytes 3145736 | tf_op jit(solution)/shard_map/ppermute | solution.py:253
  9.8 11.7 %collective-permute-start.12 = (bf16[64,896]{1,0:T(8,128)(2,1)S(1)}, bf16[64,896]{1,0:T(8,128)(2,1)S(1)}, u32[]{:S(2)}, u32[]{:S(2)}) collective-permute-start(bf16[64,896]{1,0:T(8,128)(2,1)S(1)} %get-tuple-element.30), channel_id=1, source_target_pairs={{0,2},{1,3},{2,0},{3,1},{4,6},{5,7},{6,4},{7,5},{8,10},{9,11},{10,... | collective-permute-start | bytes 344072 | tf_op jit(solution)/shard_map/ppermute | solution.py:36
  11.8 18.5 %collective-permute-start.13 = (bf16[64,896]{1,0:T(8,128)(2,1)S(1)}, bf16[64,896]{1,0:T(8,128)(2,1)S(1)}, u32[]{:S(2)}, u32[]{:S(2)}) collective-permute-start(bf16[64,896]{1,0:T(8,128)(2,1)S(1)} %get-tuple-element.31), channel_id=1, source_target_pairs={{0,4},{1,5},{2,6},{3,7},{4,0},{5,1},{6,2},{7,3},{8,12},{9,13},{10,... | collective-permute-start | bytes 344072 | tf_op jit(solution)/shard_map/ppermute | solution.py:36
  15.0 20.0 %collective-permute-start.14 = (bf16[64,896]{1,0:T(8,128)(2,1)S(1)}, bf16[64,896]{1,0:T(8,128)(2,1)S(1)}, u32[]{:S(2)}, u32[]{:S(2)}) collective-permute-start(bf16[64,896]{1,0:T(8,128)(2,1)S(1)} %get-tuple-element.32), channel_id=1, source_target_pairs={{0,6},{1,7},{2,4},{3,5},{4,2},{5,3},{6,0},{7,1},{8,14},{9,15},{10,... | collective-permute-start | bytes 344072 | tf_op jit(solution)/shard_map/ppermute | solution.py:36
  15.0 20.0 %collective-permute-start.15 = (bf16[64,896]{1,0:T(8,128)(2,1)S(1)}, bf16[64,896]{1,0:T(8,128)(2,1)S(1)}, u32[]{:S(2)}, u32[]{:S(2)}) collective-permute-start(bf16[64,896]{1,0:T(8,128)(2,1)S(1)} %get-tuple-element.33), channel_id=1, source_target_pairs={{0,8},{1,9},{2,10},{3,11},{4,12},{5,13},{6,14},{7,15},{8,0},{9,1},... | collective-permute-start | bytes 344072 | tf_op jit(solution)/shard_map/ppermute | solution.py:36
  21.4 17.4 %collective-permute-start.16 = (bf16[64,896]{1,0:T(8,128)(2,1)S(1)}, bf16[64,896]{1,0:T(8,128)(2,1)S(1)}, u32[]{:S(2)}, u32[]{:S(2)}) collective-permute-start(bf16[64,896]{1,0:T(8,128)(2,1)S(1)} %get-tuple-element.34), channel_id=1, source_target_pairs={{0,10},{1,11},{2,8},{3,9},{4,14},{5,15},{6,12},{7,13},{8,2},{9,3},... | collective-permute-start | bytes 344072 | tf_op jit(solution)/shard_map/ppermute | solution.py:36
  21.4 17.7 %collective-permute-start.17 = (bf16[64,896]{1,0:T(8,128)(2,1)S(1)}, bf16[64,896]{1,0:T(8,128)(2,1)S(1)}, u32[]{:S(2)}, u32[]{:S(2)}) collective-permute-start(bf16[64,896]{1,0:T(8,128)(2,1)S(1)} %get-tuple-element.35), channel_id=1, source_target_pairs={{0,12},{1,13},{2,14},{3,15},{4,8},{5,9},{6,10},{7,11},{8,4},{9,5},... | collective-permute-start | bytes 344072 | tf_op jit(solution)/shard_map/ppermute | solution.py:36
  30.2 12.0 %collective-permute-start.18 = (bf16[64,896]{1,0:T(8,128)(2,1)S(1)}, bf16[64,896]{1,0:T(8,128)(2,1)S(1)}, u32[]{:S(2)}, u32[]{:S(2)}) collective-permute-start(bf16[64,896]{1,0:T(8,128)(2,1)S(1)} %get-tuple-element.36), channel_id=1, source_target_pairs={{0,14},{1,15},{2,12},{3,13},{4,10},{5,11},{6,8},{7,9},{8,6},{9,7},... | collective-permute-start | bytes 344072 | tf_op jit(solution)/shard_map/ppermute | solution.py:36
  43.6 44.6 %collective-permute-start.19 = (bf16[8,64,512]{2,1,0:T(8,128)(2,1)S(1)}, bf16[8,64,512]{2,1,0:T(8,128)(2,1)S(1)}, u32[]{:S(2)}, u32[]{:S(2)}) collective-permute-start(bf16[8,64,512]{2,1,0:T(8,128)(2,1)S(1)} %shard_map.49), channel_id=1, source_target_pairs={{0,0},{1,161},{2,18},{3,179},{4,36},{5,133},{6,54},{7,151},{8,72},... | collective-permute-start | bytes 1572872 | tf_op jit(solution)/shard_map/ppermute | solution.py:46
  45.2 73.8 %copy-start.1 = (bf16[16,64,256]{2,1,0:T(8,128)(2,1)S(1)}, bf16[16,64,256]{2,1,0:T(8,128)(2,1)}, u32[]{:S(2)}) copy-start(bf16[16,64,256]{2,1,0:T(8,128)(2,1)} %refs_10_.1) | copy-start | bytes 1572868
  45.2 15.6 %collective-permute-start.1 = (bf16[64,896]{1,0:T(8,128)(2,1)S(1)}, bf16[64,896]{1,0:T(8,128)(2,1)S(1)}, u32[]{:S(2)}, u32[]{:S(2)}) collective-permute-start(bf16[64,896]{1,0:T(8,128)(2,1)S(1)} %get-tuple-element.21), channel_id=1, source_target_pairs={{0,128},{1,33},{2,146},{3,51},{4,164},{5,5},{6,182},{7,23},{8,200}... | collective-permute-start | bytes 344072 | tf_op jit(solution)/shard_map/ppermute | solution.py:46
  50.4 15.3 %collective-permute-start.2 = (bf16[64,896]{1,0:T(8,128)(2,1)S(1)}, bf16[64,896]{1,0:T(8,128)(2,1)S(1)}, u32[]{:S(2)}, u32[]{:S(2)}) collective-permute-start(bf16[64,896]{1,0:T(8,128)(2,1)S(1)} %get-tuple-element.22), channel_id=1, source_target_pairs={{0,146},{1,51},{2,128},{3,33},{4,182},{5,23},{6,164},{7,5},{8,218}... | collective-permute-start | bytes 344072 | tf_op jit(solution)/shard_map/ppermute | solution.py:46
  52.9 16.3 %collective-permute-start.3 = (bf16[64,896]{1,0:T(8,128)(2,1)S(1)}, bf16[64,896]{1,0:T(8,128)(2,1)S(1)}, u32[]{:S(2)}, u32[]{:S(2)}) collective-permute-start(bf16[64,896]{1,0:T(8,128)(2,1)S(1)} %get-tuple-element.23), channel_id=1, source_target_pairs={{0,164},{1,5},{2,182},{3,23},{4,128},{5,33},{6,146},{7,51},{8,236}... | collective-permute-start | bytes 344072 | tf_op jit(solution)/shard_map/ppermute | solution.py:46
  60.7 14.1 %collective-permute-start.4 = (bf16[64,896]{1,0:T(8,128)(2,1)S(1)}, bf16[64,896]{1,0:T(8,128)(2,1)S(1)}, u32[]{:S(2)}, u32[]{:S(2)}) collective-permute-start(bf16[64,896]{1,0:T(8,128)(2,1)S(1)} %get-tuple-element.24), channel_id=1, source_target_pairs={{0,182},{1,23},{2,164},{3,5},{4,146},{5,51},{6,128},{7,33},{8,254}... | collective-permute-start | bytes 344072 | tf_op jit(solution)/shard_map/ppermute | solution.py:46
  60.7 15.8 %collective-permute-start.5 = (bf16[64,896]{1,0:T(8,128)(2,1)S(1)}, bf16[64,896]{1,0:T(8,128)(2,1)S(1)}, u32[]{:S(2)}, u32[]{:S(2)}) collective-permute-start(bf16[64,896]{1,0:T(8,128)(2,1)S(1)} %get-tuple-element.25), channel_id=1, source_target_pairs={{0,200},{1,105},{2,218},{3,123},{4,236},{5,77},{6,254},{7,95},{8,1... | collective-permute-start | bytes 344072 | tf_op jit(solution)/shard_map/ppermute | solution.py:46
  65.7 14.2 %collective-permute-start.6 = (bf16[64,896]{1,0:T(8,128)(2,1)S(1)}, bf16[64,896]{1,0:T(8,128)(2,1)S(1)}, u32[]{:S(2)}, u32[]{:S(2)}) collective-permute-start(bf16[64,896]{1,0:T(8,128)(2,1)S(1)} %get-tuple-element.26), channel_id=1, source_target_pairs={{0,218},{1,123},{2,200},{3,105},{4,254},{5,95},{6,236},{7,77},{8,1... | collective-permute-start | bytes 344072 | tf_op jit(solution)/shard_map/ppermute | solution.py:46
  69.2 12.4 %collective-permute-start.7 = (bf16[64,896]{1,0:T(8,128)(2,1)S(1)}, bf16[64,896]{1,0:T(8,128)(2,1)S(1)}, u32[]{:S(2)}, u32[]{:S(2)}) collective-permute-start(bf16[64,896]{1,0:T(8,128)(2,1)S(1)} %get-tuple-element.27), channel_id=1, source_target_pairs={{0,236},{1,77},{2,254},{3,95},{4,200},{5,105},{6,218},{7,123},{8,1... | collective-permute-start | bytes 344072 | tf_op jit(solution)/shard_map/ppermute | solution.py:46
  74.8 12.0 %collective-permute-start.8 = (bf16[64,896]{1,0:T(8,128)(2,1)S(1)}, bf16[64,896]{1,0:T(8,128)(2,1)S(1)}, u32[]{:S(2)}, u32[]{:S(2)}) collective-permute-start(bf16[64,896]{1,0:T(8,128)(2,1)S(1)} %get-tuple-element.28), channel_id=1, source_target_pairs={{0,254},{1,95},{2,236},{3,77},{4,218},{5,123},{6,200},{7,105},{8,1... | collective-permute-start | bytes 344072 | tf_op jit(solution)/shard_map/ppermute | solution.py:46
  88.2 15.1 %collective-permute-start.20 = (bf16[2,64,512]{2,1,0:T(8,128)(2,1)S(1)}, bf16[2,64,512]{2,1,0:T(8,128)(2,1)S(1)}, u32[]{:S(2)}, u32[]{:S(2)}) collective-permute-start(bf16[2,64,512]{2,1,0:T(8,128)(2,1)S(1)} %pad_maximum_fusion), channel_id=1, source_target_pairs={{0,8},{1,9},{2,10},{3,11},{4,12},{5,13},{6,14},{7,15},{8,0},{9,1},... | collective-permute-start | bytes 393224 | tf_op jit(solution)/shard_map/ppermute | solution.py:36
  91.7 10.6 %collective-permute-start.28 = (bf16[64,512]{1,0:T(8,128)(2,1)S(1)}, bf16[64,512]{1,0:T(8,128)(2,1)S(1)}, u32[]{:S(2)}, u32[]{:S(2)}) collective-permute-start(bf16[64,512]{1,0:T(8,128)(2,1)S(1)} %get-tuple-element.39), channel_id=1, source_target_pairs={{0,14},{1,15},{2,12},{3,13},{4,10},{5,11},{6,8},{7,9},{8,6},{9,7},... | collective-permute-start | bytes 196616 | tf_op jit(solution)/shard_map/ppermute | solution.py:36
  92.8 12.6 %collective-permute-start.27 = (bf16[64,512]{1,0:T(8,128)(2,1)S(1)}, bf16[64,512]{1,0:T(8,128)(2,1)S(1)}, u32[]{:S(2)}, u32[]{:S(2)}) collective-permute-start(bf16[64,512]{1,0:T(8,128)(2,1)S(1)} %get-tuple-element.40), channel_id=1, source_target_pairs={{0,12},{1,13},{2,14},{3,15},{4,8},{5,9},{6,10},{7,11},{8,4},{9,5},... | collective-permute-start | bytes 196616 | tf_op jit(solution)/shard_map/ppermute | solution.py:36
  98.3 8.0 %collective-permute-start.26 = (bf16[64,512]{1,0:T(8,128)(2,1)S(1)}, bf16[64,512]{1,0:T(8,128)(2,1)S(1)}, u32[]{:S(2)}, u32[]{:S(2)}) collective-permute-start(bf16[64,512]{1,0:T(8,128)(2,1)S(1)} %get-tuple-element.41), channel_id=1, source_target_pairs={{0,6},{1,7},{2,4},{3,5},{4,2},{5,3},{6,0},{7,1},{8,14},{9,15},{10,... | collective-permute-start | bytes 196616 | tf_op jit(solution)/shard_map/ppermute | solution.py:36
  99.6 11.4 %collective-permute-start.25 = (bf16[64,512]{1,0:T(8,128)(2,1)S(1)}, bf16[64,512]{1,0:T(8,128)(2,1)S(1)}, u32[]{:S(2)}, u32[]{:S(2)}) collective-permute-start(bf16[64,512]{1,0:T(8,128)(2,1)S(1)} %get-tuple-element.42), channel_id=1, source_target_pairs={{0,4},{1,5},{2,6},{3,7},{4,0},{5,1},{6,2},{7,3},{8,12},{9,13},{10,... | collective-permute-start | bytes 196616 | tf_op jit(solution)/shard_map/ppermute | solution.py:36
  102.4 10.0 %collective-permute-start.24 = (bf16[64,512]{1,0:T(8,128)(2,1)S(1)}, bf16[64,512]{1,0:T(8,128)(2,1)S(1)}, u32[]{:S(2)}, u32[]{:S(2)}) collective-permute-start(bf16[64,512]{1,0:T(8,128)(2,1)S(1)} %get-tuple-element.43), channel_id=1, source_target_pairs={{0,2},{1,3},{2,0},{3,1},{4,6},{5,7},{6,4},{7,5},{8,10},{9,11},{10,... | collective-permute-start | bytes 196616 | tf_op jit(solution)/shard_map/ppermute | solution.py:36
  103.4 9.0 %collective-permute-start.21 = (bf16[2,64,512]{2,1,0:T(8,128)(2,1)S(1)}, bf16[2,64,512]{2,1,0:T(8,128)(2,1)S(1)}, u32[]{:S(2)}, u32[]{:S(2)}) collective-permute-start(bf16[2,64,512]{2,1,0:T(8,128)(2,1)S(1)} %pad_maximum_fusion.1), channel_id=1, source_target_pairs={{0,10},{1,11},{2,8},{3,9},{4,14},{5,15},{6,12},{7,13},{8,2},{9,3},... | collective-permute-start | bytes 393224 | tf_op jit(solution)/shard_map/ppermute | solution.py:36
  105.3 12.0 %collective-permute-start.23 = (bf16[64,512]{1,0:T(8,128)(2,1)S(1)}, bf16[64,512]{1,0:T(8,128)(2,1)S(1)}, u32[]{:S(2)}, u32[]{:S(2)}) collective-permute-start(bf16[64,512]{1,0:T(8,128)(2,1)S(1)} %get-tuple-element.47), channel_id=1, source_target_pairs={{0,14},{1,15},{2,12},{3,13},{4,10},{5,11},{6,8},{7,9},{8,6},{9,7},... | collective-permute-start | bytes 196616 | tf_op jit(solution)/shard_map/ppermute | solution.py:36
  106.3 11.0 %collective-permute-start.22 = (bf16[64,512]{1,0:T(8,128)(2,1)S(1)}, bf16[64,512]{1,0:T(8,128)(2,1)S(1)}, u32[]{:S(2)}, u32[]{:S(2)}) collective-permute-start(bf16[64,512]{1,0:T(8,128)(2,1)S(1)} %get-tuple-element.48), channel_id=1, source_target_pairs={{0,12},{1,13},{2,14},{3,15},{4,8},{5,9},{6,10},{7,11},{8,4},{9,5},... | collective-permute-start | bytes 196616 | tf_op jit(solution)/shard_map/ppermute | solution.py:36
  111.0 7.4 %collective-permute-start.11 = (bf16[64,512]{1,0:T(8,128)(2,1)S(1)}, bf16[64,512]{1,0:T(8,128)(2,1)S(1)}, u32[]{:S(2)}, u32[]{:S(2)}) collective-permute-start(bf16[64,512]{1,0:T(8,128)(2,1)S(1)} %get-tuple-element.51), channel_id=1, source_target_pairs={{0,6},{1,7},{2,4},{3,5},{4,2},{5,3},{6,0},{7,1},{8,14},{9,15},{10,... | collective-permute-start | bytes 196616 | tf_op jit(solution)/shard_map/ppermute | solution.py:36
  112.3 6.1 %collective-permute-start.10 = (bf16[64,512]{1,0:T(8,128)(2,1)S(1)}, bf16[64,512]{1,0:T(8,128)(2,1)S(1)}, u32[]{:S(2)}, u32[]{:S(2)}) collective-permute-start(bf16[64,512]{1,0:T(8,128)(2,1)S(1)} %get-tuple-element.52), channel_id=1, source_target_pairs={{0,4},{1,5},{2,6},{3,7},{4,0},{5,1},{6,2},{7,3},{8,12},{9,13},{10,... | collective-permute-start | bytes 196616 | tf_op jit(solution)/shard_map/ppermute | solution.py:36
  112.3 6.6 %collective-permute-start.9 = (bf16[64,512]{1,0:T(8,128)(2,1)S(1)}, bf16[64,512]{1,0:T(8,128)(2,1)S(1)}, u32[]{:S(2)}, u32[]{:S(2)}) collective-permute-start(bf16[64,512]{1,0:T(8,128)(2,1)S(1)} %get-tuple-element.53), channel_id=1, source_target_pairs={{0,2},{1,3},{2,0},{3,1},{4,6},{5,7},{6,4},{7,5},{8,10},{9,11},{10,... | collective-permute-start | bytes 196616 | tf_op jit(solution)/shard_map/ppermute | solution.py:36

commit v2 on v1

--- a/solution.py
+++ b/solution.py
@@ -23,13 +23,15 @@
 VMEM = pl.BlockSpec(memory_space=pltpu.VMEM)
 SMEM = pl.BlockSpec(memory_space=pltpu.SMEM)
 HBM = pl.BlockSpec(memory_space=pltpu.HBM)
+TOP = (8, 0)
+TWIST = 6
 FAR_FIRST = (4, 5, 3, 7, 6, 2, 1)
-FAR = (4, 5)
-NEAR = (3, 7, 6, 2, 1)
+FAR = (4, 5, 3, 7, 6, 2, 1)
+NEAR = ()
 
 
 def base_of(r_ref):
-    return r_ref[0] ^ r_ref[1] ^ (10 * r_ref[2])
+    return r_ref[0] ^ r_ref[1] ^ (TWIST * r_ref[2])
 
 
 def z_swap(array, d):
@@ -41,7 +43,7 @@
     for r in range(N_ROW):
         for c in range(N_COL):
             to_col = c ^ (2 * d)
-            to_row = r ^ (to_col >> 1) ^ (8 * b) ^ (10 * (c & 1))
+            to_row = r ^ (to_col >> 1) ^ TOP[b] ^ (TWIST * (c & 1))
             pairs.append((r * N_COL + c, to_row * N_COL + to_col))
     return lax.ppermute(array, ("row", "col"), pairs)
 
@@ -121,17 +123,20 @@
 
 
 def message_kernel(b, r_ref, own_ref, partner_ref, t_ref, *outs):
-    base = base_of(r_ref)
+    base, z = base_of(r_ref), r_ref[1]
     for core in range(2):
 
         @pl.when(r_ref[2] == core)
         def _(low=partner_ref if core else own_ref, high=own_ref if core else partner_ref):
             for d in range(N_Z):
-                s = base ^ (d | 8 * b)
+                s = base ^ (d | TOP[b])
                 joined = jnp.concatenate([low[s], high[s]], axis=0)
                 outs[d][:, :LANES] = dot(t_ref[0, s], joined).astype(BF)
                 for e in range(Z_LEVELS):
-                    outs[d][:, LANES + e * PAIR : LANES + (e + 1) * PAIR] = t_ref[1 + e, s]
+                    t = t_ref[1 + e, s]
+                    flipped = jnp.concatenate([t[:, RANK:], t[:, :RANK]], axis=1)
+                    host_bit = ((z ^ d) >> e) & 1
+                    outs[d][:, LANES + e * PAIR : LANES + (e + 1) * PAIR] = jnp.where(host_bit == 0, t, flipped)
 
 
 def messages(b, where, own, partner, t_mid):
@@ -145,10 +150,8 @@
     )(where, own, partner, t_mid)
 
 
-def host_kernel(r_ref, *refs):
-    msgs, (out, c_ref) = refs[:N_Z], refs[N_Z:]
-    for d in range(N_Z):
-        c_ref[r_ref[1] ^ d] = msgs[d][...]
+def host_kernel(*refs):
+    msgs, out = refs[:N_Z], refs[N_Z]
     for e in range(Z_LEVELS):
         stride = 1 << e
         lanes = slice(LANES + e * PAIR, LANES + (e + 1) * PAIR)
@@ -156,33 +159,29 @@
             if lo & stride:
                 continue
             hi = lo + stride
-            joined = jnp.concatenate([c_ref[lo, :, :LANES], c_ref[hi, :, :LANES]], axis=0)
-            weights = jnp.concatenate([c_ref[lo, :, lanes], c_ref[hi, :, lanes]], axis=0)
-            merged = dot(weights, joined).astype(BF)
-            for z, block in ((lo, merged[:RANK]), (hi, merged[RANK:])):
-                if e < Z_LEVELS - 1:
-                    c_ref[z, :, :LANES] = block
-                else:
-                    out[r_ref[1] ^ z] = block
-
-
-def host_merge(where, msgs):
+            joined = [out[d] if e else msgs[d][:, :LANES] for d in (lo, hi)]
+            weights = [msgs[d][:, lanes] for d in (lo, hi)]
+            merged = dot(jnp.concatenate(weights, axis=0), jnp.concatenate(joined, axis=0)).astype(BF)
+            out[lo] = merged[:RANK]
+            out[hi] = merged[RANK:]
+
+
+def host_merge(msgs):
     return pl.pallas_call(
         host_kernel,
-        in_specs=[SMEM] + [VMEM] * N_Z,
+        in_specs=[VMEM] * N_Z,
         out_specs=VMEM,
         out_shape=jax.ShapeDtypeStruct((N_Z, RANK, LANES), BF),
-        scratch_shapes=[pltpu.VMEM((N_Z, RANK, MSG), BF)],
         cost_estimate=pl.CostEstimate(flops=200_000_000, bytes_accessed=1_400_000, transcendentals=0),
         compiler_params=pltpu.CompilerParams(vmem_limit_bytes=6 << 20),
-    )(where, *msgs)
+    )(*msgs)
 
 
 def half_levels(b, r_ref, msgs, t_ref, c_ref):
     base = base_of(r_ref)
-    top = (base & 8) ^ (8 * b)
+    top = (base & 8) ^ TOP[b]
     for d in range(N_Z):
-        c_ref[base ^ (d | 8 * b)] = msgs[d][...]
+        c_ref[base ^ (d | TOP[b])] = msgs[d][...]
     for e in range(3):
         stride = 1 << e
         for j in range(N_Z):
@@ -213,8 +212,9 @@
     msgs, (half_ref, t_ref, s_ref, o_hbm, c_ref, o_buf, sem) = refs[:N_Z], refs[N_Z:]
     base = base_of(r_ref)
     half_levels(1, r_ref, msgs, t_ref, c_ref)
+    first = (base & 8) ^ TOP[0]
     for j in range(N_Z):
-        c_ref[(base & 8) + j] = half_ref[(base & 8) + j]
+        c_ref[first + j] = half_ref[first + j]
     copies = []
     for j in range(N_Z):
         merge_pair(c_ref, j, j + 8, t_ref[3, j], t_ref[3, j + 8])
@@ -262,7 +262,7 @@
         groups.append(group)
     merged, arrived = [], []
     for b in range(2):
-        blocks = host_merge(where, groups[b])
+        blocks = host_merge(groups[b])
         if b == 0:
             blocks = to_target_row(blocks, 0)
         group = [blocks[0]] * N_Z

time: 125 us -> 124 us (level)
  waiting for transfers between devices: 27.2 us -> 38.8 us
  starting transfers between devices: 78.1 us -> 67.7 us
    ppermute x19 -> x14, waiting for transfers between devices: 15.9 us -> 26.9 us  [z_swap(): return lax.ppermute(array, 'col', [(c, c ^ 2 * d) for c in range(N_COL)])]
    ppermute x19 -> x14, starting transfers between devices: 46 us -> 37.4 us  [z_swap(): return lax.ppermute(array, 'col', [(c, c ^ 2 * d) for c in range(N_COL)])]
    ppermute x9, starting transfers between devices: 32 us -> 30.2 us  [to_target_row(): return lax.ppermute(array, ('row', 'col'), pairs)]
    pallas_call x2, Pallas kernels: 2.62 us -> 1.37 us  [host_merge(): pl.pallas_call(host_kernel, in_specs=[VMEM] * N_Z, out_specs=VMEM, out_sh...]
  transfers between devices with their start and end apart: 29 -> 24, of which waited for: 11 -> 11; matrix products, arithmetic and copies ran while one was open for 2% -> 2% of each run, Pallas kernels for 3% -> 1%
where the time goes in v2:
time: 124 us
  starting transfers between devices  67.7 us (55%)
  waiting for transfers between devices  38.8 us (31%)
  Pallas kernels  14.9 us (12%)
  local copies, waits for them, and re-layouts  1.97 us (2%)
    ppermute x14, starting transfers between devices, z_swap(): return lax.ppermute(array, 'col', [(c, c ^ 2 * d) for c in range(N_COL)])  37.4 us
    ppermute x9, starting transfers between devices, to_target_row(): return lax.ppermute(array, ('row', 'col'), pairs)  30.2 us
    ppermute x14, waiting for transfers between devices, z_swap(): return lax.ppermute(array, 'col', [(c, c ^ 2 * d) for c in range(N_COL)])  26.9 us
    ppermute x9, waiting for transfers between devices, to_target_row(): return lax.ppermute(array, ('row', 'col'), pairs)  10.9 us
    pallas_call x1, Pallas kernels, front(): pl.pallas_call(front_kernel, in_specs=[HBM] * 3, out_specs=VMEM, out_shap...  5.92 us
    pallas_call x1, Pallas kernels, tail(): pl.pallas_call(tail_kernel, in_specs=[SMEM] + [VMEM] * (N_Z + 3), out_spe...  4.62 us
  transfers between devices with their start and end apart: 24, of which 11 were waited for; matrix products, arithmetic and copies ran while one was open for 2% of the time, Pallas kernels for 1%

profile of v2, /device:TPU:2, one launch (start us, length us, event | category | flops | bytes accessed | tf_op | source)
XLA Modules:
  0.0 123.9 jit_solution(13093726411695263637)
XLA Ops:
  0.0 5.9 %front.1.own_ref = bf16[16,64,512]{2,1,0:T(8,128)(2,1)} custom-call(bf16[16,256,512]{2,1,0:T(8,128)(2,1)} %f_hbm.1, bf16[16,64,256]{2,1,0:T(8,128)(2,1)} %a_hbm.1, bf16[12,16,64,128]{3,2,1,0:T(8,128)(2,1)} %t_hbm.1), custom_call_target="tpu_custom_call" | custom-call | flops 800000000 | bytes 7000000 | tf_op jit(solution)/shard_map/front/pallas_call | solution.py:106
  5.9 0.0 copy-start
  5.9 0.1 collective-permute-start
  6.1 0.1 pad_add_fusion.r_ref
  6.1 1.8 %fusion = (bf16[4,16,64,128]{3,2,1,0:T(8,128)(2,1)S(1)}, bf16[4,16,64,128]{3,2,1,0:T(8,128)(2,1)S(1)}) fusion(bf16[12,16,64,128]{3,2,1,0:T(8,128)(2,1)} %t_hbm.1), kind=kLoop, calls=%fused_computation.24 | loop fusion | bytes 4194304 | tf_op jit(solution)/shard_map/slice | solution.py:252
  7.9 1.0 collective-permute-done.partner_ref
  8.9 0.0 copy-done
  8.9 0.8 shard_map.48
  9.8 2.0 %collective-permute-start.9 = (bf16[64,896]{1,0:T(8,128)(2,1)S(1)}, bf16[64,896]{1,0:T(8,128)(2,1)S(1)}, u32[]{:S(2)}, u32[]{:S(2)}) collective-permute-start(bf16[64,896]{1,0:T(8,128)(2,1)S(1)} %get-tuple-element.30), channel_id=1, source_target_pairs={{0,2},{1,3},{2,0},{3,1},{4,6},{5,7},{6,4},{7,5},{8,10},{9,11},{10,... | collective-permute-start | bytes 344072 | tf_op jit(solution)/shard_map/ppermute | solution.py:38
  11.8 3.3 %collective-permute-start.10 = (bf16[64,896]{1,0:T(8,128)(2,1)S(1)}, bf16[64,896]{1,0:T(8,128)(2,1)S(1)}, u32[]{:S(2)}, u32[]{:S(2)}) collective-permute-start(bf16[64,896]{1,0:T(8,128)(2,1)S(1)} %get-tuple-element.31), channel_id=1, source_target_pairs={{0,4},{1,5},{2,6},{3,7},{4,0},{5,1},{6,2},{7,3},{8,12},{9,13},{10,... | collective-permute-start | bytes 344072 | tf_op jit(solution)/shard_map/ppermute | solution.py:38
  15.0 0.0 collective-permute-start.11
  15.0 6.4 %collective-permute-start.12 = (bf16[64,896]{1,0:T(8,128)(2,1)S(1)}, bf16[64,896]{1,0:T(8,128)(2,1)S(1)}, u32[]{:S(2)}, u32[]{:S(2)}) collective-permute-start(bf16[64,896]{1,0:T(8,128)(2,1)S(1)} %get-tuple-element.33), channel_id=1, source_target_pairs={{0,8},{1,9},{2,10},{3,11},{4,12},{5,13},{6,14},{7,15},{8,0},{9,1},... | collective-permute-start | bytes 344072 | tf_op jit(solution)/shard_map/ppermute | solution.py:38
  21.4 0.0 collective-permute-start.13
  21.4 0.0 collective-permute-done.9.refs_1_
  21.4 4.6 %collective-permute-start.14 = (bf16[64,896]{1,0:T(8,128)(2,1)S(1)}, bf16[64,896]{1,0:T(8,128)(2,1)S(1)}, u32[]{:S(2)}, u32[]{:S(2)}) collective-permute-start(bf16[64,896]{1,0:T(8,128)(2,1)S(1)} %get-tuple-element.35), channel_id=1, source_target_pairs={{0,12},{1,13},{2,14},{3,15},{4,8},{5,9},{6,10},{7,11},{8,4},{9,5},... | collective-permute-start | bytes 344072 | tf_op jit(solution)/shard_map/ppermute | solution.py:38
  26.0 4.2 %collective-permute-done.10.refs_2_ = bf16[64,896]{1,0:T(8,128)(2,1)S(1)} collective-permute-done((bf16[64,896]{1,0:T(8,128)(2,1)S(1)}, bf16[64,896]{1,0:T(8,128)(2,1)S(1)}, u32[]{:S(2)}, u32[]{:S(2)}) %collective-permute-start.10) | collective-permute-done | bytes 114720 | tf_op jit(solution)/shard_map/ppermute | solution.py:38
  30.3 4.8 %collective-permute-start.15 = (bf16[64,896]{1,0:T(8,128)(2,1)S(1)}, bf16[64,896]{1,0:T(8,128)(2,1)S(1)}, u32[]{:S(2)}, u32[]{:S(2)}) collective-permute-start(bf16[64,896]{1,0:T(8,128)(2,1)S(1)} %get-tuple-element.36), channel_id=1, source_target_pairs={{0,14},{1,15},{2,12},{3,13},{4,10},{5,11},{6,8},{7,9},{8,6},{9,7},... | collective-permute-start | bytes 344072 | tf_op jit(solution)/shard_map/ppermute | solution.py:38
  35.1 0.0 collective-permute-done.11.refs_3_
  35.1 0.0 collective-permute-done.12.refs_4_
  35.1 3.8 %collective-permute-done.13.refs_5_ = bf16[64,896]{1,0:T(8,128)(2,1)S(1)} collective-permute-done((bf16[64,896]{1,0:T(8,128)(2,1)S(1)}, bf16[64,896]{1,0:T(8,128)(2,1)S(1)}, u32[]{:S(2)}, u32[]{:S(2)}) %collective-permute-start.13) | collective-permute-done | bytes 114720 | tf_op jit(solution)/shard_map/ppermute | solution.py:38
  38.9 0.3 collective-permute-done.14.refs_6_
  39.2 3.1 %collective-permute-done.15.refs_7_ = bf16[64,896]{1,0:T(8,128)(2,1)S(1)} collective-permute-done((bf16[64,896]{1,0:T(8,128)(2,1)S(1)}, bf16[64,896]{1,0:T(8,128)(2,1)S(1)}, u32[]{:S(2)}, u32[]{:S(2)}) %collective-permute-start.15) | collective-permute-done | bytes 114720 | tf_op jit(solution)/shard_map/ppermute | solution.py:38
  42.3 0.7 shard_map.49
  43.0 3.3 %collective-permute-start.16 = (bf16[8,64,512]{2,1,0:T(8,128)(2,1)S(1)}, bf16[8,64,512]{2,1,0:T(8,128)(2,1)S(1)}, u32[]{:S(2)}, u32[]{:S(2)}) collective-permute-start(bf16[8,64,512]{2,1,0:T(8,128)(2,1)S(1)} %shard_map.49), channel_id=1, source_target_pairs={{0,128},{1,225},{2,146},{3,243},{4,164},{5,197},{6,182},{7,215},{8... | collective-permute-start | bytes 1572872 | tf_op jit(solution)/shard_map/ppermute | solution.py:48
  46.3 0.9 shard_map.46
  47.1 0.7 collective-permute-start.1
  47.8 2.8 %collective-permute-start.2 = (bf16[64,896]{1,0:T(8,128)(2,1)S(1)}, bf16[64,896]{1,0:T(8,128)(2,1)S(1)}, u32[]{:S(2)}, u32[]{:S(2)}) collective-permute-start(bf16[64,896]{1,0:T(8,128)(2,1)S(1)} %get-tuple-element.22), channel_id=1, source_target_pairs={{0,18},{1,115},{2,0},{3,97},{4,54},{5,87},{6,36},{7,69},{8,90},{9,... | collective-permute-start | bytes 344072 | tf_op jit(solution)/shard_map/ppermute | solution.py:48
  50.6 5.2 %collective-permute-start.3 = (bf16[64,896]{1,0:T(8,128)(2,1)S(1)}, bf16[64,896]{1,0:T(8,128)(2,1)S(1)}, u32[]{:S(2)}, u32[]{:S(2)}) collective-permute-start(bf16[64,896]{1,0:T(8,128)(2,1)S(1)} %get-tuple-element.23), channel_id=1, source_target_pairs={{0,36},{1,69},{2,54},{3,87},{4,0},{5,97},{6,18},{7,115},{8,108},{9... | collective-permute-start | bytes 344072 | tf_op jit(solution)/shard_map/ppermute | solution.py:48
  55.7 0.0 collective-permute-start.4
  55.7 0.0 collective-permute-done.1.refs_0_
  55.7 5.4 %collective-permute-start.5 = (bf16[64,896]{1,0:T(8,128)(2,1)S(1)}, bf16[64,896]{1,0:T(8,128)(2,1)S(1)}, u32[]{:S(2)}, u32[]{:S(2)}) collective-permute-start(bf16[64,896]{1,0:T(8,128)(2,1)S(1)} %get-tuple-element.25), channel_id=1, source_target_pairs={{0,72},{1,41},{2,90},{3,59},{4,108},{5,13},{6,126},{7,31},{8,0},{9... | collective-permute-start | bytes 344072 | tf_op jit(solution)/shard_map/ppermute | solution.py:48
  61.2 0.0 collective-permute-done.2.refs_1_
  61.2 3.8 %collective-permute-start.6 = (bf16[64,896]{1,0:T(8,128)(2,1)S(1)}, bf16[64,896]{1,0:T(8,128)(2,1)S(1)}, u32[]{:S(2)}, u32[]{:S(2)}) collective-permute-start(bf16[64,896]{1,0:T(8,128)(2,1)S(1)} %get-tuple-element.26), channel_id=1, source_target_pairs={{0,90},{1,59},{2,72},{3,41},{4,126},{5,31},{6,108},{7,13},{8,18},{... | collective-permute-start | bytes 344072 | tf_op jit(solution)/shard_map/ppermute | solution.py:48
  65.0 0.0 collective-permute-done.3.refs_2_
  65.0 7.4 %collective-permute-start.7 = (bf16[64,896]{1,0:T(8,128)(2,1)S(1)}, bf16[64,896]{1,0:T(8,128)(2,1)S(1)}, u32[]{:S(2)}, u32[]{:S(2)}) collective-permute-start(bf16[64,896]{1,0:T(8,128)(2,1)S(1)} %get-tuple-element.27), channel_id=1, source_target_pairs={{0,108},{1,13},{2,126},{3,31},{4,72},{5,41},{6,90},{7,59},{8,36},{... | collective-permute-start | bytes 344072 | tf_op jit(solution)/shard_map/ppermute | solution.py:48
  72.4 0.0 collective-permute-done.4.refs_3_
  72.4 1.6 %collective-permute-start.8 = (bf16[64,896]{1,0:T(8,128)(2,1)S(1)}, bf16[64,896]{1,0:T(8,128)(2,1)S(1)}, u32[]{:S(2)}, u32[]{:S(2)}) collective-permute-start(bf16[64,896]{1,0:T(8,128)(2,1)S(1)} %get-tuple-element.28), channel_id=1, source_target_pairs={{0,126},{1,31},{2,108},{3,13},{4,90},{5,59},{6,72},{7,41},{8,54},{... | collective-permute-start | bytes 344072 | tf_op jit(solution)/shard_map/ppermute | solution.py:48
  74.1 0.0 collective-permute-done.5.refs_4_
  74.1 1.4 %collective-permute-done.6.refs_5_ = bf16[64,896]{1,0:T(8,128)(2,1)S(1)} collective-permute-done((bf16[64,896]{1,0:T(8,128)(2,1)S(1)}, bf16[64,896]{1,0:T(8,128)(2,1)S(1)}, u32[]{:S(2)}, u32[]{:S(2)}) %collective-permute-start.6) | collective-permute-done | bytes 114720 | tf_op jit(solution)/shard_map/ppermute | solution.py:48
  75.5 3.2 %collective-permute-done.7.refs_6_ = bf16[64,896]{1,0:T(8,128)(2,1)S(1)} collective-permute-done((bf16[64,896]{1,0:T(8,128)(2,1)S(1)}, bf16[64,896]{1,0:T(8,128)(2,1)S(1)}, u32[]{:S(2)}, u32[]{:S(2)}) %collective-permute-start.7) | collective-permute-done | bytes 114720 | tf_op jit(solution)/shard_map/ppermute | solution.py:48
  78.7 6.3 %collective-permute-done.8.refs_7_ = bf16[64,896]{1,0:T(8,128)(2,1)S(1)} collective-permute-done((bf16[64,896]{1,0:T(8,128)(2,1)S(1)}, bf16[64,896]{1,0:T(8,128)(2,1)S(1)}, u32[]{:S(2)}, u32[]{:S(2)}) %collective-permute-start.8) | collective-permute-done | bytes 114720 | tf_op jit(solution)/shard_map/ppermute | solution.py:48
  85.0 0.7 shard_map.47
  85.7 0.0 copy-start.1
  85.7 0.0 collective-permute-done.16
  85.8 0.1 collective-permute-start.17
  85.9 3.1 %collective-permute-start.18 = (bf16[2,64,512]{2,1,0:T(8,128)(2,1)S(1)}, bf16[2,64,512]{2,1,0:T(8,128)(2,1)S(1)}, u32[]{:S(2)}, u32[]{:S(2)}) collective-permute-start(bf16[2,64,512]{2,1,0:T(8,128)(2,1)S(1)} %pad_maximum_fusion.1), channel_id=1, source_target_pairs={{0,4},{1,5},{2,6},{3,7},{4,0},{5,1},{6,2},{7,3},{8,12},{9,13},{10,... | collective-permute-start | bytes 393224 | tf_op jit(solution)/shard_map/ppermute | solution.py:38
  89.1 1.4 %collective-permute-start.19 = (bf16[2,64,512]{2,1,0:T(8,128)(2,1)S(1)}, bf16[2,64,512]{2,1,0:T(8,128)(2,1)S(1)}, u32[]{:S(2)}, u32[]{:S(2)}) collective-permute-start(bf16[2,64,512]{2,1,0:T(8,128)(2,1)S(1)} %pad_maximum_fusion.2), channel_id=1, source_target_pairs={{0,6},{1,7},{2,4},{3,5},{4,2},{5,3},{6,0},{7,1},{8,14},{9,15},{10,... | collective-permute-start | bytes 393224 | tf_op jit(solution)/shard_map/ppermute | solution.py:38
  90.5 3.1 %collective-permute-start.20 = (bf16[2,64,512]{2,1,0:T(8,128)(2,1)S(1)}, bf16[2,64,512]{2,1,0:T(8,128)(2,1)S(1)}, u32[]{:S(2)}, u32[]{:S(2)}) collective-permute-start(bf16[2,64,512]{2,1,0:T(8,128)(2,1)S(1)} %pad_maximum_fusion.3), channel_id=1, source_target_pairs={{0,8},{1,9},{2,10},{3,11},{4,12},{5,13},{6,14},{7,15},{8,0},{9,1},... | collective-permute-start | bytes 393224 | tf_op jit(solution)/shard_map/ppermute | solution.py:38
  93.6 0.9 collective-permute-start.21
  94.5 0.0 collective-permute-done.17
  94.5 4.8 %collective-permute-start.22 = (bf16[2,64,512]{2,1,0:T(8,128)(2,1)S(1)}, bf16[2,64,512]{2,1,0:T(8,128)(2,1)S(1)}, u32[]{:S(2)}, u32[]{:S(2)}) collective-permute-start(bf16[2,64,512]{2,1,0:T(8,128)(2,1)S(1)} %pad_maximum_fusion.5), channel_id=1, source_target_pairs={{0,12},{1,13},{2,14},{3,15},{4,8},{5,9},{6,10},{7,11},{8,4},{9,5},... | collective-permute-start | bytes 393224 | tf_op jit(solution)/shard_map/ppermute | solution.py:38
  99.3 7.0 %collective-permute-done.18 = bf16[2,64,512]{2,1,0:T(8,128)(2,1)S(1)} collective-permute-done((bf16[2,64,512]{2,1,0:T(8,128)(2,1)S(1)}, bf16[2,64,512]{2,1,0:T(8,128)(2,1)S(1)}, u32[]{:S(2)}, u32[]{:S(2)}) %collective-permute-start.18) | collective-permute-done | bytes 131104 | tf_op jit(solution)/shard_map/ppermute | solution.py:38
  106.3 3.0 %collective-permute-start.23 = (bf16[2,64,512]{2,1,0:T(8,128)(2,1)S(1)}, bf16[2,64,512]{2,1,0:T(8,128)(2,1)S(1)}, u32[]{:S(2)}, u32[]{:S(2)}) collective-permute-start(bf16[2,64,512]{2,1,0:T(8,128)(2,1)S(1)} %pad_maximum_fusion.6), channel_id=1, source_target_pairs={{0,14},{1,15},{2,12},{3,13},{4,10},{5,11},{6,8},{7,9},{8,6},{9,7},... | collective-permute-start | bytes 393224 | tf_op jit(solution)/shard_map/ppermute | solution.py:38
  109.3 0.0 collective-permute-done.19
  109.4 0.0 collective-permute-done.20
  109.4 4.4 %collective-permute-done.21 = bf16[2,64,512]{2,1,0:T(8,128)(2,1)S(1)} collective-permute-done((bf16[2,64,512]{2,1,0:T(8,128)(2,1)S(1)}, bf16[2,64,512]{2,1,0:T(8,128)(2,1)S(1)}, u32[]{:S(2)}, u32[]{:S(2)}) %collective-permute-start.21) | collective-permute-done | bytes 131104 | tf_op jit(solution)/shard_map/ppermute | solution.py:38
  113.8 0.0 collective-permute-done.22
  113.8 4.0 %collective-permute-done.23 = bf16[2,64,512]{2,1,0:T(8,128)(2,1)S(1)} collective-permute-done((bf16[2,64,512]{2,1,0:T(8,128)(2,1)S(1)}, bf16[2,64,512]{2,1,0:T(8,128)(2,1)S(1)}, u32[]{:S(2)}, u32[]{:S(2)}) %collective-permute-start.23) | collective-permute-done | bytes 131104 | tf_op jit(solution)/shard_map/ppermute | solution.py:38
  117.9 1.3 %first_half.1.refs_8_ = bf16[16,64,512]{2,1,0:T(8,128)(2,1)S(1)} custom-call(s32[3]{0:T(128)S(1)} %pad_add_fusion.r_ref, bf16[64,512]{1,0:T(8,128)(2,1)S(1)} %get-tuple-element.39.refs_0_, bf16[64,512]{1,0:T(8,128)(2,1)S(1)} %get-tuple-element.67.refs_1_, bf16[64,512]{1,0:T(8,128)(2,1)S(1)} %get-tuple-element.65.refs_2_, ...), custom_call_target="tpu_custom_call" | custom-call | flops 200000000 | bytes 1400000 | tf_op jit(solution)/shard_map/first_half/pallas_call | solution.py:200
  119.1 0.0 copy-done.1
  119.1 4.6 %tail.1 = bf16[16,256,512]{2,1,0:T(8,128)(2,1)} custom-call(s32[3]{0:T(128)S(1)} %pad_add_fusion.r_ref, bf16[64,512]{1,0:T(8,128)(2,1)S(1)} %get-tuple-element.54.refs_0_, bf16[64,512]{1,0:T(8,128)(2,1)S(1)} %get-tuple-element.68.refs_1_, bf16[64,512]{1,0:T(8,128)(2,1)S(1)} %get-tuple-element.66.refs_2_, bf16[64,512]{1,0:T(8,128)(2,1)S(1)} %get-tuple-element.64.refs_3_, ...), custom_call_target="tpu_custom_call" | custom-call | flops 800000000 | bytes 7000000 | tf_op jit(solution)/shard_map/tail/pallas_call | solution.py:232
  (16 shorter events, 0.3 us)
Async XLA Ops:
  5.9 3.0 %copy-start = (bf16[16,64,512]{2,1,0:T(8,128)(2,1)S(1)}, bf16[16,64,512]{2,1,0:T(8,128)(2,1)}, u32[]{:S(2)}) copy-start(bf16[16,64,512]{2,1,0:T(8,128)(2,1)} %front.1.own_ref) | copy-start | bytes 3145732
  5.9 3.0 %collective-permute-start = (bf16[16,64,512]{2,1,0:T(8,128)(2,1)}, bf16[16,64,512]{2,1,0:T(8,128)(2,1)S(1)}, u32[]{:S(2)}, u32[]{:S(2)}) collective-permute-start(bf16[16,64,512]{2,1,0:T(8,128)(2,1)} %front.1.own_ref), channel_id=1, source_target_pairs={{0,1},{1,0},{2,3},{3,2},{4,5},{5,4},{6,7},{7,6},{8,9},{9,8},{10,11... | collective-permute-start | bytes 3145736 | tf_op jit(solution)/shard_map/ppermute | solution.py:253
  9.8 11.7 %collective-permute-start.9 = (bf16[64,896]{1,0:T(8,128)(2,1)S(1)}, bf16[64,896]{1,0:T(8,128)(2,1)S(1)}, u32[]{:S(2)}, u32[]{:S(2)}) collective-permute-start(bf16[64,896]{1,0:T(8,128)(2,1)S(1)} %get-tuple-element.30), channel_id=1, source_target_pairs={{0,2},{1,3},{2,0},{3,1},{4,6},{5,7},{6,4},{7,5},{8,10},{9,11},{10,... | collective-permute-start | bytes 344072 | tf_op jit(solution)/shard_map/ppermute | solution.py:38
  11.8 18.5 %collective-permute-start.10 = (bf16[64,896]{1,0:T(8,128)(2,1)S(1)}, bf16[64,896]{1,0:T(8,128)(2,1)S(1)}, u32[]{:S(2)}, u32[]{:S(2)}) collective-permute-start(bf16[64,896]{1,0:T(8,128)(2,1)S(1)} %get-tuple-element.31), channel_id=1, source_target_pairs={{0,4},{1,5},{2,6},{3,7},{4,0},{5,1},{6,2},{7,3},{8,12},{9,13},{10,... | collective-permute-start | bytes 344072 | tf_op jit(solution)/shard_map/ppermute | solution.py:38
  15.0 20.0 %collective-permute-start.11 = (bf16[64,896]{1,0:T(8,128)(2,1)S(1)}, bf16[64,896]{1,0:T(8,128)(2,1)S(1)}, u32[]{:S(2)}, u32[]{:S(2)}) collective-permute-start(bf16[64,896]{1,0:T(8,128)(2,1)S(1)} %get-tuple-element.32), channel_id=1, source_target_pairs={{0,6},{1,7},{2,4},{3,5},{4,2},{5,3},{6,0},{7,1},{8,14},{9,15},{10,... | collective-permute-start | bytes 344072 | tf_op jit(solution)/shard_map/ppermute | solution.py:38
  15.0 20.0 %collective-permute-start.12 = (bf16[64,896]{1,0:T(8,128)(2,1)S(1)}, bf16[64,896]{1,0:T(8,128)(2,1)S(1)}, u32[]{:S(2)}, u32[]{:S(2)}) collective-permute-start(bf16[64,896]{1,0:T(8,128)(2,1)S(1)} %get-tuple-element.33), channel_id=1, source_target_pairs={{0,8},{1,9},{2,10},{3,11},{4,12},{5,13},{6,14},{7,15},{8,0},{9,1},... | collective-permute-start | bytes 344072 | tf_op jit(solution)/shard_map/ppermute | solution.py:38
  21.4 17.4 %collective-permute-start.13 = (bf16[64,896]{1,0:T(8,128)(2,1)S(1)}, bf16[64,896]{1,0:T(8,128)(2,1)S(1)}, u32[]{:S(2)}, u32[]{:S(2)}) collective-permute-start(bf16[64,896]{1,0:T(8,128)(2,1)S(1)} %get-tuple-element.34), channel_id=1, source_target_pairs={{0,10},{1,11},{2,8},{3,9},{4,14},{5,15},{6,12},{7,13},{8,2},{9,3},... | collective-permute-start | bytes 344072 | tf_op jit(solution)/shard_map/ppermute | solution.py:38
  21.4 17.8 %collective-permute-start.14 = (bf16[64,896]{1,0:T(8,128)(2,1)S(1)}, bf16[64,896]{1,0:T(8,128)(2,1)S(1)}, u32[]{:S(2)}, u32[]{:S(2)}) collective-permute-start(bf16[64,896]{1,0:T(8,128)(2,1)S(1)} %get-tuple-element.35), channel_id=1, source_target_pairs={{0,12},{1,13},{2,14},{3,15},{4,8},{5,9},{6,10},{7,11},{8,4},{9,5},... | collective-permute-start | bytes 344072 | tf_op jit(solution)/shard_map/ppermute | solution.py:38
  30.3 12.0 %collective-permute-start.15 = (bf16[64,896]{1,0:T(8,128)(2,1)S(1)}, bf16[64,896]{1,0:T(8,128)(2,1)S(1)}, u32[]{:S(2)}, u32[]{:S(2)}) collective-permute-start(bf16[64,896]{1,0:T(8,128)(2,1)S(1)} %get-tuple-element.36), channel_id=1, source_target_pairs={{0,14},{1,15},{2,12},{3,13},{4,10},{5,11},{6,8},{7,9},{8,6},{9,7},... | collective-permute-start | bytes 344072 | tf_op jit(solution)/shard_map/ppermute | solution.py:38
  43.0 42.8 %collective-permute-start.16 = (bf16[8,64,512]{2,1,0:T(8,128)(2,1)S(1)}, bf16[8,64,512]{2,1,0:T(8,128)(2,1)S(1)}, u32[]{:S(2)}, u32[]{:S(2)}) collective-permute-start(bf16[8,64,512]{2,1,0:T(8,128)(2,1)S(1)} %shard_map.49), channel_id=1, source_target_pairs={{0,128},{1,225},{2,146},{3,243},{4,164},{5,197},{6,182},{7,215},{8... | collective-permute-start | bytes 1572872 | tf_op jit(solution)/shard_map/ppermute | solution.py:48
  47.1 8.6 %collective-permute-start.1 = (bf16[64,896]{1,0:T(8,128)(2,1)S(1)}, bf16[64,896]{1,0:T(8,128)(2,1)S(1)}, u32[]{:S(2)}, u32[]{:S(2)}) collective-permute-start(bf16[64,896]{1,0:T(8,128)(2,1)S(1)} %get-tuple-element.21), channel_id=1, source_target_pairs={{0,0},{1,97},{2,18},{3,115},{4,36},{5,69},{6,54},{7,87},{8,72},{9,... | collective-permute-start | bytes 344072 | tf_op jit(solution)/shard_map/ppermute | solution.py:48
  47.8 13.4 %collective-permute-start.2 = (bf16[64,896]{1,0:T(8,128)(2,1)S(1)}, bf16[64,896]{1,0:T(8,128)(2,1)S(1)}, u32[]{:S(2)}, u32[]{:S(2)}) collective-permute-start(bf16[64,896]{1,0:T(8,128)(2,1)S(1)} %get-tuple-element.22), channel_id=1, source_target_pairs={{0,18},{1,115},{2,0},{3,97},{4,54},{5,87},{6,36},{7,69},{8,90},{9,... | collective-permute-start | bytes 344072 | tf_op jit(solution)/shard_map/ppermute | solution.py:48
  50.6 14.5 %collective-permute-start.3 = (bf16[64,896]{1,0:T(8,128)(2,1)S(1)}, bf16[64,896]{1,0:T(8,128)(2,1)S(1)}, u32[]{:S(2)}, u32[]{:S(2)}) collective-permute-start(bf16[64,896]{1,0:T(8,128)(2,1)S(1)} %get-tuple-element.23), channel_id=1, source_target_pairs={{0,36},{1,69},{2,54},{3,87},{4,0},{5,97},{6,18},{7,115},{8,108},{9... | collective-permute-start | bytes 344072 | tf_op jit(solution)/shard_map/ppermute | solution.py:48
  55.7 16.7 %collective-permute-start.4 = (bf16[64,896]{1,0:T(8,128)(2,1)S(1)}, bf16[64,896]{1,0:T(8,128)(2,1)S(1)}, u32[]{:S(2)}, u32[]{:S(2)}) collective-permute-start(bf16[64,896]{1,0:T(8,128)(2,1)S(1)} %get-tuple-element.24), channel_id=1, source_target_pairs={{0,54},{1,87},{2,36},{3,69},{4,18},{5,115},{6,0},{7,97},{8,126},{9... | collective-permute-start | bytes 344072 | tf_op jit(solution)/shard_map/ppermute | solution.py:48
  55.7 18.3 %collective-permute-start.5 = (bf16[64,896]{1,0:T(8,128)(2,1)S(1)}, bf16[64,896]{1,0:T(8,128)(2,1)S(1)}, u32[]{:S(2)}, u32[]{:S(2)}) collective-permute-start(bf16[64,896]{1,0:T(8,128)(2,1)S(1)} %get-tuple-element.25), channel_id=1, source_target_pairs={{0,72},{1,41},{2,90},{3,59},{4,108},{5,13},{6,126},{7,31},{8,0},{9... | collective-permute-start | bytes 344072 | tf_op jit(solution)/shard_map/ppermute | solution.py:48
  61.2 14.3 %collective-permute-start.6 = (bf16[64,896]{1,0:T(8,128)(2,1)S(1)}, bf16[64,896]{1,0:T(8,128)(2,1)S(1)}, u32[]{:S(2)}, u32[]{:S(2)}) collective-permute-start(bf16[64,896]{1,0:T(8,128)(2,1)S(1)} %get-tuple-element.26), channel_id=1, source_target_pairs={{0,90},{1,59},{2,72},{3,41},{4,126},{5,31},{6,108},{7,13},{8,18},{... | collective-permute-start | bytes 344072 | tf_op jit(solution)/shard_map/ppermute | solution.py:48
  65.0 13.7 %collective-permute-start.7 = (bf16[64,896]{1,0:T(8,128)(2,1)S(1)}, bf16[64,896]{1,0:T(8,128)(2,1)S(1)}, u32[]{:S(2)}, u32[]{:S(2)}) collective-permute-start(bf16[64,896]{1,0:T(8,128)(2,1)S(1)} %get-tuple-element.27), channel_id=1, source_target_pairs={{0,108},{1,13},{2,126},{3,31},{4,72},{5,41},{6,90},{7,59},{8,36},{... | collective-permute-start | bytes 344072 | tf_op jit(solution)/shard_map/ppermute | solution.py:48
  72.4 12.5 %collective-permute-start.8 = (bf16[64,896]{1,0:T(8,128)(2,1)S(1)}, bf16[64,896]{1,0:T(8,128)(2,1)S(1)}, u32[]{:S(2)}, u32[]{:S(2)}) collective-permute-start(bf16[64,896]{1,0:T(8,128)(2,1)S(1)} %get-tuple-element.28), channel_id=1, source_target_pairs={{0,126},{1,31},{2,108},{3,13},{4,90},{5,59},{6,72},{7,41},{8,54},{... | collective-permute-start | bytes 344072 | tf_op jit(solution)/shard_map/ppermute | solution.py:48
  85.7 33.5 %copy-start.1 = (bf16[16,64,256]{2,1,0:T(8,128)(2,1)S(1)}, bf16[16,64,256]{2,1,0:T(8,128)(2,1)}, u32[]{:S(2)}) copy-start(bf16[16,64,256]{2,1,0:T(8,128)(2,1)} %refs_10_.1) | copy-start | bytes 1572868
  85.8 8.7 %collective-permute-start.17 = (bf16[2,64,512]{2,1,0:T(8,128)(2,1)S(1)}, bf16[2,64,512]{2,1,0:T(8,128)(2,1)S(1)}, u32[]{:S(2)}, u32[]{:S(2)}) collective-permute-start(bf16[2,64,512]{2,1,0:T(8,128)(2,1)S(1)} %pad_maximum_fusion), channel_id=1, source_target_pairs={{0,2},{1,3},{2,0},{3,1},{4,6},{5,7},{6,4},{7,5},{8,10},{9,11},{10,... | collective-permute-start | bytes 393224 | tf_op jit(solution)/shard_map/ppermute | solution.py:38
  85.9 20.4 %collective-permute-start.18 = (bf16[2,64,512]{2,1,0:T(8,128)(2,1)S(1)}, bf16[2,64,512]{2,1,0:T(8,128)(2,1)S(1)}, u32[]{:S(2)}, u32[]{:S(2)}) collective-permute-start(bf16[2,64,512]{2,1,0:T(8,128)(2,1)S(1)} %pad_maximum_fusion.1), channel_id=1, source_target_pairs={{0,4},{1,5},{2,6},{3,7},{4,0},{5,1},{6,2},{7,3},{8,12},{9,13},{10,... | collective-permute-start | bytes 393224 | tf_op jit(solution)/shard_map/ppermute | solution.py:38
  89.1 20.3 %collective-permute-start.19 = (bf16[2,64,512]{2,1,0:T(8,128)(2,1)S(1)}, bf16[2,64,512]{2,1,0:T(8,128)(2,1)S(1)}, u32[]{:S(2)}, u32[]{:S(2)}) collective-permute-start(bf16[2,64,512]{2,1,0:T(8,128)(2,1)S(1)} %pad_maximum_fusion.2), channel_id=1, source_target_pairs={{0,6},{1,7},{2,4},{3,5},{4,2},{5,3},{6,0},{7,1},{8,14},{9,15},{10,... | collective-permute-start | bytes 393224 | tf_op jit(solution)/shard_map/ppermute | solution.py:38
  90.5 18.9 %collective-permute-start.20 = (bf16[2,64,512]{2,1,0:T(8,128)(2,1)S(1)}, bf16[2,64,512]{2,1,0:T(8,128)(2,1)S(1)}, u32[]{:S(2)}, u32[]{:S(2)}) collective-permute-start(bf16[2,64,512]{2,1,0:T(8,128)(2,1)S(1)} %pad_maximum_fusion.3), channel_id=1, source_target_pairs={{0,8},{1,9},{2,10},{3,11},{4,12},{5,13},{6,14},{7,15},{8,0},{9,1},... | collective-permute-start | bytes 393224 | tf_op jit(solution)/shard_map/ppermute | solution.py:38
  93.6 20.2 %collective-permute-start.21 = (bf16[2,64,512]{2,1,0:T(8,128)(2,1)S(1)}, bf16[2,64,512]{2,1,0:T(8,128)(2,1)S(1)}, u32[]{:S(2)}, u32[]{:S(2)}) collective-permute-start(bf16[2,64,512]{2,1,0:T(8,128)(2,1)S(1)} %pad_maximum_fusion.4), channel_id=1, source_target_pairs={{0,10},{1,11},{2,8},{3,9},{4,14},{5,15},{6,12},{7,13},{8,2},{9,3},... | collective-permute-start | bytes 393224 | tf_op jit(solution)/shard_map/ppermute | solution.py:38
  94.5 19.3 %collective-permute-start.22 = (bf16[2,64,512]{2,1,0:T(8,128)(2,1)S(1)}, bf16[2,64,512]{2,1,0:T(8,128)(2,1)S(1)}, u32[]{:S(2)}, u32[]{:S(2)}) collective-permute-start(bf16[2,64,512]{2,1,0:T(8,128)(2,1)S(1)} %pad_maximum_fusion.5), channel_id=1, source_target_pairs={{0,12},{1,13},{2,14},{3,15},{4,8},{5,9},{6,10},{7,11},{8,4},{9,5},... | collective-permute-start | bytes 393224 | tf_op jit(solution)/shard_map/ppermute | solution.py:38
  106.3 11.5 %collective-permute-start.23 = (bf16[2,64,512]{2,1,0:T(8,128)(2,1)S(1)}, bf16[2,64,512]{2,1,0:T(8,128)(2,1)S(1)}, u32[]{:S(2)}, u32[]{:S(2)}) collective-permute-start(bf16[2,64,512]{2,1,0:T(8,128)(2,1)S(1)} %pad_maximum_fusion.6), channel_id=1, source_target_pairs={{0,14},{1,15},{2,12},{3,13},{4,10},{5,11},{6,8},{7,9},{8,6},{9,7},... | collective-permute-start | bytes 393224 | tf_op jit(solution)/shard_map/ppermute | solution.py:38

commit v3 on v2

--- a/solution.py
+++ b/solution.py
@@ -26,8 +26,6 @@
 TOP = (8, 0)
 TWIST = 6
 FAR_FIRST = (4, 5, 3, 7, 6, 2, 1)
-FAR = (4, 5, 3, 7, 6, 2, 1)
-NEAR = ()
 
 
 def base_of(r_ref):
@@ -177,44 +175,18 @@
     )(*msgs)
 
 
-def half_levels(b, r_ref, msgs, t_ref, c_ref):
+def tail_kernel(r_ref, *refs):
+    local, msgs, (t_ref, s_ref, o_hbm, c_ref, o_buf, sem) = refs[:2], refs[2 : 1 + N_Z], refs[1 + N_Z :]
     base = base_of(r_ref)
-    top = (base & 8) ^ TOP[b]
-    for d in range(N_Z):
-        c_ref[base ^ (d | TOP[b])] = msgs[d][...]
+    for b in range(2):
+        c_ref[base ^ TOP[b]] = local[b][0]
+        for d in range(1, N_Z):
+            c_ref[base ^ (d | TOP[b])] = msgs[d - 1][b]
     for e in range(3):
-        stride = 1 << e
-        for j in range(N_Z):
-            if j & stride:
-                continue
-            lo, hi = top + j, top + j + stride
-            merge_pair(c_ref, lo, hi, t_ref[e, lo], t_ref[e, hi])
-
-
-def first_half_kernel(r_ref, *refs):
-    msgs, (t_ref, c_ref) = refs[:N_Z], refs[N_Z:]
-    half_levels(0, r_ref, msgs, t_ref, c_ref)
-
-
-def first_half(where, msgs, t_tail):
-    return pl.pallas_call(
-        first_half_kernel,
-        in_specs=[SMEM] + [VMEM] * (N_Z + 1),
-        out_specs=VMEM,
-        out_shape=jax.ShapeDtypeStruct((SLOTS, RANK, LANES), BF),
-        cost_estimate=pl.CostEstimate(flops=200_000_000, bytes_accessed=1_400_000, transcendentals=0),
-        compiler_params=pltpu.CompilerParams(vmem_limit_bytes=6 << 20),
-        name="first_half",
-    )(where, *msgs, t_tail)
-
-
-def tail_kernel(r_ref, *refs):
-    msgs, (half_ref, t_ref, s_ref, o_hbm, c_ref, o_buf, sem) = refs[:N_Z], refs[N_Z:]
-    base = base_of(r_ref)
-    half_levels(1, r_ref, msgs, t_ref, c_ref)
-    first = (base & 8) ^ TOP[0]
-    for j in range(N_Z):
-        c_ref[first + j] = half_ref[first + j]
+        for lo in range(SLOTS):
+            if not (lo >> e) & 1:
+                hi = lo + (1 << e)
+                merge_pair(c_ref, lo, hi, t_ref[e, lo], t_ref[e, hi])
     copies = []
     for j in range(N_Z):
         merge_pair(c_ref, j, j + 8, t_ref[3, j], t_ref[3, j + 8])
@@ -228,7 +200,7 @@
         copy.wait()
 
 
-def tail(where, msgs, half, t_tail, synthesis):
+def tail(where, local, msgs, t_tail, synthesis):
     return pl.pallas_call(
         tail_kernel,
         in_specs=[SMEM] + [VMEM] * (N_Z + 3),
@@ -242,7 +214,7 @@
         cost_estimate=pl.CostEstimate(flops=800_000_000, bytes_accessed=7_000_000, transcendentals=0),
         compiler_params=pltpu.CompilerParams(vmem_limit_bytes=14 << 20),
         name="tail",
-    )(where, *msgs, half, t_tail, synthesis)
+    )(where, *local, *msgs, t_tail, synthesis)
 
 
 def pipeline(features, analysis, transitions, synthesis):
@@ -260,21 +232,16 @@
             elif d:
                 group[d] = z_swap(group[d], d)
         groups.append(group)
-    merged, arrived = [], []
+    merged = []
     for b in range(2):
         blocks = host_merge(groups[b])
         if b == 0:
             blocks = to_target_row(blocks, 0)
-        group = [blocks[0]] * N_Z
-        for d in NEAR:
-            group[d] = z_swap(blocks[d], d)
         merged.append(blocks)
-        arrived.append(group)
-    for d in FAR:
-        pair = z_swap(jnp.stack([merged[0][d], merged[1][d]]), d)
-        arrived[0][d], arrived[1][d] = pair[0], pair[1]
-    half = first_half(where, arrived[0], t_tail)
-    return tail(where, arrived[1], half, t_tail, synthesis)
+    arrived = {}
+    for d in FAR_FIRST:
+        arrived[d] = z_swap(jnp.stack([merged[0][d], merged[1][d]]), d)
+    return tail(where, merged, [arrived[d] for d in range(1, N_Z)], t_tail, synthesis)
 
 
 def solution(mesh):

time: 124 us -> 123 us (level)
    pallas_call x1 -> x0, Pallas kernels: 1.27 us -> none  [first_half(): pl.pallas_call(first_half_kernel, in_specs=[SMEM] + [VMEM] * (N_Z + 1), o...]
where the time goes in v3:
time: 123 us
  starting transfers between devices  67.8 us (55%)
  waiting for transfers between devices  38.8 us (32%)
  Pallas kernels  13.7 us (11%)
  local copies, waits for them, and re-layouts  1.89 us (2%)
    ppermute x14, starting transfers between devices, z_swap(): return lax.ppermute(array, 'col', [(c, c ^ 2 * d) for c in range(N_COL)])  37.5 us
    ppermute x9, starting transfers between devices, to_target_row(): return lax.ppermute(array, ('row', 'col'), pairs)  30.2 us
    ppermute x14, waiting for transfers between devices, z_swap(): return lax.ppermute(array, 'col', [(c, c ^ 2 * d) for c in range(N_COL)])  26.9 us
    ppermute x9, waiting for transfers between devices, to_target_row(): return lax.ppermute(array, ('row', 'col'), pairs)  10.9 us
    pallas_call x1, Pallas kernels, front(): pl.pallas_call(front_kernel, in_specs=[HBM] * 3, out_specs=VMEM, out_shap...  5.92 us
    pallas_call x1, Pallas kernels, tail(): pl.pallas_call(tail_kernel, in_specs=[SMEM] + [VMEM] * (N_Z + 3), out_spe...  4.74 us
  transfers between devices with their start and end apart: 24, of which 11 were waited for; matrix products, arithmetic and copies ran while one was open for 2% of the time, Pallas kernels for 1%

profile of v3, /device:TPU:2, one launch (start us, length us, event | category | flops | bytes accessed | tf_op | source)
XLA Modules:
  0.0 122.7 jit_solution(6245604477035285537)
XLA Ops:
  0.0 5.9 %front.1.own_ref = bf16[16,64,512]{2,1,0:T(8,128)(2,1)} custom-call(bf16[16,256,512]{2,1,0:T(8,128)(2,1)} %f_hbm.1, bf16[16,64,256]{2,1,0:T(8,128)(2,1)} %a_hbm.1, bf16[12,16,64,128]{3,2,1,0:T(8,128)(2,1)} %t_hbm.1), custom_call_target="tpu_custom_call" | custom-call | flops 800000000 | bytes 7000000 | tf_op jit(solution)/shard_map/front/pallas_call | solution.py:104
  5.9 0.0 copy-start
  5.9 0.1 collective-permute-start
  6.1 0.1 pad_add_fusion.r_ref
  6.1 1.8 %fusion = (bf16[4,16,64,128]{3,2,1,0:T(8,128)(2,1)S(1)}, bf16[4,16,64,128]{3,2,1,0:T(8,128)(2,1)S(1)}) fusion(bf16[12,16,64,128]{3,2,1,0:T(8,128)(2,1)} %t_hbm.1), kind=kLoop, calls=%fused_computation.8 | loop fusion | bytes 4194304 | tf_op jit(solution)/shard_map/slice | solution.py:224
  7.9 1.0 collective-permute-done.partner_ref
  8.9 0.0 copy-done
  8.9 0.8 shard_map.46
  9.8 2.0 %collective-permute-start.1 = (bf16[64,896]{1,0:T(8,128)(2,1)S(1)}, bf16[64,896]{1,0:T(8,128)(2,1)S(1)}, u32[]{:S(2)}, u32[]{:S(2)}) collective-permute-start(bf16[64,896]{1,0:T(8,128)(2,1)S(1)} %get-tuple-element.22), channel_id=1, source_target_pairs={{0,2},{1,3},{2,0},{3,1},{4,6},{5,7},{6,4},{7,5},{8,10},{9,11},{10,... | collective-permute-start | bytes 344072 | tf_op jit(solution)/shard_map/ppermute | solution.py:36
  11.8 3.3 %collective-permute-start.2 = (bf16[64,896]{1,0:T(8,128)(2,1)S(1)}, bf16[64,896]{1,0:T(8,128)(2,1)S(1)}, u32[]{:S(2)}, u32[]{:S(2)}) collective-permute-start(bf16[64,896]{1,0:T(8,128)(2,1)S(1)} %get-tuple-element.23), channel_id=1, source_target_pairs={{0,4},{1,5},{2,6},{3,7},{4,0},{5,1},{6,2},{7,3},{8,12},{9,13},{10,... | collective-permute-start | bytes 344072 | tf_op jit(solution)/shard_map/ppermute | solution.py:36
  15.0 0.0 collective-permute-start.3
  15.0 6.4 %collective-permute-start.4 = (bf16[64,896]{1,0:T(8,128)(2,1)S(1)}, bf16[64,896]{1,0:T(8,128)(2,1)S(1)}, u32[]{:S(2)}, u32[]{:S(2)}) collective-permute-start(bf16[64,896]{1,0:T(8,128)(2,1)S(1)} %get-tuple-element.25), channel_id=1, source_target_pairs={{0,8},{1,9},{2,10},{3,11},{4,12},{5,13},{6,14},{7,15},{8,0},{9,1},... | collective-permute-start | bytes 344072 | tf_op jit(solution)/shard_map/ppermute | solution.py:36
  21.4 0.0 collective-permute-start.5
  21.4 0.0 collective-permute-done.1.refs_1_
  21.4 4.6 %collective-permute-start.6 = (bf16[64,896]{1,0:T(8,128)(2,1)S(1)}, bf16[64,896]{1,0:T(8,128)(2,1)S(1)}, u32[]{:S(2)}, u32[]{:S(2)}) collective-permute-start(bf16[64,896]{1,0:T(8,128)(2,1)S(1)} %get-tuple-element.27), channel_id=1, source_target_pairs={{0,12},{1,13},{2,14},{3,15},{4,8},{5,9},{6,10},{7,11},{8,4},{9,5},... | collective-permute-start | bytes 344072 | tf_op jit(solution)/shard_map/ppermute | solution.py:36
  26.0 4.2 %collective-permute-done.2.refs_2_ = bf16[64,896]{1,0:T(8,128)(2,1)S(1)} collective-permute-done((bf16[64,896]{1,0:T(8,128)(2,1)S(1)}, bf16[64,896]{1,0:T(8,128)(2,1)S(1)}, u32[]{:S(2)}, u32[]{:S(2)}) %collective-permute-start.2) | collective-permute-done | bytes 114720 | tf_op jit(solution)/shard_map/ppermute | solution.py:36
  30.3 4.8 %collective-permute-start.7 = (bf16[64,896]{1,0:T(8,128)(2,1)S(1)}, bf16[64,896]{1,0:T(8,128)(2,1)S(1)}, u32[]{:S(2)}, u32[]{:S(2)}) collective-permute-start(bf16[64,896]{1,0:T(8,128)(2,1)S(1)} %get-tuple-element.28), channel_id=1, source_target_pairs={{0,14},{1,15},{2,12},{3,13},{4,10},{5,11},{6,8},{7,9},{8,6},{9,7},... | collective-permute-start | bytes 344072 | tf_op jit(solution)/shard_map/ppermute | solution.py:36
  35.1 0.0 collective-permute-done.3.refs_3_
  35.1 0.0 collective-permute-done.4.refs_4_
  35.1 3.8 %collective-permute-done.5.refs_5_ = bf16[64,896]{1,0:T(8,128)(2,1)S(1)} collective-permute-done((bf16[64,896]{1,0:T(8,128)(2,1)S(1)}, bf16[64,896]{1,0:T(8,128)(2,1)S(1)}, u32[]{:S(2)}, u32[]{:S(2)}) %collective-permute-start.5) | collective-permute-done | bytes 114720 | tf_op jit(solution)/shard_map/ppermute | solution.py:36
  38.9 0.3 collective-permute-done.6.refs_6_
  39.2 3.1 %collective-permute-done.7.refs_7_ = bf16[64,896]{1,0:T(8,128)(2,1)S(1)} collective-permute-done((bf16[64,896]{1,0:T(8,128)(2,1)S(1)}, bf16[64,896]{1,0:T(8,128)(2,1)S(1)}, u32[]{:S(2)}, u32[]{:S(2)}) %collective-permute-start.7) | collective-permute-done | bytes 114720 | tf_op jit(solution)/shard_map/ppermute | solution.py:36
  42.3 0.7 shard_map.47
  43.0 0.0 copy-start.1
  43.0 3.3 %collective-permute-start.8 = (bf16[8,64,512]{2,1,0:T(8,128)(2,1)S(1)}, bf16[8,64,512]{2,1,0:T(8,128)(2,1)S(1)}, u32[]{:S(2)}, u32[]{:S(2)}) collective-permute-start(bf16[8,64,512]{2,1,0:T(8,128)(2,1)S(1)} %shard_map.47), channel_id=1, source_target_pairs={{0,128},{1,225},{2,146},{3,243},{4,164},{5,197},{6,182},{7,215},{8... | collective-permute-start | bytes 1572872 | tf_op jit(solution)/shard_map/ppermute | solution.py:46
  46.3 0.8 shard_map.48
  47.1 0.7 collective-permute-start.9
  47.8 2.8 %collective-permute-start.10 = (bf16[64,896]{1,0:T(8,128)(2,1)S(1)}, bf16[64,896]{1,0:T(8,128)(2,1)S(1)}, u32[]{:S(2)}, u32[]{:S(2)}) collective-permute-start(bf16[64,896]{1,0:T(8,128)(2,1)S(1)} %get-tuple-element.30), channel_id=1, source_target_pairs={{0,18},{1,115},{2,0},{3,97},{4,54},{5,87},{6,36},{7,69},{8,90},{9,... | collective-permute-start | bytes 344072 | tf_op jit(solution)/shard_map/ppermute | solution.py:46
  50.6 5.2 %collective-permute-start.11 = (bf16[64,896]{1,0:T(8,128)(2,1)S(1)}, bf16[64,896]{1,0:T(8,128)(2,1)S(1)}, u32[]{:S(2)}, u32[]{:S(2)}) collective-permute-start(bf16[64,896]{1,0:T(8,128)(2,1)S(1)} %get-tuple-element.31), channel_id=1, source_target_pairs={{0,36},{1,69},{2,54},{3,87},{4,0},{5,97},{6,18},{7,115},{8,108},{9... | collective-permute-start | bytes 344072 | tf_op jit(solution)/shard_map/ppermute | solution.py:46
  55.7 0.0 collective-permute-start.12
  55.7 0.0 collective-permute-done.9.refs_0_
  55.7 5.4 %collective-permute-start.13 = (bf16[64,896]{1,0:T(8,128)(2,1)S(1)}, bf16[64,896]{1,0:T(8,128)(2,1)S(1)}, u32[]{:S(2)}, u32[]{:S(2)}) collective-permute-start(bf16[64,896]{1,0:T(8,128)(2,1)S(1)} %get-tuple-element.33), channel_id=1, source_target_pairs={{0,72},{1,41},{2,90},{3,59},{4,108},{5,13},{6,126},{7,31},{8,0},{9... | collective-permute-start | bytes 344072 | tf_op jit(solution)/shard_map/ppermute | solution.py:46
  61.2 0.0 collective-permute-done.10.refs_1_
  61.2 3.9 %collective-permute-start.14 = (bf16[64,896]{1,0:T(8,128)(2,1)S(1)}, bf16[64,896]{1,0:T(8,128)(2,1)S(1)}, u32[]{:S(2)}, u32[]{:S(2)}) collective-permute-start(bf16[64,896]{1,0:T(8,128)(2,1)S(1)} %get-tuple-element.34), channel_id=1, source_target_pairs={{0,90},{1,59},{2,72},{3,41},{4,126},{5,31},{6,108},{7,13},{8,18},{... | collective-permute-start | bytes 344072 | tf_op jit(solution)/shard_map/ppermute | solution.py:46
  65.0 0.0 collective-permute-done.11.refs_2_
  65.0 7.4 %collective-permute-start.15 = (bf16[64,896]{1,0:T(8,128)(2,1)S(1)}, bf16[64,896]{1,0:T(8,128)(2,1)S(1)}, u32[]{:S(2)}, u32[]{:S(2)}) collective-permute-start(bf16[64,896]{1,0:T(8,128)(2,1)S(1)} %get-tuple-element.35), channel_id=1, source_target_pairs={{0,108},{1,13},{2,126},{3,31},{4,72},{5,41},{6,90},{7,59},{8,36},{... | collective-permute-start | bytes 344072 | tf_op jit(solution)/shard_map/ppermute | solution.py:46
  72.5 0.0 collective-permute-done.12.refs_3_
  72.5 1.6 %collective-permute-start.16 = (bf16[64,896]{1,0:T(8,128)(2,1)S(1)}, bf16[64,896]{1,0:T(8,128)(2,1)S(1)}, u32[]{:S(2)}, u32[]{:S(2)}) collective-permute-start(bf16[64,896]{1,0:T(8,128)(2,1)S(1)} %get-tuple-element.36), channel_id=1, source_target_pairs={{0,126},{1,31},{2,108},{3,13},{4,90},{5,59},{6,72},{7,41},{8,54},{... | collective-permute-start | bytes 344072 | tf_op jit(solution)/shard_map/ppermute | solution.py:46
  74.1 0.0 collective-permute-done.13.refs_4_
  74.1 1.4 %collective-permute-done.14.refs_5_ = bf16[64,896]{1,0:T(8,128)(2,1)S(1)} collective-permute-done((bf16[64,896]{1,0:T(8,128)(2,1)S(1)}, bf16[64,896]{1,0:T(8,128)(2,1)S(1)}, u32[]{:S(2)}, u32[]{:S(2)}) %collective-permute-start.14) | collective-permute-done | bytes 114720 | tf_op jit(solution)/shard_map/ppermute | solution.py:46
  75.5 3.3 %collective-permute-done.15.refs_6_ = bf16[64,896]{1,0:T(8,128)(2,1)S(1)} collective-permute-done((bf16[64,896]{1,0:T(8,128)(2,1)S(1)}, bf16[64,896]{1,0:T(8,128)(2,1)S(1)}, u32[]{:S(2)}, u32[]{:S(2)}) %collective-permute-start.15) | collective-permute-done | bytes 114720 | tf_op jit(solution)/shard_map/ppermute | solution.py:46
  78.7 6.3 %collective-permute-done.16.refs_7_ = bf16[64,896]{1,0:T(8,128)(2,1)S(1)} collective-permute-done((bf16[64,896]{1,0:T(8,128)(2,1)S(1)}, bf16[64,896]{1,0:T(8,128)(2,1)S(1)}, u32[]{:S(2)}, u32[]{:S(2)}) %collective-permute-start.16) | collective-permute-done | bytes 114720 | tf_op jit(solution)/shard_map/ppermute | solution.py:46
  85.0 0.7 shard_map.49.refs_1_
  85.7 0.0 collective-permute-done.8.refs_0_
  85.8 0.1 collective-permute-start.17
  85.9 3.1 %collective-permute-start.18 = (bf16[2,64,512]{2,1,0:T(8,128)(2,1)S(1)}, bf16[2,64,512]{2,1,0:T(8,128)(2,1)S(1)}, u32[]{:S(2)}, u32[]{:S(2)}) collective-permute-start(bf16[2,64,512]{2,1,0:T(8,128)(2,1)S(1)} %pad_maximum_fusion.1), channel_id=1, source_target_pairs={{0,4},{1,5},{2,6},{3,7},{4,0},{5,1},{6,2},{7,3},{8,12},{9,13},{10,... | collective-permute-start | bytes 393224 | tf_op jit(solution)/shard_map/ppermute | solution.py:36
  89.1 1.4 %collective-permute-start.19 = (bf16[2,64,512]{2,1,0:T(8,128)(2,1)S(1)}, bf16[2,64,512]{2,1,0:T(8,128)(2,1)S(1)}, u32[]{:S(2)}, u32[]{:S(2)}) collective-permute-start(bf16[2,64,512]{2,1,0:T(8,128)(2,1)S(1)} %pad_maximum_fusion.2), channel_id=1, source_target_pairs={{0,6},{1,7},{2,4},{3,5},{4,2},{5,3},{6,0},{7,1},{8,14},{9,15},{10,... | collective-permute-start | bytes 393224 | tf_op jit(solution)/shard_map/ppermute | solution.py:36
  90.5 3.1 %collective-permute-start.20 = (bf16[2,64,512]{2,1,0:T(8,128)(2,1)S(1)}, bf16[2,64,512]{2,1,0:T(8,128)(2,1)S(1)}, u32[]{:S(2)}, u32[]{:S(2)}) collective-permute-start(bf16[2,64,512]{2,1,0:T(8,128)(2,1)S(1)} %pad_maximum_fusion.3), channel_id=1, source_target_pairs={{0,8},{1,9},{2,10},{3,11},{4,12},{5,13},{6,14},{7,15},{8,0},{9,1},... | collective-permute-start | bytes 393224 | tf_op jit(solution)/shard_map/ppermute | solution.py:36
  93.6 0.8 collective-permute-start.21
  94.5 0.0 collective-permute-done.17.refs_2_
  94.5 4.8 %collective-permute-start.22 = (bf16[2,64,512]{2,1,0:T(8,128)(2,1)S(1)}, bf16[2,64,512]{2,1,0:T(8,128)(2,1)S(1)}, u32[]{:S(2)}, u32[]{:S(2)}) collective-permute-start(bf16[2,64,512]{2,1,0:T(8,128)(2,1)S(1)} %pad_maximum_fusion.5), channel_id=1, source_target_pairs={{0,12},{1,13},{2,14},{3,15},{4,8},{5,9},{6,10},{7,11},{8,4},{9,5},... | collective-permute-start | bytes 393224 | tf_op jit(solution)/shard_map/ppermute | solution.py:36
  99.3 6.9 %collective-permute-done.18.refs_3_ = bf16[2,64,512]{2,1,0:T(8,128)(2,1)S(1)} collective-permute-done((bf16[2,64,512]{2,1,0:T(8,128)(2,1)S(1)}, bf16[2,64,512]{2,1,0:T(8,128)(2,1)S(1)}, u32[]{:S(2)}, u32[]{:S(2)}) %collective-permute-start.18) | collective-permute-done | bytes 131104 | tf_op jit(solution)/shard_map/ppermute | solution.py:36
  106.2 3.1 %collective-permute-start.23 = (bf16[2,64,512]{2,1,0:T(8,128)(2,1)S(1)}, bf16[2,64,512]{2,1,0:T(8,128)(2,1)S(1)}, u32[]{:S(2)}, u32[]{:S(2)}) collective-permute-start(bf16[2,64,512]{2,1,0:T(8,128)(2,1)S(1)} %pad_maximum_fusion.6), channel_id=1, source_target_pairs={{0,14},{1,15},{2,12},{3,13},{4,10},{5,11},{6,8},{7,9},{8,6},{9,7},... | collective-permute-start | bytes 393224 | tf_op jit(solution)/shard_map/ppermute | solution.py:36
  109.3 0.0 collective-permute-done.19.refs_4_
  109.3 0.0 collective-permute-done.20.refs_5_
  109.3 4.5 %collective-permute-done.21.refs_6_ = bf16[2,64,512]{2,1,0:T(8,128)(2,1)S(1)} collective-permute-done((bf16[2,64,512]{2,1,0:T(8,128)(2,1)S(1)}, bf16[2,64,512]{2,1,0:T(8,128)(2,1)S(1)}, u32[]{:S(2)}, u32[]{:S(2)}) %collective-permute-start.21) | collective-permute-done | bytes 131104 | tf_op jit(solution)/shard_map/ppermute | solution.py:36
  113.8 0.0 collective-permute-done.22.refs_7_
  113.8 4.1 %collective-permute-done.23.refs_8_ = bf16[2,64,512]{2,1,0:T(8,128)(2,1)S(1)} collective-permute-done((bf16[2,64,512]{2,1,0:T(8,128)(2,1)S(1)}, bf16[2,64,512]{2,1,0:T(8,128)(2,1)S(1)}, u32[]{:S(2)}, u32[]{:S(2)}) %collective-permute-start.23) | collective-permute-done | bytes 131104 | tf_op jit(solution)/shard_map/ppermute | solution.py:36
  117.8 0.0 copy-done.1
  117.8 4.7 %tail.1 = bf16[16,256,512]{2,1,0:T(8,128)(2,1)} custom-call(s32[3]{0:T(128)S(1)} %pad_add_fusion.r_ref, bf16[8,64,512]{2,1,0:T(8,128)(2,1)S(1)} %collective-permute-done.8.refs_0_, bf16[8,64,512]{2,1,0:T(8,128)(2,1)S(1)} %shard_map.49.refs_1_, bf16[2,64,512]{2,1,0:T(8,128)(2,1)S(1)} %collective-permute-done.17.refs_2_, ...), custom_call_target="tpu_custom_call" | custom-call | flops 800000000 | bytes 7000000 | tf_op jit(solution)/shard_map/tail/pallas_call | solution.py:204
  (9 shorter events, 0.2 us)
Async XLA Ops:
  5.9 3.0 %copy-start = (bf16[16,64,512]{2,1,0:T(8,128)(2,1)S(1)}, bf16[16,64,512]{2,1,0:T(8,128)(2,1)}, u32[]{:S(2)}) copy-start(bf16[16,64,512]{2,1,0:T(8,128)(2,1)} %front.1.own_ref) | copy-start | bytes 3145732
  5.9 3.0 %collective-permute-start = (bf16[16,64,512]{2,1,0:T(8,128)(2,1)}, bf16[16,64,512]{2,1,0:T(8,128)(2,1)S(1)}, u32[]{:S(2)}, u32[]{:S(2)}) collective-permute-start(bf16[16,64,512]{2,1,0:T(8,128)(2,1)} %front.1.own_ref), channel_id=1, source_target_pairs={{0,1},{1,0},{2,3},{3,2},{4,5},{5,4},{6,7},{7,6},{8,9},{9,8},{10,11... | collective-permute-start | bytes 3145736 | tf_op jit(solution)/shard_map/ppermute | solution.py:225
  9.8 11.7 %collective-permute-start.1 = (bf16[64,896]{1,0:T(8,128)(2,1)S(1)}, bf16[64,896]{1,0:T(8,128)(2,1)S(1)}, u32[]{:S(2)}, u32[]{:S(2)}) collective-permute-start(bf16[64,896]{1,0:T(8,128)(2,1)S(1)} %get-tuple-element.22), channel_id=1, source_target_pairs={{0,2},{1,3},{2,0},{3,1},{4,6},{5,7},{6,4},{7,5},{8,10},{9,11},{10,... | collective-permute-start | bytes 344072 | tf_op jit(solution)/shard_map/ppermute | solution.py:36
  11.8 18.5 %collective-permute-start.2 = (bf16[64,896]{1,0:T(8,128)(2,1)S(1)}, bf16[64,896]{1,0:T(8,128)(2,1)S(1)}, u32[]{:S(2)}, u32[]{:S(2)}) collective-permute-start(bf16[64,896]{1,0:T(8,128)(2,1)S(1)} %get-tuple-element.23), channel_id=1, source_target_pairs={{0,4},{1,5},{2,6},{3,7},{4,0},{5,1},{6,2},{7,3},{8,12},{9,13},{10,... | collective-permute-start | bytes 344072 | tf_op jit(solution)/shard_map/ppermute | solution.py:36
  15.0 20.0 %collective-permute-start.3 = (bf16[64,896]{1,0:T(8,128)(2,1)S(1)}, bf16[64,896]{1,0:T(8,128)(2,1)S(1)}, u32[]{:S(2)}, u32[]{:S(2)}) collective-permute-start(bf16[64,896]{1,0:T(8,128)(2,1)S(1)} %get-tuple-element.24), channel_id=1, source_target_pairs={{0,6},{1,7},{2,4},{3,5},{4,2},{5,3},{6,0},{7,1},{8,14},{9,15},{10,... | collective-permute-start | bytes 344072 | tf_op jit(solution)/shard_map/ppermute | solution.py:36
  15.0 20.0 %collective-permute-start.4 = (bf16[64,896]{1,0:T(8,128)(2,1)S(1)}, bf16[64,896]{1,0:T(8,128)(2,1)S(1)}, u32[]{:S(2)}, u32[]{:S(2)}) collective-permute-start(bf16[64,896]{1,0:T(8,128)(2,1)S(1)} %get-tuple-element.25), channel_id=1, source_target_pairs={{0,8},{1,9},{2,10},{3,11},{4,12},{5,13},{6,14},{7,15},{8,0},{9,1},... | collective-permute-start | bytes 344072 | tf_op jit(solution)/shard_map/ppermute | solution.py:36
  21.4 17.4 %collective-permute-start.5 = (bf16[64,896]{1,0:T(8,128)(2,1)S(1)}, bf16[64,896]{1,0:T(8,128)(2,1)S(1)}, u32[]{:S(2)}, u32[]{:S(2)}) collective-permute-start(bf16[64,896]{1,0:T(8,128)(2,1)S(1)} %get-tuple-element.26), channel_id=1, source_target_pairs={{0,10},{1,11},{2,8},{3,9},{4,14},{5,15},{6,12},{7,13},{8,2},{9,3},... | collective-permute-start | bytes 344072 | tf_op jit(solution)/shard_map/ppermute | solution.py:36
  21.4 17.8 %collective-permute-start.6 = (bf16[64,896]{1,0:T(8,128)(2,1)S(1)}, bf16[64,896]{1,0:T(8,128)(2,1)S(1)}, u32[]{:S(2)}, u32[]{:S(2)}) collective-permute-start(bf16[64,896]{1,0:T(8,128)(2,1)S(1)} %get-tuple-element.27), channel_id=1, source_target_pairs={{0,12},{1,13},{2,14},{3,15},{4,8},{5,9},{6,10},{7,11},{8,4},{9,5},... | collective-permute-start | bytes 344072 | tf_op jit(solution)/shard_map/ppermute | solution.py:36
  30.3 12.0 %collective-permute-start.7 = (bf16[64,896]{1,0:T(8,128)(2,1)S(1)}, bf16[64,896]{1,0:T(8,128)(2,1)S(1)}, u32[]{:S(2)}, u32[]{:S(2)}) collective-permute-start(bf16[64,896]{1,0:T(8,128)(2,1)S(1)} %get-tuple-element.28), channel_id=1, source_target_pairs={{0,14},{1,15},{2,12},{3,13},{4,10},{5,11},{6,8},{7,9},{8,6},{9,7},... | collective-permute-start | bytes 344072 | tf_op jit(solution)/shard_map/ppermute | solution.py:36
  43.0 74.9 %copy-start.1 = (bf16[16,64,256]{2,1,0:T(8,128)(2,1)S(1)}, bf16[16,64,256]{2,1,0:T(8,128)(2,1)}, u32[]{:S(2)}) copy-start(bf16[16,64,256]{2,1,0:T(8,128)(2,1)} %refs_10_.1) | copy-start | bytes 1572868
  43.0 42.7 %collective-permute-start.8 = (bf16[8,64,512]{2,1,0:T(8,128)(2,1)S(1)}, bf16[8,64,512]{2,1,0:T(8,128)(2,1)S(1)}, u32[]{:S(2)}, u32[]{:S(2)}) collective-permute-start(bf16[8,64,512]{2,1,0:T(8,128)(2,1)S(1)} %shard_map.47), channel_id=1, source_target_pairs={{0,128},{1,225},{2,146},{3,243},{4,164},{5,197},{6,182},{7,215},{8... | collective-permute-start | bytes 1572872 | tf_op jit(solution)/shard_map/ppermute | solution.py:46
  47.1 8.6 %collective-permute-start.9 = (bf16[64,896]{1,0:T(8,128)(2,1)S(1)}, bf16[64,896]{1,0:T(8,128)(2,1)S(1)}, u32[]{:S(2)}, u32[]{:S(2)}) collective-permute-start(bf16[64,896]{1,0:T(8,128)(2,1)S(1)} %get-tuple-element.29), channel_id=1, source_target_pairs={{0,0},{1,97},{2,18},{3,115},{4,36},{5,69},{6,54},{7,87},{8,72},{9,... | collective-permute-start | bytes 344072 | tf_op jit(solution)/shard_map/ppermute | solution.py:46
  47.8 13.4 %collective-permute-start.10 = (bf16[64,896]{1,0:T(8,128)(2,1)S(1)}, bf16[64,896]{1,0:T(8,128)(2,1)S(1)}, u32[]{:S(2)}, u32[]{:S(2)}) collective-permute-start(bf16[64,896]{1,0:T(8,128)(2,1)S(1)} %get-tuple-element.30), channel_id=1, source_target_pairs={{0,18},{1,115},{2,0},{3,97},{4,54},{5,87},{6,36},{7,69},{8,90},{9,... | collective-permute-start | bytes 344072 | tf_op jit(solution)/shard_map/ppermute | solution.py:46
  50.6 14.5 %collective-permute-start.11 = (bf16[64,896]{1,0:T(8,128)(2,1)S(1)}, bf16[64,896]{1,0:T(8,128)(2,1)S(1)}, u32[]{:S(2)}, u32[]{:S(2)}) collective-permute-start(bf16[64,896]{1,0:T(8,128)(2,1)S(1)} %get-tuple-element.31), channel_id=1, source_target_pairs={{0,36},{1,69},{2,54},{3,87},{4,0},{5,97},{6,18},{7,115},{8,108},{9... | collective-permute-start | bytes 344072 | tf_op jit(solution)/shard_map/ppermute | solution.py:46
  55.7 16.7 %collective-permute-start.12 = (bf16[64,896]{1,0:T(8,128)(2,1)S(1)}, bf16[64,896]{1,0:T(8,128)(2,1)S(1)}, u32[]{:S(2)}, u32[]{:S(2)}) collective-permute-start(bf16[64,896]{1,0:T(8,128)(2,1)S(1)} %get-tuple-element.32), channel_id=1, source_target_pairs={{0,54},{1,87},{2,36},{3,69},{4,18},{5,115},{6,0},{7,97},{8,126},{9... | collective-permute-start | bytes 344072 | tf_op jit(solution)/shard_map/ppermute | solution.py:46
  55.7 18.3 %collective-permute-start.13 = (bf16[64,896]{1,0:T(8,128)(2,1)S(1)}, bf16[64,896]{1,0:T(8,128)(2,1)S(1)}, u32[]{:S(2)}, u32[]{:S(2)}) collective-permute-start(bf16[64,896]{1,0:T(8,128)(2,1)S(1)} %get-tuple-element.33), channel_id=1, source_target_pairs={{0,72},{1,41},{2,90},{3,59},{4,108},{5,13},{6,126},{7,31},{8,0},{9... | collective-permute-start | bytes 344072 | tf_op jit(solution)/shard_map/ppermute | solution.py:46
  61.2 14.3 %collective-permute-start.14 = (bf16[64,896]{1,0:T(8,128)(2,1)S(1)}, bf16[64,896]{1,0:T(8,128)(2,1)S(1)}, u32[]{:S(2)}, u32[]{:S(2)}) collective-permute-start(bf16[64,896]{1,0:T(8,128)(2,1)S(1)} %get-tuple-element.34), channel_id=1, source_target_pairs={{0,90},{1,59},{2,72},{3,41},{4,126},{5,31},{6,108},{7,13},{8,18},{... | collective-permute-start | bytes 344072 | tf_op jit(solution)/shard_map/ppermute | solution.py:46
  65.0 13.7 %collective-permute-start.15 = (bf16[64,896]{1,0:T(8,128)(2,1)S(1)}, bf16[64,896]{1,0:T(8,128)(2,1)S(1)}, u32[]{:S(2)}, u32[]{:S(2)}) collective-permute-start(bf16[64,896]{1,0:T(8,128)(2,1)S(1)} %get-tuple-element.35), channel_id=1, source_target_pairs={{0,108},{1,13},{2,126},{3,31},{4,72},{5,41},{6,90},{7,59},{8,36},{... | collective-permute-start | bytes 344072 | tf_op jit(solution)/shard_map/ppermute | solution.py:46
  72.5 12.5 %collective-permute-start.16 = (bf16[64,896]{1,0:T(8,128)(2,1)S(1)}, bf16[64,896]{1,0:T(8,128)(2,1)S(1)}, u32[]{:S(2)}, u32[]{:S(2)}) collective-permute-start(bf16[64,896]{1,0:T(8,128)(2,1)S(1)} %get-tuple-element.36), channel_id=1, source_target_pairs={{0,126},{1,31},{2,108},{3,13},{4,90},{5,59},{6,72},{7,41},{8,54},{... | collective-permute-start | bytes 344072 | tf_op jit(solution)/shard_map/ppermute | solution.py:46
  85.8 8.6 %collective-permute-start.17 = (bf16[2,64,512]{2,1,0:T(8,128)(2,1)S(1)}, bf16[2,64,512]{2,1,0:T(8,128)(2,1)S(1)}, u32[]{:S(2)}, u32[]{:S(2)}) collective-permute-start(bf16[2,64,512]{2,1,0:T(8,128)(2,1)S(1)} %pad_maximum_fusion), channel_id=1, source_target_pairs={{0,2},{1,3},{2,0},{3,1},{4,6},{5,7},{6,4},{7,5},{8,10},{9,11},{10,... | collective-permute-start | bytes 393224 | tf_op jit(solution)/shard_map/ppermute | solution.py:36
  85.9 20.3 %collective-permute-start.18 = (bf16[2,64,512]{2,1,0:T(8,128)(2,1)S(1)}, bf16[2,64,512]{2,1,0:T(8,128)(2,1)S(1)}, u32[]{:S(2)}, u32[]{:S(2)}) collective-permute-start(bf16[2,64,512]{2,1,0:T(8,128)(2,1)S(1)} %pad_maximum_fusion.1), channel_id=1, source_target_pairs={{0,4},{1,5},{2,6},{3,7},{4,0},{5,1},{6,2},{7,3},{8,12},{9,13},{10,... | collective-permute-start | bytes 393224 | tf_op jit(solution)/shard_map/ppermute | solution.py:36
  89.1 20.3 %collective-permute-start.19 = (bf16[2,64,512]{2,1,0:T(8,128)(2,1)S(1)}, bf16[2,64,512]{2,1,0:T(8,128)(2,1)S(1)}, u32[]{:S(2)}, u32[]{:S(2)}) collective-permute-start(bf16[2,64,512]{2,1,0:T(8,128)(2,1)S(1)} %pad_maximum_fusion.2), channel_id=1, source_target_pairs={{0,6},{1,7},{2,4},{3,5},{4,2},{5,3},{6,0},{7,1},{8,14},{9,15},{10,... | collective-permute-start | bytes 393224 | tf_op jit(solution)/shard_map/ppermute | solution.py:36
  90.5 18.8 %collective-permute-start.20 = (bf16[2,64,512]{2,1,0:T(8,128)(2,1)S(1)}, bf16[2,64,512]{2,1,0:T(8,128)(2,1)S(1)}, u32[]{:S(2)}, u32[]{:S(2)}) collective-permute-start(bf16[2,64,512]{2,1,0:T(8,128)(2,1)S(1)} %pad_maximum_fusion.3), channel_id=1, source_target_pairs={{0,8},{1,9},{2,10},{3,11},{4,12},{5,13},{6,14},{7,15},{8,0},{9,1},... | collective-permute-start | bytes 393224 | tf_op jit(solution)/shard_map/ppermute | solution.py:36
  93.6 20.2 %collective-permute-start.21 = (bf16[2,64,512]{2,1,0:T(8,128)(2,1)S(1)}, bf16[2,64,512]{2,1,0:T(8,128)(2,1)S(1)}, u32[]{:S(2)}, u32[]{:S(2)}) collective-permute-start(bf16[2,64,512]{2,1,0:T(8,128)(2,1)S(1)} %pad_maximum_fusion.4), channel_id=1, source_target_pairs={{0,10},{1,11},{2,8},{3,9},{4,14},{5,15},{6,12},{7,13},{8,2},{9,3},... | collective-permute-start | bytes 393224 | tf_op jit(solution)/shard_map/ppermute | solution.py:36
  94.5 19.3 %collective-permute-start.22 = (bf16[2,64,512]{2,1,0:T(8,128)(2,1)S(1)}, bf16[2,64,512]{2,1,0:T(8,128)(2,1)S(1)}, u32[]{:S(2)}, u32[]{:S(2)}) collective-permute-start(bf16[2,64,512]{2,1,0:T(8,128)(2,1)S(1)} %pad_maximum_fusion.5), channel_id=1, source_target_pairs={{0,12},{1,13},{2,14},{3,15},{4,8},{5,9},{6,10},{7,11},{8,4},{9,5},... | collective-permute-start | bytes 393224 | tf_op jit(solution)/shard_map/ppermute | solution.py:36
  106.2 11.6 %collective-permute-start.23 = (bf16[2,64,512]{2,1,0:T(8,128)(2,1)S(1)}, bf16[2,64,512]{2,1,0:T(8,128)(2,1)S(1)}, u32[]{:S(2)}, u32[]{:S(2)}) collective-permute-start(bf16[2,64,512]{2,1,0:T(8,128)(2,1)S(1)} %pad_maximum_fusion.6), channel_id=1, source_target_pairs={{0,14},{1,15},{2,12},{3,13},{4,10},{5,11},{6,8},{7,9},{8,6},{9,7},... | collective-permute-start | bytes 393224 | tf_op jit(solution)/shard_map/ppermute | solution.py:36

commit v4 on v3

--- a/solution.py
+++ b/solution.py
@@ -188,8 +188,11 @@
                 hi = lo + (1 << e)
                 merge_pair(c_ref, lo, hi, t_ref[e, lo], t_ref[e, hi])
     copies = []
+    merge_pair(c_ref, 0, 8, t_ref[3, 0], t_ref[3, 8])
+    merge_pair(c_ref, 1, 9, t_ref[3, 1], t_ref[3, 9])
     for j in range(N_Z):
-        merge_pair(c_ref, j, j + 8, t_ref[3, j], t_ref[3, j + 8])
+        if j + 2 < N_Z:
+            merge_pair(c_ref, j + 2, j + 10, t_ref[3, j + 2], t_ref[3, j + 10])
         for l in (j, j + 8):
             o_buf[l] = lax.dot_general(
                 s_ref[l], c_ref[l], (((0,), (0,)), ((), ())), preferred_element_type=F32

time: 123 us -> 122 us (level)
  no operation moved by 1% of the time
where the time goes in v4:
time: 122 us
  starting transfers between devices  67.8 us (56%)
  waiting for transfers between devices  38.8 us (32%)
  Pallas kernels  12.9 us (11%)
  local copies, waits for them, and re-layouts  1.89 us (2%)
    ppermute x14, starting transfers between devices, z_swap(): return lax.ppermute(array, 'col', [(c, c ^ 2 * d) for c in range(N_COL)])  37.5 us
    ppermute x9, starting transfers between devices, to_target_row(): return lax.ppermute(array, ('row', 'col'), pairs)  30.2 us
    ppermute x14, waiting for transfers between devices, z_swap(): return lax.ppermute(array, 'col', [(c, c ^ 2 * d) for c in range(N_COL)])  26.9 us
    ppermute x9, waiting for transfers between devices, to_target_row(): return lax.ppermute(array, ('row', 'col'), pairs)  10.9 us
    pallas_call x1, Pallas kernels, front(): pl.pallas_call(front_kernel, in_specs=[HBM] * 3, out_specs=VMEM, out_shap...  5.92 us
    pallas_call x1, Pallas kernels, tail(): pl.pallas_call(tail_kernel, in_specs=[SMEM] + [VMEM] * (N_Z + 3), out_spe...  3.94 us
  transfers between devices with their start and end apart: 24, of which 11 were waited for; matrix products, arithmetic and copies ran while one was open for 2% of the time, Pallas kernels for 1%

profile of v4, /device:TPU:2, one launch (start us, length us, event | category | flops | bytes accessed | tf_op | source)
XLA Modules:
  0.0 121.9 jit_solution(10203841269659313364)
XLA Ops:
  0.0 5.9 %front.1.own_ref = bf16[16,64,512]{2,1,0:T(8,128)(2,1)} custom-call(bf16[16,256,512]{2,1,0:T(8,128)(2,1)} %f_hbm.1, bf16[16,64,256]{2,1,0:T(8,128)(2,1)} %a_hbm.1, bf16[12,16,64,128]{3,2,1,0:T(8,128)(2,1)} %t_hbm.1), custom_call_target="tpu_custom_call" | custom-call | flops 800000000 | bytes 7000000 | tf_op jit(solution)/shard_map/front/pallas_call | solution.py:104
  5.9 0.0 copy-start
  5.9 0.1 collective-permute-start
  6.1 0.1 pad_add_fusion.r_ref
  6.1 1.8 %fusion = (bf16[4,16,64,128]{3,2,1,0:T(8,128)(2,1)S(1)}, bf16[4,16,64,128]{3,2,1,0:T(8,128)(2,1)S(1)}) fusion(bf16[12,16,64,128]{3,2,1,0:T(8,128)(2,1)} %t_hbm.1), kind=kLoop, calls=%fused_computation.8 | loop fusion | bytes 4194304 | tf_op jit(solution)/shard_map/slice | solution.py:227
  7.9 1.0 collective-permute-done.partner_ref
  8.9 0.0 copy-done
  8.9 0.8 shard_map.46
  9.8 2.0 %collective-permute-start.1 = (bf16[64,896]{1,0:T(8,128)(2,1)S(1)}, bf16[64,896]{1,0:T(8,128)(2,1)S(1)}, u32[]{:S(2)}, u32[]{:S(2)}) collective-permute-start(bf16[64,896]{1,0:T(8,128)(2,1)S(1)} %get-tuple-element.22), channel_id=1, source_target_pairs={{0,2},{1,3},{2,0},{3,1},{4,6},{5,7},{6,4},{7,5},{8,10},{9,11},{10,... | collective-permute-start | bytes 344072 | tf_op jit(solution)/shard_map/ppermute | solution.py:36
  11.8 3.3 %collective-permute-start.2 = (bf16[64,896]{1,0:T(8,128)(2,1)S(1)}, bf16[64,896]{1,0:T(8,128)(2,1)S(1)}, u32[]{:S(2)}, u32[]{:S(2)}) collective-permute-start(bf16[64,896]{1,0:T(8,128)(2,1)S(1)} %get-tuple-element.23), channel_id=1, source_target_pairs={{0,4},{1,5},{2,6},{3,7},{4,0},{5,1},{6,2},{7,3},{8,12},{9,13},{10,... | collective-permute-start | bytes 344072 | tf_op jit(solution)/shard_map/ppermute | solution.py:36
  15.0 0.0 collective-permute-start.3
  15.0 6.4 %collective-permute-start.4 = (bf16[64,896]{1,0:T(8,128)(2,1)S(1)}, bf16[64,896]{1,0:T(8,128)(2,1)S(1)}, u32[]{:S(2)}, u32[]{:S(2)}) collective-permute-start(bf16[64,896]{1,0:T(8,128)(2,1)S(1)} %get-tuple-element.25), channel_id=1, source_target_pairs={{0,8},{1,9},{2,10},{3,11},{4,12},{5,13},{6,14},{7,15},{8,0},{9,1},... | collective-permute-start | bytes 344072 | tf_op jit(solution)/shard_map/ppermute | solution.py:36
  21.4 0.0 collective-permute-start.5
  21.4 0.0 collective-permute-done.1.refs_1_
  21.4 4.6 %collective-permute-start.6 = (bf16[64,896]{1,0:T(8,128)(2,1)S(1)}, bf16[64,896]{1,0:T(8,128)(2,1)S(1)}, u32[]{:S(2)}, u32[]{:S(2)}) collective-permute-start(bf16[64,896]{1,0:T(8,128)(2,1)S(1)} %get-tuple-element.27), channel_id=1, source_target_pairs={{0,12},{1,13},{2,14},{3,15},{4,8},{5,9},{6,10},{7,11},{8,4},{9,5},... | collective-permute-start | bytes 344072 | tf_op jit(solution)/shard_map/ppermute | solution.py:36
  26.0 4.2 %collective-permute-done.2.refs_2_ = bf16[64,896]{1,0:T(8,128)(2,1)S(1)} collective-permute-done((bf16[64,896]{1,0:T(8,128)(2,1)S(1)}, bf16[64,896]{1,0:T(8,128)(2,1)S(1)}, u32[]{:S(2)}, u32[]{:S(2)}) %collective-permute-start.2) | collective-permute-done | bytes 114720 | tf_op jit(solution)/shard_map/ppermute | solution.py:36
  30.3 4.8 %collective-permute-start.7 = (bf16[64,896]{1,0:T(8,128)(2,1)S(1)}, bf16[64,896]{1,0:T(8,128)(2,1)S(1)}, u32[]{:S(2)}, u32[]{:S(2)}) collective-permute-start(bf16[64,896]{1,0:T(8,128)(2,1)S(1)} %get-tuple-element.28), channel_id=1, source_target_pairs={{0,14},{1,15},{2,12},{3,13},{4,10},{5,11},{6,8},{7,9},{8,6},{9,7},... | collective-permute-start | bytes 344072 | tf_op jit(solution)/shard_map/ppermute | solution.py:36
  35.1 0.0 collective-permute-done.3.refs_3_
  35.1 0.0 collective-permute-done.4.refs_4_
  35.1 3.8 %collective-permute-done.5.refs_5_ = bf16[64,896]{1,0:T(8,128)(2,1)S(1)} collective-permute-done((bf16[64,896]{1,0:T(8,128)(2,1)S(1)}, bf16[64,896]{1,0:T(8,128)(2,1)S(1)}, u32[]{:S(2)}, u32[]{:S(2)}) %collective-permute-start.5) | collective-permute-done | bytes 114720 | tf_op jit(solution)/shard_map/ppermute | solution.py:36
  38.9 0.3 collective-permute-done.6.refs_6_
  39.2 3.1 %collective-permute-done.7.refs_7_ = bf16[64,896]{1,0:T(8,128)(2,1)S(1)} collective-permute-done((bf16[64,896]{1,0:T(8,128)(2,1)S(1)}, bf16[64,896]{1,0:T(8,128)(2,1)S(1)}, u32[]{:S(2)}, u32[]{:S(2)}) %collective-permute-start.7) | collective-permute-done | bytes 114720 | tf_op jit(solution)/shard_map/ppermute | solution.py:36
  42.3 0.7 shard_map.47
  43.0 0.0 copy-start.1
  43.0 3.3 %collective-permute-start.8 = (bf16[8,64,512]{2,1,0:T(8,128)(2,1)S(1)}, bf16[8,64,512]{2,1,0:T(8,128)(2,1)S(1)}, u32[]{:S(2)}, u32[]{:S(2)}) collective-permute-start(bf16[8,64,512]{2,1,0:T(8,128)(2,1)S(1)} %shard_map.47), channel_id=1, source_target_pairs={{0,128},{1,225},{2,146},{3,243},{4,164},{5,197},{6,182},{7,215},{8... | collective-permute-start | bytes 1572872 | tf_op jit(solution)/shard_map/ppermute | solution.py:46
  46.3 0.8 shard_map.48
  47.1 0.7 collective-permute-start.9
  47.8 2.8 %collective-permute-start.10 = (bf16[64,896]{1,0:T(8,128)(2,1)S(1)}, bf16[64,896]{1,0:T(8,128)(2,1)S(1)}, u32[]{:S(2)}, u32[]{:S(2)}) collective-permute-start(bf16[64,896]{1,0:T(8,128)(2,1)S(1)} %get-tuple-element.30), channel_id=1, source_target_pairs={{0,18},{1,115},{2,0},{3,97},{4,54},{5,87},{6,36},{7,69},{8,90},{9,... | collective-permute-start | bytes 344072 | tf_op jit(solution)/shard_map/ppermute | solution.py:46
  50.6 5.2 %collective-permute-start.11 = (bf16[64,896]{1,0:T(8,128)(2,1)S(1)}, bf16[64,896]{1,0:T(8,128)(2,1)S(1)}, u32[]{:S(2)}, u32[]{:S(2)}) collective-permute-start(bf16[64,896]{1,0:T(8,128)(2,1)S(1)} %get-tuple-element.31), channel_id=1, source_target_pairs={{0,36},{1,69},{2,54},{3,87},{4,0},{5,97},{6,18},{7,115},{8,108},{9... | collective-permute-start | bytes 344072 | tf_op jit(solution)/shard_map/ppermute | solution.py:46
  55.7 0.0 collective-permute-start.12
  55.7 0.0 collective-permute-done.9.refs_0_
  55.7 5.4 %collective-permute-start.13 = (bf16[64,896]{1,0:T(8,128)(2,1)S(1)}, bf16[64,896]{1,0:T(8,128)(2,1)S(1)}, u32[]{:S(2)}, u32[]{:S(2)}) collective-permute-start(bf16[64,896]{1,0:T(8,128)(2,1)S(1)} %get-tuple-element.33), channel_id=1, source_target_pairs={{0,72},{1,41},{2,90},{3,59},{4,108},{5,13},{6,126},{7,31},{8,0},{9... | collective-permute-start | bytes 344072 | tf_op jit(solution)/shard_map/ppermute | solution.py:46
  61.2 0.0 collective-permute-done.10.refs_1_
  61.2 3.9 %collective-permute-start.14 = (bf16[64,896]{1,0:T(8,128)(2,1)S(1)}, bf16[64,896]{1,0:T(8,128)(2,1)S(1)}, u32[]{:S(2)}, u32[]{:S(2)}) collective-permute-start(bf16[64,896]{1,0:T(8,128)(2,1)S(1)} %get-tuple-element.34), channel_id=1, source_target_pairs={{0,90},{1,59},{2,72},{3,41},{4,126},{5,31},{6,108},{7,13},{8,18},{... | collective-permute-start | bytes 344072 | tf_op jit(solution)/shard_map/ppermute | solution.py:46
  65.0 0.0 collective-permute-done.11.refs_2_
  65.0 7.4 %collective-permute-start.15 = (bf16[64,896]{1,0:T(8,128)(2,1)S(1)}, bf16[64,896]{1,0:T(8,128)(2,1)S(1)}, u32[]{:S(2)}, u32[]{:S(2)}) collective-permute-start(bf16[64,896]{1,0:T(8,128)(2,1)S(1)} %get-tuple-element.35), channel_id=1, source_target_pairs={{0,108},{1,13},{2,126},{3,31},{4,72},{5,41},{6,90},{7,59},{8,36},{... | collective-permute-start | bytes 344072 | tf_op jit(solution)/shard_map/ppermute | solution.py:46
  72.5 0.0 collective-permute-done.12.refs_3_
  72.5 1.6 %collective-permute-start.16 = (bf16[64,896]{1,0:T(8,128)(2,1)S(1)}, bf16[64,896]{1,0:T(8,128)(2,1)S(1)}, u32[]{:S(2)}, u32[]{:S(2)}) collective-permute-start(bf16[64,896]{1,0:T(8,128)(2,1)S(1)} %get-tuple-element.36), channel_id=1, source_target_pairs={{0,126},{1,31},{2,108},{3,13},{4,90},{5,59},{6,72},{7,41},{8,54},{... | collective-permute-start | bytes 344072 | tf_op jit(solution)/shard_map/ppermute | solution.py:46
  74.1 0.0 collective-permute-done.13.refs_4_
  74.1 1.4 %collective-permute-done.14.refs_5_ = bf16[64,896]{1,0:T(8,128)(2,1)S(1)} collective-permute-done((bf16[64,896]{1,0:T(8,128)(2,1)S(1)}, bf16[64,896]{1,0:T(8,128)(2,1)S(1)}, u32[]{:S(2)}, u32[]{:S(2)}) %collective-permute-start.14) | collective-permute-done | bytes 114720 | tf_op jit(solution)/shard_map/ppermute | solution.py:46
  75.5 3.3 %collective-permute-done.15.refs_6_ = bf16[64,896]{1,0:T(8,128)(2,1)S(1)} collective-permute-done((bf16[64,896]{1,0:T(8,128)(2,1)S(1)}, bf16[64,896]{1,0:T(8,128)(2,1)S(1)}, u32[]{:S(2)}, u32[]{:S(2)}) %collective-permute-start.15) | collective-permute-done | bytes 114720 | tf_op jit(solution)/shard_map/ppermute | solution.py:46
  78.7 6.3 %collective-permute-done.16.refs_7_ = bf16[64,896]{1,0:T(8,128)(2,1)S(1)} collective-permute-done((bf16[64,896]{1,0:T(8,128)(2,1)S(1)}, bf16[64,896]{1,0:T(8,128)(2,1)S(1)}, u32[]{:S(2)}, u32[]{:S(2)}) %collective-permute-start.16) | collective-permute-done | bytes 114720 | tf_op jit(solution)/shard_map/ppermute | solution.py:46
  85.0 0.7 shard_map.49.refs_1_
  85.7 0.0 collective-permute-done.8.refs_0_
  85.8 0.1 collective-permute-start.17
  85.9 3.1 %collective-permute-start.18 = (bf16[2,64,512]{2,1,0:T(8,128)(2,1)S(1)}, bf16[2,64,512]{2,1,0:T(8,128)(2,1)S(1)}, u32[]{:S(2)}, u32[]{:S(2)}) collective-permute-start(bf16[2,64,512]{2,1,0:T(8,128)(2,1)S(1)} %pad_maximum_fusion.1), channel_id=1, source_target_pairs={{0,4},{1,5},{2,6},{3,7},{4,0},{5,1},{6,2},{7,3},{8,12},{9,13},{10,... | collective-permute-start | bytes 393224 | tf_op jit(solution)/shard_map/ppermute | solution.py:36
  89.1 1.4 %collective-permute-start.19 = (bf16[2,64,512]{2,1,0:T(8,128)(2,1)S(1)}, bf16[2,64,512]{2,1,0:T(8,128)(2,1)S(1)}, u32[]{:S(2)}, u32[]{:S(2)}) collective-permute-start(bf16[2,64,512]{2,1,0:T(8,128)(2,1)S(1)} %pad_maximum_fusion.2), channel_id=1, source_target_pairs={{0,6},{1,7},{2,4},{3,5},{4,2},{5,3},{6,0},{7,1},{8,14},{9,15},{10,... | collective-permute-start | bytes 393224 | tf_op jit(solution)/shard_map/ppermute | solution.py:36
  90.5 3.1 %collective-permute-start.20 = (bf16[2,64,512]{2,1,0:T(8,128)(2,1)S(1)}, bf16[2,64,512]{2,1,0:T(8,128)(2,1)S(1)}, u32[]{:S(2)}, u32[]{:S(2)}) collective-permute-start(bf16[2,64,512]{2,1,0:T(8,128)(2,1)S(1)} %pad_maximum_fusion.3), channel_id=1, source_target_pairs={{0,8},{1,9},{2,10},{3,11},{4,12},{5,13},{6,14},{7,15},{8,0},{9,1},... | collective-permute-start | bytes 393224 | tf_op jit(solution)/shard_map/ppermute | solution.py:36
  93.6 0.8 collective-permute-start.21
  94.5 0.0 collective-permute-done.17.refs_2_
  94.5 4.8 %collective-permute-start.22 = (bf16[2,64,512]{2,1,0:T(8,128)(2,1)S(1)}, bf16[2,64,512]{2,1,0:T(8,128)(2,1)S(1)}, u32[]{:S(2)}, u32[]{:S(2)}) collective-permute-start(bf16[2,64,512]{2,1,0:T(8,128)(2,1)S(1)} %pad_maximum_fusion.5), channel_id=1, source_target_pairs={{0,12},{1,13},{2,14},{3,15},{4,8},{5,9},{6,10},{7,11},{8,4},{9,5},... | collective-permute-start | bytes 393224 | tf_op jit(solution)/shard_map/ppermute | solution.py:36
  99.3 6.9 %collective-permute-done.18.refs_3_ = bf16[2,64,512]{2,1,0:T(8,128)(2,1)S(1)} collective-permute-done((bf16[2,64,512]{2,1,0:T(8,128)(2,1)S(1)}, bf16[2,64,512]{2,1,0:T(8,128)(2,1)S(1)}, u32[]{:S(2)}, u32[]{:S(2)}) %collective-permute-start.18) | collective-permute-done | bytes 131104 | tf_op jit(solution)/shard_map/ppermute | solution.py:36
  106.2 3.1 %collective-permute-start.23 = (bf16[2,64,512]{2,1,0:T(8,128)(2,1)S(1)}, bf16[2,64,512]{2,1,0:T(8,128)(2,1)S(1)}, u32[]{:S(2)}, u32[]{:S(2)}) collective-permute-start(bf16[2,64,512]{2,1,0:T(8,128)(2,1)S(1)} %pad_maximum_fusion.6), channel_id=1, source_target_pairs={{0,14},{1,15},{2,12},{3,13},{4,10},{5,11},{6,8},{7,9},{8,6},{9,7},... | collective-permute-start | bytes 393224 | tf_op jit(solution)/shard_map/ppermute | solution.py:36
  109.3 0.0 collective-permute-done.19.refs_4_
  109.3 0.0 collective-permute-done.20.refs_5_
  109.3 4.5 %collective-permute-done.21.refs_6_ = bf16[2,64,512]{2,1,0:T(8,128)(2,1)S(1)} collective-permute-done((bf16[2,64,512]{2,1,0:T(8,128)(2,1)S(1)}, bf16[2,64,512]{2,1,0:T(8,128)(2,1)S(1)}, u32[]{:S(2)}, u32[]{:S(2)}) %collective-permute-start.21) | collective-permute-done | bytes 131104 | tf_op jit(solution)/shard_map/ppermute | solution.py:36
  113.8 0.0 collective-permute-done.22.refs_7_
  113.8 4.1 %collective-permute-done.23.refs_8_ = bf16[2,64,512]{2,1,0:T(8,128)(2,1)S(1)} collective-permute-done((bf16[2,64,512]{2,1,0:T(8,128)(2,1)S(1)}, bf16[2,64,512]{2,1,0:T(8,128)(2,1)S(1)}, u32[]{:S(2)}, u32[]{:S(2)}) %collective-permute-start.23) | collective-permute-done | bytes 131104 | tf_op jit(solution)/shard_map/ppermute | solution.py:36
  117.8 0.0 copy-done.1
  117.8 3.9 %tail.1 = bf16[16,256,512]{2,1,0:T(8,128)(2,1)} custom-call(s32[3]{0:T(128)S(1)} %pad_add_fusion.r_ref, bf16[8,64,512]{2,1,0:T(8,128)(2,1)S(1)} %collective-permute-done.8.refs_0_, bf16[8,64,512]{2,1,0:T(8,128)(2,1)S(1)} %shard_map.49.refs_1_, bf16[2,64,512]{2,1,0:T(8,128)(2,1)S(1)} %collective-permute-done.17.refs_2_, ...), custom_call_target="tpu_custom_call" | custom-call | flops 800000000 | bytes 7000000 | tf_op jit(solution)/shard_map/tail/pallas_call | solution.py:207
  (9 shorter events, 0.2 us)
Async XLA Ops:
  5.9 3.0 %copy-start = (bf16[16,64,512]{2,1,0:T(8,128)(2,1)S(1)}, bf16[16,64,512]{2,1,0:T(8,128)(2,1)}, u32[]{:S(2)}) copy-start(bf16[16,64,512]{2,1,0:T(8,128)(2,1)} %front.1.own_ref) | copy-start | bytes 3145732
  5.9 3.0 %collective-permute-start = (bf16[16,64,512]{2,1,0:T(8,128)(2,1)}, bf16[16,64,512]{2,1,0:T(8,128)(2,1)S(1)}, u32[]{:S(2)}, u32[]{:S(2)}) collective-permute-start(bf16[16,64,512]{2,1,0:T(8,128)(2,1)} %front.1.own_ref), channel_id=1, source_target_pairs={{0,1},{1,0},{2,3},{3,2},{4,5},{5,4},{6,7},{7,6},{8,9},{9,8},{10,11... | collective-permute-start | bytes 3145736 | tf_op jit(solution)/shard_map/ppermute | solution.py:228
  9.8 11.7 %collective-permute-start.1 = (bf16[64,896]{1,0:T(8,128)(2,1)S(1)}, bf16[64,896]{1,0:T(8,128)(2,1)S(1)}, u32[]{:S(2)}, u32[]{:S(2)}) collective-permute-start(bf16[64,896]{1,0:T(8,128)(2,1)S(1)} %get-tuple-element.22), channel_id=1, source_target_pairs={{0,2},{1,3},{2,0},{3,1},{4,6},{5,7},{6,4},{7,5},{8,10},{9,11},{10,... | collective-permute-start | bytes 344072 | tf_op jit(solution)/shard_map/ppermute | solution.py:36
  11.8 18.5 %collective-permute-start.2 = (bf16[64,896]{1,0:T(8,128)(2,1)S(1)}, bf16[64,896]{1,0:T(8,128)(2,1)S(1)}, u32[]{:S(2)}, u32[]{:S(2)}) collective-permute-start(bf16[64,896]{1,0:T(8,128)(2,1)S(1)} %get-tuple-element.23), channel_id=1, source_target_pairs={{0,4},{1,5},{2,6},{3,7},{4,0},{5,1},{6,2},{7,3},{8,12},{9,13},{10,... | collective-permute-start | bytes 344072 | tf_op jit(solution)/shard_map/ppermute | solution.py:36
  15.0 20.0 %collective-permute-start.3 = (bf16[64,896]{1,0:T(8,128)(2,1)S(1)}, bf16[64,896]{1,0:T(8,128)(2,1)S(1)}, u32[]{:S(2)}, u32[]{:S(2)}) collective-permute-start(bf16[64,896]{1,0:T(8,128)(2,1)S(1)} %get-tuple-element.24), channel_id=1, source_target_pairs={{0,6},{1,7},{2,4},{3,5},{4,2},{5,3},{6,0},{7,1},{8,14},{9,15},{10,... | collective-permute-start | bytes 344072 | tf_op jit(solution)/shard_map/ppermute | solution.py:36
  15.0 20.0 %collective-permute-start.4 = (bf16[64,896]{1,0:T(8,128)(2,1)S(1)}, bf16[64,896]{1,0:T(8,128)(2,1)S(1)}, u32[]{:S(2)}, u32[]{:S(2)}) collective-permute-start(bf16[64,896]{1,0:T(8,128)(2,1)S(1)} %get-tuple-element.25), channel_id=1, source_target_pairs={{0,8},{1,9},{2,10},{3,11},{4,12},{5,13},{6,14},{7,15},{8,0},{9,1},... | collective-permute-start | bytes 344072 | tf_op jit(solution)/shard_map/ppermute | solution.py:36
  21.4 17.4 %collective-permute-start.5 = (bf16[64,896]{1,0:T(8,128)(2,1)S(1)}, bf16[64,896]{1,0:T(8,128)(2,1)S(1)}, u32[]{:S(2)}, u32[]{:S(2)}) collective-permute-start(bf16[64,896]{1,0:T(8,128)(2,1)S(1)} %get-tuple-element.26), channel_id=1, source_target_pairs={{0,10},{1,11},{2,8},{3,9},{4,14},{5,15},{6,12},{7,13},{8,2},{9,3},... | collective-permute-start | bytes 344072 | tf_op jit(solution)/shard_map/ppermute | solution.py:36
  21.4 17.8 %collective-permute-start.6 = (bf16[64,896]{1,0:T(8,128)(2,1)S(1)}, bf16[64,896]{1,0:T(8,128)(2,1)S(1)}, u32[]{:S(2)}, u32[]{:S(2)}) collective-permute-start(bf16[64,896]{1,0:T(8,128)(2,1)S(1)} %get-tuple-element.27), channel_id=1, source_target_pairs={{0,12},{1,13},{2,14},{3,15},{4,8},{5,9},{6,10},{7,11},{8,4},{9,5},... | collective-permute-start | bytes 344072 | tf_op jit(solution)/shard_map/ppermute | solution.py:36
  30.3 12.0 %collective-permute-start.7 = (bf16[64,896]{1,0:T(8,128)(2,1)S(1)}, bf16[64,896]{1,0:T(8,128)(2,1)S(1)}, u32[]{:S(2)}, u32[]{:S(2)}) collective-permute-start(bf16[64,896]{1,0:T(8,128)(2,1)S(1)} %get-tuple-element.28), channel_id=1, source_target_pairs={{0,14},{1,15},{2,12},{3,13},{4,10},{5,11},{6,8},{7,9},{8,6},{9,7},... | collective-permute-start | bytes 344072 | tf_op jit(solution)/shard_map/ppermute | solution.py:36
  43.0 74.9 %copy-start.1 = (bf16[16,64,256]{2,1,0:T(8,128)(2,1)S(1)}, bf16[16,64,256]{2,1,0:T(8,128)(2,1)}, u32[]{:S(2)}) copy-start(bf16[16,64,256]{2,1,0:T(8,128)(2,1)} %refs_10_.1) | copy-start | bytes 1572868
  43.0 42.7 %collective-permute-start.8 = (bf16[8,64,512]{2,1,0:T(8,128)(2,1)S(1)}, bf16[8,64,512]{2,1,0:T(8,128)(2,1)S(1)}, u32[]{:S(2)}, u32[]{:S(2)}) collective-permute-start(bf16[8,64,512]{2,1,0:T(8,128)(2,1)S(1)} %shard_map.47), channel_id=1, source_target_pairs={{0,128},{1,225},{2,146},{3,243},{4,164},{5,197},{6,182},{7,215},{8... | collective-permute-start | bytes 1572872 | tf_op jit(solution)/shard_map/ppermute | solution.py:46
  47.1 8.6 %collective-permute-start.9 = (bf16[64,896]{1,0:T(8,128)(2,1)S(1)}, bf16[64,896]{1,0:T(8,128)(2,1)S(1)}, u32[]{:S(2)}, u32[]{:S(2)}) collective-permute-start(bf16[64,896]{1,0:T(8,128)(2,1)S(1)} %get-tuple-element.29), channel_id=1, source_target_pairs={{0,0},{1,97},{2,18},{3,115},{4,36},{5,69},{6,54},{7,87},{8,72},{9,... | collective-permute-start | bytes 344072 | tf_op jit(solution)/shard_map/ppermute | solution.py:46
  47.8 13.4 %collective-permute-start.10 = (bf16[64,896]{1,0:T(8,128)(2,1)S(1)}, bf16[64,896]{1,0:T(8,128)(2,1)S(1)}, u32[]{:S(2)}, u32[]{:S(2)}) collective-permute-start(bf16[64,896]{1,0:T(8,128)(2,1)S(1)} %get-tuple-element.30), channel_id=1, source_target_pairs={{0,18},{1,115},{2,0},{3,97},{4,54},{5,87},{6,36},{7,69},{8,90},{9,... | collective-permute-start | bytes 344072 | tf_op jit(solution)/shard_map/ppermute | solution.py:46
  50.6 14.5 %collective-permute-start.11 = (bf16[64,896]{1,0:T(8,128)(2,1)S(1)}, bf16[64,896]{1,0:T(8,128)(2,1)S(1)}, u32[]{:S(2)}, u32[]{:S(2)}) collective-permute-start(bf16[64,896]{1,0:T(8,128)(2,1)S(1)} %get-tuple-element.31), channel_id=1, source_target_pairs={{0,36},{1,69},{2,54},{3,87},{4,0},{5,97},{6,18},{7,115},{8,108},{9... | collective-permute-start | bytes 344072 | tf_op jit(solution)/shard_map/ppermute | solution.py:46
  55.7 16.7 %collective-permute-start.12 = (bf16[64,896]{1,0:T(8,128)(2,1)S(1)}, bf16[64,896]{1,0:T(8,128)(2,1)S(1)}, u32[]{:S(2)}, u32[]{:S(2)}) collective-permute-start(bf16[64,896]{1,0:T(8,128)(2,1)S(1)} %get-tuple-element.32), channel_id=1, source_target_pairs={{0,54},{1,87},{2,36},{3,69},{4,18},{5,115},{6,0},{7,97},{8,126},{9... | collective-permute-start | bytes 344072 | tf_op jit(solution)/shard_map/ppermute | solution.py:46
  55.7 18.3 %collective-permute-start.13 = (bf16[64,896]{1,0:T(8,128)(2,1)S(1)}, bf16[64,896]{1,0:T(8,128)(2,1)S(1)}, u32[]{:S(2)}, u32[]{:S(2)}) collective-permute-start(bf16[64,896]{1,0:T(8,128)(2,1)S(1)} %get-tuple-element.33), channel_id=1, source_target_pairs={{0,72},{1,41},{2,90},{3,59},{4,108},{5,13},{6,126},{7,31},{8,0},{9... | collective-permute-start | bytes 344072 | tf_op jit(solution)/shard_map/ppermute | solution.py:46
  61.2 14.3 %collective-permute-start.14 = (bf16[64,896]{1,0:T(8,128)(2,1)S(1)}, bf16[64,896]{1,0:T(8,128)(2,1)S(1)}, u32[]{:S(2)}, u32[]{:S(2)}) collective-permute-start(bf16[64,896]{1,0:T(8,128)(2,1)S(1)} %get-tuple-element.34), channel_id=1, source_target_pairs={{0,90},{1,59},{2,72},{3,41},{4,126},{5,31},{6,108},{7,13},{8,18},{... | collective-permute-start | bytes 344072 | tf_op jit(solution)/shard_map/ppermute | solution.py:46
  65.0 13.7 %collective-permute-start.15 = (bf16[64,896]{1,0:T(8,128)(2,1)S(1)}, bf16[64,896]{1,0:T(8,128)(2,1)S(1)}, u32[]{:S(2)}, u32[]{:S(2)}) collective-permute-start(bf16[64,896]{1,0:T(8,128)(2,1)S(1)} %get-tuple-element.35), channel_id=1, source_target_pairs={{0,108},{1,13},{2,126},{3,31},{4,72},{5,41},{6,90},{7,59},{8,36},{... | collective-permute-start | bytes 344072 | tf_op jit(solution)/shard_map/ppermute | solution.py:46
  72.5 12.5 %collective-permute-start.16 = (bf16[64,896]{1,0:T(8,128)(2,1)S(1)}, bf16[64,896]{1,0:T(8,128)(2,1)S(1)}, u32[]{:S(2)}, u32[]{:S(2)}) collective-permute-start(bf16[64,896]{1,0:T(8,128)(2,1)S(1)} %get-tuple-element.36), channel_id=1, source_target_pairs={{0,126},{1,31},{2,108},{3,13},{4,90},{5,59},{6,72},{7,41},{8,54},{... | collective-permute-start | bytes 344072 | tf_op jit(solution)/shard_map/ppermute | solution.py:46
  85.8 8.6 %collective-permute-start.17 = (bf16[2,64,512]{2,1,0:T(8,128)(2,1)S(1)}, bf16[2,64,512]{2,1,0:T(8,128)(2,1)S(1)}, u32[]{:S(2)}, u32[]{:S(2)}) collective-permute-start(bf16[2,64,512]{2,1,0:T(8,128)(2,1)S(1)} %pad_maximum_fusion), channel_id=1, source_target_pairs={{0,2},{1,3},{2,0},{3,1},{4,6},{5,7},{6,4},{7,5},{8,10},{9,11},{10,... | collective-permute-start | bytes 393224 | tf_op jit(solution)/shard_map/ppermute | solution.py:36
  85.9 20.3 %collective-permute-start.18 = (bf16[2,64,512]{2,1,0:T(8,128)(2,1)S(1)}, bf16[2,64,512]{2,1,0:T(8,128)(2,1)S(1)}, u32[]{:S(2)}, u32[]{:S(2)}) collective-permute-start(bf16[2,64,512]{2,1,0:T(8,128)(2,1)S(1)} %pad_maximum_fusion.1), channel_id=1, source_target_pairs={{0,4},{1,5},{2,6},{3,7},{4,0},{5,1},{6,2},{7,3},{8,12},{9,13},{10,... | collective-permute-start | bytes 393224 | tf_op jit(solution)/shard_map/ppermute | solution.py:36
  89.1 20.3 %collective-permute-start.19 = (bf16[2,64,512]{2,1,0:T(8,128)(2,1)S(1)}, bf16[2,64,512]{2,1,0:T(8,128)(2,1)S(1)}, u32[]{:S(2)}, u32[]{:S(2)}) collective-permute-start(bf16[2,64,512]{2,1,0:T(8,128)(2,1)S(1)} %pad_maximum_fusion.2), channel_id=1, source_target_pairs={{0,6},{1,7},{2,4},{3,5},{4,2},{5,3},{6,0},{7,1},{8,14},{9,15},{10,... | collective-permute-start | bytes 393224 | tf_op jit(solution)/shard_map/ppermute | solution.py:36
  90.5 18.8 %collective-permute-start.20 = (bf16[2,64,512]{2,1,0:T(8,128)(2,1)S(1)}, bf16[2,64,512]{2,1,0:T(8,128)(2,1)S(1)}, u32[]{:S(2)}, u32[]{:S(2)}) collective-permute-start(bf16[2,64,512]{2,1,0:T(8,128)(2,1)S(1)} %pad_maximum_fusion.3), channel_id=1, source_target_pairs={{0,8},{1,9},{2,10},{3,11},{4,12},{5,13},{6,14},{7,15},{8,0},{9,1},... | collective-permute-start | bytes 393224 | tf_op jit(solution)/shard_map/ppermute | solution.py:36
  93.6 20.2 %collective-permute-start.21 = (bf16[2,64,512]{2,1,0:T(8,128)(2,1)S(1)}, bf16[2,64,512]{2,1,0:T(8,128)(2,1)S(1)}, u32[]{:S(2)}, u32[]{:S(2)}) collective-permute-start(bf16[2,64,512]{2,1,0:T(8,128)(2,1)S(1)} %pad_maximum_fusion.4), channel_id=1, source_target_pairs={{0,10},{1,11},{2,8},{3,9},{4,14},{5,15},{6,12},{7,13},{8,2},{9,3},... | collective-permute-start | bytes 393224 | tf_op jit(solution)/shard_map/ppermute | solution.py:36
  94.5 19.3 %collective-permute-start.22 = (bf16[2,64,512]{2,1,0:T(8,128)(2,1)S(1)}, bf16[2,64,512]{2,1,0:T(8,128)(2,1)S(1)}, u32[]{:S(2)}, u32[]{:S(2)}) collective-permute-start(bf16[2,64,512]{2,1,0:T(8,128)(2,1)S(1)} %pad_maximum_fusion.5), channel_id=1, source_target_pairs={{0,12},{1,13},{2,14},{3,15},{4,8},{5,9},{6,10},{7,11},{8,4},{9,5},... | collective-permute-start | bytes 393224 | tf_op jit(solution)/shard_map/ppermute | solution.py:36
  106.2 11.6 %collective-permute-start.23 = (bf16[2,64,512]{2,1,0:T(8,128)(2,1)S(1)}, bf16[2,64,512]{2,1,0:T(8,128)(2,1)S(1)}, u32[]{:S(2)}, u32[]{:S(2)}) collective-permute-start(bf16[2,64,512]{2,1,0:T(8,128)(2,1)S(1)} %pad_maximum_fusion.6), channel_id=1, source_target_pairs={{0,14},{1,15},{2,12},{3,13},{4,10},{5,11},{6,8},{7,9},{8,6},{9,7},... | collective-permute-start | bytes 393224 | tf_op jit(solution)/shard_map/ppermute | solution.py:36
